TPU v7x, 32 devices: a whole 2x2x4 slice. The times are simulated.
32 devices in a mesh: fsdp: 2 (over x), ctx: 4 (over y, core), tp: 4 (over z).
Axes of the slice: x: 2, y: 2, z: 4, core: 2. Of those that a mesh axis runs over, the one named last changes fastest.
Arguments:
- tokens: bfloat16 [196, 8, 4, 768], P('tp', 'ctx', 'fsdp'), may hold values from -6 to 6
- norm_gains: bfloat16 [3, 768], P(None, 'fsdp'), may hold values from 0.099609375 to 1.8984375
- temporal_qkv: bfloat16 [768, 3, 768], P('fsdp', None, 'tp'), may hold values from -0.21875 to 0.21875
- temporal_proj: bfloat16 [768, 768], P('tp', 'fsdp'), may hold values from -0.3125 to 0.3125
- spatial_qkv: bfloat16 [768, 3, 768], P('fsdp', None, 'tp'), may hold values from -0.21875 to 0.21875
- spatial_proj: bfloat16 [768, 768], P('tp', 'fsdp'), may hold values from -1.5 to 1.5
- up_weight: bfloat16 [768, 3072], P('fsdp', 'tp'), may hold values from -0.21875 to 0.21875
- down_weight: bfloat16 [3072, 768], P('tp', 'fsdp'), may hold values from -0.109375 to 0.109375
- cotangent: bfloat16 [196, 8, 4, 768], P('tp', 'ctx', 'fsdp'), may hold values from -6 to 6
Outputs:
- block_out: bfloat16 [196, 8, 4, 768], P('tp', 'ctx', 'fsdp')
- tokens_grad: float32 [196, 8, 4, 768], P('tp', 'ctx', 'fsdp')
- norm_gains_grad: float32 [3, 768], P(None, 'fsdp')
- temporal_qkv_grad: float32 [768, 3, 768], P('fsdp', None, 'tp')
- temporal_proj_grad: float32 [768, 768], P('tp', 'fsdp')
- spatial_qkv_grad: float32 [768, 3, 768], P('fsdp', None, 'tp')
- spatial_proj_grad: float32 [768, 768], P('tp', 'fsdp')
- up_weight_grad: float32 [768, 3072], P('fsdp', 'tp')
- down_weight_grad: float32 [3072, 768], P('tp', 'fsdp')
All inputs are finite; a program needn't handle non-finite values.
Results may differ from a plain program's by a relative error of at most 0.03.
Values may be sent and summed in bfloat16 or wider, within the bound.
No kernel may reach another device: no remote copies, remote signals or barrier semaphores. Data moves between devices by JAX's collectives and lax.ppermute only.
A program may use at most 128 MiB of HBM per device.

v0:
```python
import jax
import jax.numpy as jnp
from jax import lax
from jax.sharding import PartitionSpec as P

HEAD_DIM = 64


EPSILON = 1e-06


def layer_norm(values, gain_row):
    center = values - jnp.mean(values, axis=-1, keepdims=True)
    spread = jnp.mean(center * center, axis=-1, keepdims=True)
    return center * lax.rsqrt(spread + EPSILON) * gain_row


def exact_gelu(values):
    return jax.nn.gelu(values, approximate=False)


def split_heads(joined_rows):
    head_shape = joined_rows.shape[:3] + (joined_rows.shape[4] // HEAD_DIM, HEAD_DIM)
    return tuple((joined_rows[:, :, :, member].reshape(head_shape) for member in range(3)))


def gather_rows(values):
    return lax.all_gather(values, "tp", axis=0, tiled=True)


def gather_grads(values):
    return lax.all_gather(values, "tp", axis=0, tiled=True)


def row_partial(operand, weight_part, pattern):
    return jnp.einsum(pattern, operand, weight_part, preferred_element_type=jnp.float32)


def scatter_rows(operand, weight_part, pattern):
    return lax.psum_scatter(
        row_partial(operand, weight_part, pattern).astype(jnp.bfloat16),
        "tp",
        scatter_dimension=0,
        tiled=True,
    ).astype(jnp.float32)


def scatter_back(operand, weight_part, pattern):
    return lax.psum_scatter(
        row_partial(operand, weight_part, pattern).astype(jnp.bfloat16),
        "tp",
        scatter_dimension=0,
        tiled=True,
    ).astype(jnp.float32)


def temporal_attend(queries, key_side, value_side):
    scores = jnp.einsum(
        "pfchd,pgchd->pchfg", queries, key_side, preferred_element_type=jnp.float32
    ) * HEAD_DIM ** (-0.5)
    log_total = jax.nn.logsumexp(scores, axis=-1, keepdims=True)
    weights = jnp.exp(scores - log_total).astype(jnp.bfloat16)
    heads_out = jnp.einsum(
        "pchfg,pgchd->pfchd", weights, value_side, preferred_element_type=jnp.float32
    )
    return (heads_out.astype(jnp.bfloat16), log_total)


def temporal_terms(queries, key_side, value_side, log_total, heads_grad):
    scale_factor = HEAD_DIM ** (-0.5)
    scores = (
        jnp.einsum("pfchd,pgchd->pchfg", queries, key_side, preferred_element_type=jnp.float32)
        * scale_factor
    )
    weights = jnp.exp(scores - log_total)
    weights_low = weights.astype(jnp.bfloat16)
    weight_grad = jnp.einsum(
        "pfchd,pgchd->pchfg", heads_grad, value_side, preferred_element_type=jnp.float32
    )
    score_grad = (
        weights * (weight_grad - jnp.sum(weights * weight_grad, axis=-1, keepdims=True))
    ).astype(jnp.bfloat16)
    query_grad = (
        jnp.einsum("pchfg,pgchd->pfchd", score_grad, key_side, preferred_element_type=jnp.float32)
        * scale_factor
    )
    key_terms = (
        jnp.einsum("pchfg,pfchd->pgchd", score_grad, queries, preferred_element_type=jnp.float32)
        * scale_factor
    )
    value_terms = jnp.einsum(
        "pchfg,pfchd->pgchd", weights_low, heads_grad, preferred_element_type=jnp.float32
    )
    return (query_grad, key_terms, value_terms)


def temporal_forward(queries, key_rows, value_rows):
    key_side, value_side = (
        lax.all_gather(key_rows, "ctx", axis=1, tiled=True),
        lax.all_gather(value_rows, "ctx", axis=1, tiled=True),
    )
    heads_out, log_total = temporal_attend(queries, key_side, value_side)
    return (heads_out, (queries, key_side, value_side, log_total))


def temporal_backward(saved, heads_grad):
    queries, key_side, value_side, log_total = saved
    query_grad, key_terms, value_terms = temporal_terms(
        queries, key_side, value_side, log_total, heads_grad
    )
    key_grad, value_grad = (
        lax.psum_scatter(
            key_terms.astype(jnp.bfloat16), "ctx", scatter_dimension=1, tiled=True
        ).astype(jnp.float32),
        lax.psum_scatter(
            value_terms.astype(jnp.bfloat16), "ctx", scatter_dimension=1, tiled=True
        ).astype(jnp.float32),
    )
    return (query_grad, key_grad, value_grad)


def spatial_forward(queries, key_rows, value_rows):
    scores = jnp.einsum(
        "pfchd,qfchd->fchpq", queries, key_rows, preferred_element_type=jnp.float32
    ) * HEAD_DIM ** (-0.5)
    log_total = jax.nn.logsumexp(scores, axis=-1, keepdims=True)
    weights = jnp.exp(scores - log_total).astype(jnp.bfloat16)
    heads_out = jnp.einsum(
        "fchpq,qfchd->pfchd", weights, value_rows, preferred_element_type=jnp.float32
    )
    return (heads_out.astype(jnp.bfloat16), (queries, key_rows, value_rows, log_total))


def spatial_backward(saved, heads_grad):
    queries, key_side, value_side, log_total = saved
    scale_factor = HEAD_DIM ** (-0.5)
    scores = (
        jnp.einsum("pfchd,qfchd->fchpq", queries, key_side, preferred_element_type=jnp.float32)
        * scale_factor
    )
    weights = jnp.exp(scores - log_total)
    weights_low = weights.astype(jnp.bfloat16)
    weight_grad = jnp.einsum(
        "pfchd,qfchd->fchpq", heads_grad, value_side, preferred_element_type=jnp.float32
    )
    score_grad = (
        weights * (weight_grad - jnp.sum(weights * weight_grad, axis=-1, keepdims=True))
    ).astype(jnp.bfloat16)
    query_grad = (
        jnp.einsum("fchpq,qfchd->pfchd", score_grad, key_side, preferred_element_type=jnp.float32)
        * scale_factor
    )
    key_grad = (
        jnp.einsum("fchpq,pfchd->qfchd", score_grad, queries, preferred_element_type=jnp.float32)
        * scale_factor
    )
    value_grad = jnp.einsum(
        "fchpq,pfchd->qfchd", weights_low, heads_grad, preferred_element_type=jnp.float32
    )
    return (query_grad, key_grad, value_grad)


def branch_forward(inputs, gain_row, joined_weight, proj_weight, attend):
    normed, norm_pull = jax.vjp(layer_norm, inputs, gain_row)
    normed_all = gather_rows(normed.astype(jnp.bfloat16))
    joined_rows = jnp.einsum(
        "pfcd,dke->pfcke", normed_all, joined_weight, preferred_element_type=jnp.float32
    ).astype(jnp.bfloat16)
    queries, key_rows, value_rows = split_heads(joined_rows)
    heads_out, saved = attend(queries, key_rows, value_rows)
    heads_flat = heads_out.reshape(heads_out.shape[:3] + (-1,))
    branch_out = scatter_rows(heads_flat, proj_weight, "pfce,ed->pfcd")
    return (branch_out, (norm_pull, normed_all, saved, heads_flat))


def branch_backward(carried, kept, joined_weight, proj_weight, attend_back):
    norm_pull, normed_all, saved, heads_flat = kept
    upstream = gather_grads(carried.astype(jnp.bfloat16))
    proj_grad = jnp.einsum(
        "pfce,pfcd->ed", heads_flat, upstream, preferred_element_type=jnp.float32
    )
    heads_grad = jnp.einsum(
        "pfcd,ed->pfce", upstream, proj_weight, preferred_element_type=jnp.float32
    ).astype(jnp.bfloat16)
    head_shape = heads_flat.shape[:3] + (heads_flat.shape[3] // HEAD_DIM, HEAD_DIM)
    query_grad, key_grad, value_grad = attend_back(saved, heads_grad.reshape(head_shape))
    joined_grad = jnp.stack(
        (
            query_grad.astype(jnp.bfloat16),
            key_grad.astype(jnp.bfloat16),
            value_grad.astype(jnp.bfloat16),
        ),
        axis=3,
    )
    joined_grad = joined_grad.reshape(joined_grad.shape[:4] + (-1,))
    joined_weight_grad = jnp.einsum(
        "pfcd,pfcke->dke", normed_all, joined_grad, preferred_element_type=jnp.float32
    )
    normed_grad = scatter_back(joined_grad, joined_weight, "pfcke,dke->pfcd")
    input_part, gain_grad = norm_pull(normed_grad)
    return (carried + input_part, gain_grad, joined_weight_grad, proj_grad)


def body(
    tokens,
    norm_gains,
    temporal_qkv,
    temporal_proj,
    spatial_qkv,
    spatial_proj,
    up_weight,
    down_weight,
    cotangent,
):
    gathered = (
        lax.all_gather(norm_gains, "fsdp", axis=1, tiled=True),
        lax.all_gather(temporal_qkv, "fsdp", axis=0, tiled=True),
        lax.all_gather(temporal_proj, "fsdp", axis=1, tiled=True),
        lax.all_gather(spatial_qkv, "fsdp", axis=0, tiled=True),
        lax.all_gather(spatial_proj, "fsdp", axis=1, tiled=True),
        lax.all_gather(up_weight, "fsdp", axis=0, tiled=True),
        lax.all_gather(down_weight, "fsdp", axis=1, tiled=True),
    )
    gain_table = gathered[0].astype(jnp.float32)
    inputs = tokens.astype(jnp.float32)
    temporal_out, temporal_kept = branch_forward(
        inputs, gain_table[0], gathered[1], gathered[2], temporal_forward
    )
    after_time = inputs + temporal_out
    spatial_out, spatial_kept = branch_forward(
        after_time, gain_table[1], gathered[3], gathered[4], spatial_forward
    )
    after_space = after_time + spatial_out
    normed, norm_pull = jax.vjp(layer_norm, after_space, gain_table[2])
    normed_all = gather_rows(normed.astype(jnp.bfloat16))
    hidden = jnp.einsum(
        "pfcd,dh->pfch", normed_all, gathered[5], preferred_element_type=jnp.float32
    )
    activated, gelu_pull = jax.vjp(exact_gelu, hidden)
    activated = activated.astype(jnp.bfloat16)
    block_out = (after_space + scatter_rows(activated, gathered[6], "pfch,hd->pfcd")).astype(
        jnp.bfloat16
    )
    back_weights = (
        lax.all_gather(temporal_qkv, "fsdp", axis=0, tiled=True),
        lax.all_gather(temporal_proj, "fsdp", axis=1, tiled=True),
        lax.all_gather(spatial_qkv, "fsdp", axis=0, tiled=True),
        lax.all_gather(spatial_proj, "fsdp", axis=1, tiled=True),
        lax.all_gather(up_weight, "fsdp", axis=0, tiled=True),
        lax.all_gather(down_weight, "fsdp", axis=1, tiled=True),
    )
    upstream = gather_grads(cotangent)
    down_grad = jnp.einsum("pfch,pfcd->hd", activated, upstream, preferred_element_type=jnp.float32)
    act_grad = jnp.einsum(
        "pfcd,hd->pfch", upstream, back_weights[5], preferred_element_type=jnp.float32
    )
    hidden_grad = gelu_pull(act_grad)[0].astype(jnp.bfloat16)
    up_grad = jnp.einsum(
        "pfcd,pfch->dh", normed_all, hidden_grad, preferred_element_type=jnp.float32
    )
    normed_grad = scatter_back(hidden_grad, back_weights[4], "pfch,dh->pfcd")
    space_part, third_gain = norm_pull(normed_grad)
    space_grad = cotangent.astype(jnp.float32) + space_part
    time_grad, second_gain, spatial_qkv_grad, spatial_proj_grad = branch_backward(
        space_grad, spatial_kept, back_weights[2], back_weights[3], spatial_backward
    )
    input_grad, first_gain, temporal_qkv_grad, temporal_proj_grad = branch_backward(
        time_grad, temporal_kept, back_weights[0], back_weights[1], temporal_backward
    )
    gain_grads = lax.psum(jnp.stack((first_gain, second_gain, third_gain)), "tp")
    weight_grads = (
        gain_grads,
        temporal_qkv_grad,
        temporal_proj_grad,
        spatial_qkv_grad,
        spatial_proj_grad,
        up_grad,
        down_grad,
    )
    weight_grads = (
        lax.psum(weight_grads[0].astype(jnp.bfloat16), "ctx").astype(jnp.float32),
        lax.psum(weight_grads[1].astype(jnp.bfloat16), "ctx").astype(jnp.float32),
        lax.psum(weight_grads[2].astype(jnp.bfloat16), "ctx").astype(jnp.float32),
        lax.psum(weight_grads[3].astype(jnp.bfloat16), "ctx").astype(jnp.float32),
        lax.psum(weight_grads[4].astype(jnp.bfloat16), "ctx").astype(jnp.float32),
        lax.psum(weight_grads[5].astype(jnp.bfloat16), "ctx").astype(jnp.float32),
        lax.psum(weight_grads[6].astype(jnp.bfloat16), "ctx").astype(jnp.float32),
    )
    shards = (
        lax.psum_scatter(
            weight_grads[0].astype(jnp.bfloat16), "fsdp", scatter_dimension=1, tiled=True
        ).astype(jnp.float32),
        lax.psum_scatter(
            weight_grads[1].astype(jnp.bfloat16), "fsdp", scatter_dimension=0, tiled=True
        ).astype(jnp.float32),
        lax.psum_scatter(
            weight_grads[2].astype(jnp.bfloat16), "fsdp", scatter_dimension=1, tiled=True
        ).astype(jnp.float32),
        lax.psum_scatter(
            weight_grads[3].astype(jnp.bfloat16), "fsdp", scatter_dimension=0, tiled=True
        ).astype(jnp.float32),
        lax.psum_scatter(
            weight_grads[4].astype(jnp.bfloat16), "fsdp", scatter_dimension=1, tiled=True
        ).astype(jnp.float32),
        lax.psum_scatter(
            weight_grads[5].astype(jnp.bfloat16), "fsdp", scatter_dimension=0, tiled=True
        ).astype(jnp.float32),
        lax.psum_scatter(
            weight_grads[6].astype(jnp.bfloat16), "fsdp", scatter_dimension=1, tiled=True
        ).astype(jnp.float32),
    )
    return (
        block_out,
        input_grad,
        shards[0],
        shards[1],
        shards[2],
        shards[3],
        shards[4],
        shards[5],
        shards[6],
    )


def solution(mesh):
    in_specs = (
        P("tp", "ctx", "fsdp", None),
        P(None, "fsdp"),
        P("fsdp", None, "tp"),
        P("tp", "fsdp"),
        P("fsdp", None, "tp"),
        P("tp", "fsdp"),
        P("fsdp", "tp"),
        P("tp", "fsdp"),
        P("tp", "ctx", "fsdp", None),
    )
    out_specs = (
        P("tp", "ctx", "fsdp", None),
        P("tp", "ctx", "fsdp", None),
        P(None, "fsdp"),
        P("fsdp", None, "tp"),
        P("tp", "fsdp"),
        P("fsdp", None, "tp"),
        P("tp", "fsdp"),
        P("fsdp", "tp"),
        P("tp", "fsdp"),
    )
    return jax.shard_map(body, mesh=mesh, in_specs=in_specs, out_specs=out_specs, check_vma=False)
```

profile of v0, /device:TPU:1, one launch (start us, length us, event | category | flops | bytes accessed | tf_op | source)
XLA Modules:
  0.0 947.6 jit_solution(7955408466041700331)
XLA Ops:
  17.8 10.8 %all_gather.53 = bf16[768,3,192]{0,2,1:T(8,128)(2,1)S(1)} all-gather(bf16[384,3,192]{0,2,1:T(8,128)(2,1)S(1)} %copy-done.40), channel_id=1, replica_groups=mesh['fsdp'=2,'ctx'=4,'tp'=4] {'fsdp'}, dimensions={0}, use_global_device_ids=true | all-gather | bytes 1327104 | tf_op jit(solution)/shard_map/all_gather | solution.py:217
  28.6 22.2 %all-gather.11.cloned.1.call-done = bf16[196,2,2,768]{3,2,1,0:T(2,128)(2,1)} async-done(((bf16[49,2,2,768]{3,2,1,0:T(2,128)(2,1)}), bf16[196,2,2,768]{3,2,1,0:T(2,128)(2,1)}) %all-gather.11.cloned.1.call-update) | async-done | bytes 1204240 | tf_op jit(solution)/shard_map/all_gather | solution.py:28
  60.3 13.8 %all-gather.15.cloned.1.call-done = bf16[196,8,2,3,64]{0,4,3,2,1:T(8,128)(2,1)} async-done(((bf16[196,2,2,3,64]{0,4,3,2,1:T(8,128)(2,1)}), bf16[196,8,2,3,64]{0,4,3,2,1:T(8,128)(2,1)}) %all-gather.15.cloned.1.call-update) | async-done | bytes 1204240 | tf_op jit(solution)/shard_map/all_gather | solution.py:99
  86.2 9.7 %all-gather.13.cloned.1.call-done = bf16[196,8,2,3,64]{0,4,3,2,1:T(8,128)(2,1)} async-done(((bf16[196,2,2,3,64]{0,4,3,2,1:T(8,128)(2,1)}), bf16[196,8,2,3,64]{0,4,3,2,1:T(8,128)(2,1)}) %all-gather.13.cloned.1.call-update) | async-done | bytes 1204240 | tf_op jit(solution)/shard_map/all_gather | solution.py:100
  108.9 55.2 %all-reduce.15.cloned.1.call-done = bf16[196,2,2,768]{3,2,1,0:T(2,128)(2,1)} async-done(((bf16[196,2,2,768]{3,2,1,0:T(2,128)(2,1)}), bf16[196,2,2,768]{3,2,1,0:T(2,128)(2,1)}) %all-reduce.15.cloned.1.call-update) | async-done | bytes 1204240
  170.2 5.7 all_gather.59
  175.9 11.1 %all_gather.58 = bf16[768,3,192]{0,2,1:T(8,128)(2,1)S(1)} all-gather(bf16[384,3,192]{0,2,1:T(8,128)(2,1)S(1)} %copy-done.41), channel_id=1, replica_groups=mesh['fsdp'=2,'ctx'=4,'tp'=4] {'fsdp'}, dimensions={0}, use_global_device_ids=true | all-gather | bytes 1327104 | tf_op jit(solution)/shard_map/all_gather | solution.py:219
  187.0 12.9 %all-gather.17.cloned.1.call-done = bf16[196,2,2,768]{3,2,1,0:T(2,128)(2,1)} async-done(((bf16[49,2,2,768]{3,2,1,0:T(2,128)(2,1)}), bf16[196,2,2,768]{3,2,1,0:T(2,128)(2,1)}) %all-gather.17.cloned.1.call-update) | async-done | bytes 1204240 | tf_op jit(solution)/shard_map/all_gather | solution.py:28
  208.4 56.2 %all-reduce.17.cloned.1.call-done = bf16[196,2,2,768]{3,2,1,0:T(2,128)(2,1)} async-done(((bf16[196,2,2,768]{3,2,1,0:T(2,128)(2,1)}), bf16[196,2,2,768]{3,2,1,0:T(2,128)(2,1)}) %all-reduce.17.cloned.1.call-update) | async-done | bytes 1204240
  278.0 27.7 %all-gather.19.cloned.1.call-done = bf16[196,2,2,768]{3,2,1,0:T(2,128)(2,1)} async-done(((bf16[49,2,2,768]{3,2,1,0:T(2,128)(2,1)}), bf16[196,2,2,768]{3,2,1,0:T(2,128)(2,1)}) %all-gather.19.cloned.1.call-update) | async-done | bytes 1204240 | tf_op jit(solution)/shard_map/all_gather | solution.py:28
  310.5 6.6 multiply_convert_fusion.2
  317.1 12.3 %all-gather.23.cloned.1.call-done = bf16[768,768]{1,0:T(8,128)(2,1)} async-done(((bf16[768,384]{1,0:T(8,128)(2,1)}), bf16[768,768]{1,0:T(8,128)(2,1)}) %all-gather.23.cloned.1.call-update) | async-done | bytes 1179664 | tf_op jit(solution)/shard_map/all_gather | solution.py:222
  329.5 31.8 %all-gather.25.cloned.1.call-done = bf16[196,2,2,768]{3,2,1,0:T(2,128)(2,1)} async-done(((bf16[49,2,2,768]{3,2,1,0:T(2,128)(2,1)}), bf16[196,2,2,768]{3,2,1,0:T(2,128)(2,1)}) %all-gather.25.cloned.1.call-update) | async-done | bytes 1204240 | tf_op jit(solution)/shard_map/all_gather | solution.py:32
  361.2 4.9 add_convert_fusion
  369.4 56.2 %all-reduce.19.cloned.1.call-done = bf16[196,2,2,768]{3,2,1,0:T(2,128)(2,1)} async-done(((bf16[196,2,2,768]{3,2,1,0:T(2,128)(2,1)}), bf16[196,2,2,768]{3,2,1,0:T(2,128)(2,1)}) %all-reduce.19.cloned.1.call-update) | async-done | bytes 1204240
  440.9 29.7 %all-gather.27.cloned.1.call-done = bf16[196,2,2,768]{3,2,1,0:T(2,128)(2,1)} async-done(((bf16[49,2,2,768]{3,2,1,0:T(2,128)(2,1)}), bf16[196,2,2,768]{3,2,1,0:T(2,128)(2,1)}) %all-gather.27.cloned.1.call-update) | async-done | bytes 1204240 | tf_op jit(solution)/shard_map/all_gather | solution.py:32
  480.4 56.2 %all-reduce.21.cloned.1.call-done = bf16[196,2,2,768]{3,2,1,0:T(2,128)(2,1)} async-done(((bf16[196,2,2,768]{3,2,1,0:T(2,128)(2,1)}), bf16[196,2,2,768]{3,2,1,0:T(2,128)(2,1)}) %all-reduce.21.cloned.1.call-update) | async-done | bytes 1204240
  546.8 30.1 %all-gather.29.cloned.1.call-done = bf16[196,2,2,768]{3,2,1,0:T(2,128)(2,1)} async-done(((bf16[49,2,2,768]{3,2,1,0:T(2,128)(2,1)}), bf16[196,2,2,768]{3,2,1,0:T(2,128)(2,1)}) %all-gather.29.cloned.1.call-update) | async-done | bytes 1204240 | tf_op jit(solution)/shard_map/all_gather | solution.py:32
  581.5 5.2 convert_bitcast_fusion
  591.6 5.1 multiply_reduce_fusion.2
  614.3 5.0 reduce-scatter.24.cloned.1.call-done
  619.3 30.9 %reduce-scatter.22.cloned.1.call-done = bf16[196,2,2,3,64]{0,4,3,2,1:T(8,128)(2,1)} async-done(((bf16[196,8,2,3,64]{0,4,3,2,1:T(8,128)(2,1)}), bf16[196,2,2,3,64]{0,4,3,2,1:T(8,128)(2,1)}) %reduce-scatter.22.cloned.1.call-update) | async-done | bytes 301072 | tf_op jit(solution)/shard_map/reduce_scatter | solution.py:112
  678.0 74.3 %all-reduce.23.cloned.1.call-done = (bf16[196,2,2,768]{3,2,1,0:T(2,128)(2,1)}, bf16[196,2,2,768]{3,2,1,0:T(2,128)(2,1)}) async-done(((bf16[196,2,2,768]{3,2,1,0:T(2,128)(2,1)}, bf16[196,2,2,768]{3,2,1,0:T(2,128)(2,1)}), (bf16[196,2,2,768]{3,2,1,0:T(2,128)(2,1)}, bf16[196,2,2,768]{3,2,1,0:T(2,128)(2,1)})) %all-reduce.23.cloned.1.call-update) | async-done | bytes 2408464
  756.9 13.0 %psum.56 = bf16[3,768]{1,0:T(4,128)(2,1)S(1)} all-reduce(f32[3,768]{1,0:T(4,128)S(1)} %pad_maximum_fusion.2), channel_id=1, replica_groups=mesh['fsdp'=2,'ctx'=4,'tp'=4] {'tp'}, use_global_device_ids=true, to_apply=%region_29.0 | all-reduce | flops 2304 | bytes 13824 | tf_op jit(solution)/shard_map/psum | solution.py:270
  777.6 13.2 %reduce-scatter.36.cloned.1.call-done = bf16[384,192]{1,0:T(8,128)(2,1)} async-done(((bf16[768,192]{1,0:T(8,128)(2,1)}), bf16[384,192]{1,0:T(8,128)(2,1)}) %reduce-scatter.36.cloned.1.call-update) | async-done | bytes 147472
  792.6 20.0 %reduce-scatter.34.cloned.1.call-done = bf16[384,576]{1,0:T(8,128)(2,1)} async-done(((bf16[768,576]{1,0:T(8,128)(2,1)}), bf16[384,576]{1,0:T(8,128)(2,1)}) %reduce-scatter.34.cloned.1.call-update) | async-done | bytes 442384
  814.6 13.4 %reduce-scatter.32.cloned.1.call-done = bf16[384,192]{1,0:T(8,128)(2,1)} async-done(((bf16[768,192]{1,0:T(8,128)(2,1)}), bf16[384,192]{1,0:T(8,128)(2,1)}) %reduce-scatter.32.cloned.1.call-update) | async-done | bytes 147472
  829.7 20.0 %reduce-scatter.30.cloned.1.call-done = bf16[384,576]{1,0:T(8,128)(2,1)} async-done(((bf16[768,576]{1,0:T(8,128)(2,1)}), bf16[384,576]{1,0:T(8,128)(2,1)}) %reduce-scatter.30.cloned.1.call-update) | async-done | bytes 442384
  851.7 22.6 %reduce-scatter.26.cloned.1.call-done = bf16[384,768]{1,0:T(8,128)(2,1)} async-done(((bf16[768,768]{1,0:T(8,128)(2,1)}), bf16[384,768]{1,0:T(8,128)(2,1)}) %reduce-scatter.26.cloned.1.call-update) | async-done | bytes 589840 | tf_op jit(solution)/shard_map/reduce_scatter | solution.py:305
  879.1 8.9 reduce-scatter.28.cloned.1.call-done
  889.0 6.1 psum.64
  895.7 35.3 %all-reduce.25.cloned.1.call-done = (bf16[384,3,192]{0,2,1:T(8,128)(2,1)}, bf16[192,384]{1,0:T(8,128)(2,1)}, bf16[384,3,192]{0,2,1:T(8,128)(2,1)}, bf16[192,384]...) async-done(((bf16[384,3,192]{0,2,1:T(8,128)(2,1)}, bf16[192,384]{1,0:T(8,128)(2,1)}, bf16[384,3,192]{0,2,1:T(8,128)(2,1)}, ...) | async-done | bytes 2359312 | tf_op jit(solution)/shard_map/psum | solution.py:282
  (305 shorter events, 203.4 us)
Async XLA Ops:
  8.0 42.8 %all-gather.11.cloned.1.call-start = ((), (), s32[]{:S(2)}) async-start(), calls=%async_computation.9 | async-start | bytes 1505280 | tf_op jit(solution)/shard_map/all_gather | solution.py:28
  17.7 56.3 %all-gather.15.cloned.1.call-start = ((), (), s32[]{:S(2)}) async-start(), calls=%async_computation.11 | async-start | bytes 1966080 | tf_op jit(solution)/shard_map/all_gather | solution.py:99
  54.2 41.7 %all-gather.13.cloned.1.call-start = ((), (), s32[]{:S(2)}) async-start(), calls=%async_computation.10 | async-start | bytes 1966080 | tf_op jit(solution)/shard_map/all_gather | solution.py:100
  54.9 109.3 %all-reduce.15.cloned.1.call-start = ((), (), s32[]{:S(2)}) async-start(), calls=%async_computation.28 | async-start | bytes 2408448
  107.4 62.7 %copy-start.50 = (bf16[192,384]{1,0:T(8,128)(2,1)S(1)}, bf16[192,384]{1,0:T(8,128)(2,1)}, u32[]{:S(2)}) copy-start(bf16[192,384]{1,0:T(8,128)(2,1)} %param.14) | copy-start | bytes 442372
  107.4 92.5 %all-gather.17.cloned.1.call-start = ((), (), s32[]{:S(2)}) async-start(), calls=%async_computation.12 | async-start | bytes 1505280 | tf_op jit(solution)/shard_map/all_gather | solution.py:28
  108.9 67.0 %copy-start.41 = (bf16[384,3,192]{0,2,1:T(8,128)(2,1)S(1)}, bf16[384,3,192]{0,2,1:T(8,128)(2,1)}, u32[]{:S(2)}) copy-start(bf16[384,3,192]{0,2,1:T(8,128)(2,1)} %param.13) | copy-start | bytes 1327108
  170.1 94.5 %all-reduce.17.cloned.1.call-start = ((), (), s32[]{:S(2)}) async-start(), calls=%async_computation.29 | async-start | bytes 2408448
  207.7 70.3 %all-gather.21.cloned.1.call-start = ((), (), s32[]{:S(2)}) async-start(), calls=%async_computation.14 | async-start | bytes 1769472 | tf_op jit(solution)/shard_map/all_gather | solution.py:221
  208.3 97.4 %all-gather.19.cloned.1.call-start = ((), (), s32[]{:S(2)}) async-start(), calls=%async_computation.13 | async-start | bytes 1505280 | tf_op jit(solution)/shard_map/all_gather | solution.py:28
  276.2 53.2 %all-gather.23.cloned.1.call-start = ((), (), s32[]{:S(2)}) async-start(), calls=%async_computation.15 | async-start | bytes 1769472 | tf_op jit(solution)/shard_map/all_gather | solution.py:222
  276.8 84.4 %all-gather.25.cloned.1.call-start = ((), (), s32[]{:S(2)}) async-start(), calls=%async_computation.16 | async-start | bytes 1505280 | tf_op jit(solution)/shard_map/all_gather | solution.py:32
  277.6 148.0 %all-reduce.19.cloned.1.call-start = ((), (), s32[]{:S(2)}) async-start(), calls=%async_computation.30 | async-start | bytes 2408448
  369.4 101.3 %all-gather.27.cloned.1.call-start = ((), (), s32[]{:S(2)}) async-start(), calls=%async_computation.17 | async-start | bytes 1505280 | tf_op jit(solution)/shard_map/all_gather | solution.py:32
  440.7 95.9 %all-reduce.21.cloned.1.call-start = ((), (), s32[]{:S(2)}) async-start(), calls=%async_computation.31 | async-start | bytes 2408448
  480.3 58.9 %copy-start.52 = (f32[49,2,2]{0,2,1:T(2,128)S(1)}, f32[49,2,2]{0,2,1:T(2,128)}, u32[]{:S(2)}) copy-start(f32[49,2,2]{0,2,1:T(2,128)} %copy-done.51) | copy-start | bytes 2356
  480.3 63.7 %copy-start.1 = (f32[49,2,2,768]{3,2,1,0:T(2,128)S(1)}, f32[49,2,2,768]{3,2,1,0:T(2,128)}, u32[]{:S(2)}) copy-start(f32[49,2,2,768]{3,2,1,0:T(2,128)} %get-tuple-element.51) | copy-start | bytes 1806340
  480.3 63.7 %copy-start.13 = (bf16[49,2,2,768]{3,2,1,0:T(2,128)(2,1)S(1)}, bf16[49,2,2,768]{3,2,1,0:T(2,128)(2,1)}, u32[]{:S(2)}) copy-start(bf16[49,2,2,768]{3,2,1,0:T(2,128)(2,1)} %param.17) | copy-start | bytes 903172
  480.3 63.7 %copy-start.39 = (f32[49,2,2]{2,1,0:T(2,128)S(1)}, f32[49,2,2]{2,1,0:T(2,128)}, u32[]{:S(2)}) copy-start(f32[49,2,2]{2,1,0:T(2,128)} %copy-done.38) | copy-start | bytes 2356
  480.4 96.5 %all-gather.29.cloned.1.call-start = ((), (), s32[]{:S(2)}) async-start(), calls=%async_computation.18 | async-start | bytes 1505280 | tf_op jit(solution)/shard_map/all_gather | solution.py:32
  546.7 72.6 %reduce-scatter.24.cloned.1.call-start = ((), (), s32[]{:S(2)}) async-start(), calls=%async_computation.20 | async-start | bytes 1966080 | tf_op jit(solution)/shard_map/reduce_scatter | solution.py:115
  591.3 58.9 %reduce-scatter.22.cloned.1.call-start = ((), (), s32[]{:S(2)}) async-start(), calls=%async_computation.19 | async-start | bytes 1966080 | tf_op jit(solution)/shard_map/reduce_scatter | solution.py:112
  605.8 146.4 %all-reduce.23.cloned.1.call-start = ((), (), s32[]{:S(2)}) async-start(), calls=%async_computation.32 | async-start | bytes 4816896
  655.0 120.5 %reduce-scatter.38.cloned.1.call-start = ((), (), s32[]{:S(2)}) async-start(), calls=%async_computation.27 | async-start | bytes 1769472
  659.6 131.3 %reduce-scatter.36.cloned.1.call-start = ((), (), s32[]{:S(2)}) async-start(), calls=%async_computation.26 | async-start | bytes 589824
  662.4 150.2 %reduce-scatter.34.cloned.1.call-start = ((), (), s32[]{:S(2)}) async-start(), calls=%async_computation.25 | async-start | bytes 1474560
  666.4 161.5 %reduce-scatter.32.cloned.1.call-start = ((), (), s32[]{:S(2)}) async-start(), calls=%async_computation.24 | async-start | bytes 589824
  670.0 179.7 %reduce-scatter.30.cloned.1.call-start = ((), (), s32[]{:S(2)}) async-start(), calls=%async_computation.23 | async-start | bytes 1474560
  674.0 200.2 %reduce-scatter.26.cloned.1.call-start = ((), (), s32[]{:S(2)}) async-start(), calls=%async_computation.21 | async-start | bytes 1769472 | tf_op jit(solution)/shard_map/reduce_scatter | solution.py:305
  677.9 76.4 %copy-start.31 = (f32[49,2,2]{2,1,0:T(2,128)S(1)}, f32[49,2,2]{2,1,0:T(2,128)}, u32[]{:S(2)}) copy-start(f32[49,2,2]{2,1,0:T(2,128)} %copy-done.30) | copy-start | bytes 2356
  677.9 210.1 %reduce-scatter.28.cloned.1.call-start = ((), (), s32[]{:S(2)}) async-start(), calls=%async_computation.22 | async-start | bytes 294912
  770.8 160.2 %all-reduce.25.cloned.1.call-start = ((), (), s32[]{:S(2)}) async-start(), calls=%async_computation.33 | async-start | bytes 4718592 | tf_op jit(solution)/shard_map/psum | solution.py:282
  (52 other events, 600.8 us)
Sparse Core Ops, SparseCore 0:
  17.9 32.8 all-gather.10
  54.3 19.7 all-gather.14
  76.2 19.6 all-gather.12
  107.5 56.6 all-reduce.14
  170.2 29.6 all-gather.16
  207.9 56.6 all-reduce.16
  546.8 30.0 all-gather.28
  591.4 27.8 reduce-scatter.23
  622.0 28.1 reduce-scatter.21
  874.4 56.5 all-reduce.24
Sparse Core Ops, SparseCore 1:
  209.7 22.2 all-gather.20
  276.3 29.4 all-gather.18
  307.2 22.3 all-gather.22
  331.1 30.1 all-gather.24
  369.4 56.1 all-reduce.18
  440.8 29.8 all-gather.26
  480.4 56.1 all-reduce.20
  655.1 97.1 all-reduce.22
  755.0 20.4 reduce-scatter.37
  777.8 13.0 reduce-scatter.35
  793.1 19.5 reduce-scatter.33
  814.9 13.0 reduce-scatter.31
  830.2 19.5 reduce-scatter.29
  852.5 21.6 reduce-scatter.25
  877.1 10.8 reduce-scatter.27
where the time goes:
time: 959 us; the launch traced here: 948 us
  waiting for transfers between devices  665 us (69%)
  local copies, waits for them, and re-layouts  71.4 us (7%)
  other arithmetic  69.8 us (7%)
  matrix products  65.4 us (7%)
  blocking collectives  55.5 us (6%)
  between operations  18.1 us (2%)
    unnamed x36, waiting for transfers between devices  381 us
    all_gather x3, waiting for transfers between devices, gather_grads(): return lax.all_gather(values, 'tp', axis=0, tiled=True)  91.6 us
    all_gather x3, waiting for transfers between devices, gather_rows(): return lax.all_gather(values, 'tp', axis=0, tiled=True)  62.8 us
    psum x1, waiting for transfers between devices, body(): lax.psum(weight_grads[1].astype(jnp.bfloat16), 'ctx').astype(jnp.float32)  35.3 us
    reduce_scatter x1, waiting for transfers between devices, temporal_backward(): lax.psum_scatter(key_terms.astype(jnp.bfloat16), 'ctx', scatter_dimension...  30.9 us
    unnamed x131, local copies, waits for them, and re-layouts  24.5 us
    reduce_scatter x1, waiting for transfers between devices, body(): lax.psum_scatter(weight_grads[5].astype(jnp.bfloat16), 'fsdp', scatter_di...  22.6 us
  transfers between devices with their start and end apart: 25, of which 24 were waited for; matrix products, arithmetic and copies ran while one was open for 10% of the time, Pallas kernels for 0%

commit v1 on v0

v1 whole, which is shorter than its diff:
```python
import functools

import jax
import jax.numpy as jnp
from jax import lax
from jax.experimental import pallas as pl
from jax.experimental.pallas import tpu as pltpu
from jax.sharding import PartitionSpec as P

HEAD_DIM = 64
EPSILON = 1e-06
SCALE = HEAD_DIM ** (-0.5)
F32 = jnp.float32
LOW = jnp.bfloat16
VMEM = pltpu.VMEM


def dot(a, b, ca, cb):
    return lax.dot_general(a, b, (((ca,), (cb,)), ((), ())), preferred_element_type=F32)


def statistics(rows):
    center = rows - jnp.mean(rows, axis=-1, keepdims=True)
    rate = lax.rsqrt(jnp.mean(center * center, axis=-1, keepdims=True) + EPSILON)
    return center * rate, rate


def norm_back(grad, gain, hat, rate):
    t = grad * gain
    return rate * (
        t
        - jnp.mean(t, axis=-1, keepdims=True)
        - hat * jnp.mean(t * hat, axis=-1, keepdims=True)
    )


def to_blocks(own, pair, frames_cut):
    if not frames_cut:
        return jnp.concatenate((own, pair), axis=0)
    half = own.shape[0] // 2
    return jnp.concatenate((own[:half], pair[:half], own[half:], pair[half:]), axis=0)


def from_blocks(rows, frames_cut):
    if not frames_cut:
        return rows
    q = rows.shape[0] // 4
    return jnp.concatenate((rows[:q], rows[2 * q : 3 * q], rows[q : 2 * q], rows[3 * q :]), axis=0)


def columns(off_ref, piece, width):
    return pl.ds(pl.multiple_of(off_ref[piece], 128), width)


def attend_forward_kernel(pieces, frames_cut, *refs):
    off, own, pair, gain, bias = refs[:5]
    weights = refs[5 : 5 + 2 * pieces]
    part, normed, joined_a, joined_b, out_a, out_b, total = refs[5 + 2 * pieces :]
    rows = to_blocks(own[...].astype(F32), pair[...].astype(F32), frames_cut)
    hat, _ = statistics(rows)
    normed[...] = (hat * gain[...]).astype(LOW)
    width = weights[0].shape[0]
    heads3 = joined_a.shape[1]
    for group, joined in enumerate((joined_a, joined_b)):
        acc = None
        for p in range(pieces):
            w = weights[group * pieces + p]
            term = dot(normed[:, columns(off, p, width)], w[:, :heads3], 1, 0)
            acc = term if acc is None else acc + term
        joined[...] = acc.astype(LOW)
    block = normed.shape[0] // 2
    inner = heads3 // 3

    def one_block(b, carry):
        at = pl.ds(pl.multiple_of(b * block, 16), block)
        for joined, out in ((joined_a, out_a), (joined_b, out_b)):
            rows3 = joined[at, :]
            parts = []
            for h in range(inner // HEAD_DIM):
                lo = h * HEAD_DIM
                q = rows3[:, lo : lo + HEAD_DIM]
                k = rows3[:, inner + lo : inner + lo + HEAD_DIM]
                v = rows3[:, 2 * inner + lo : 2 * inner + lo + HEAD_DIM]
                s = dot(q, k, 1, 1) * SCALE + bias[...]
                e = jnp.exp(s - jnp.max(s, axis=-1, keepdims=True))
                w = (e / jnp.sum(e, axis=-1, keepdims=True)).astype(LOW)
                parts.append(dot(w, v, 1, 0))
            out[at, :] = jnp.concatenate(parts, axis=1).astype(LOW)
        return carry

    lax.fori_loop(0, 2, one_block, 0)
    for p in range(pieces):
        total[:, columns(off, p, width)] = dot(
            out_a[...], weights[p][:, heads3:], 1, 1
        ) + dot(out_b[...], weights[pieces + p][:, heads3:], 1, 1)
    part[...] = from_blocks(total[...], frames_cut).astype(LOW)


def attend_backward_kernel(pieces, frames_cut, *refs):
    n_in = 10 if frames_cut else 2
    off, bias, normed, joined_a, joined_b, out_a, out_b = refs[:7]
    head = refs[7 : 7 + n_in]
    weights = refs[7 + n_in : 7 + n_in + 2 * pieces]
    rest = list(refs[7 + n_in + 2 * pieces :])
    part = rest.pop(0)
    grads = [rest.pop(0) for _ in range(pieces)]
    if frames_cut:
        carried, gain_grad = rest.pop(0), rest.pop(0)
    upstream, djoined_a, djoined_b, dout_a, dout_b, total = rest
    half = upstream.shape[0] // 2
    if frames_cut:
        base_own, base_pair, add_l, add_r, grad_l, grad_r, gain, cot_own, cot_pair, _ = head
        both = []
        for lo, base, cot in ((0, base_own, cot_own), (half, base_pair, cot_pair)):
            at = slice(lo, lo + half)
            rows = base[...].astype(F32) + (add_l[at, :].astype(F32) + add_r[at, :].astype(F32))
            hat, rate = statistics(rows)
            dn = grad_l[at, :].astype(F32) + grad_r[at, :].astype(F32)
            dx = cot[...].astype(F32) + norm_back(dn, gain[...], hat, rate)
            if lo == 0:
                carried[...] = dx
                gain_grad[...] = jnp.sum(dn * hat, axis=0, keepdims=True)
            both.append(dx)
        upstream[...] = to_blocks(both[0], both[1], frames_cut).astype(LOW)
    else:
        upstream[:half, :] = head[0][...]
        upstream[half:, :] = head[1][...]
    width = weights[0].shape[0]
    heads3 = joined_a.shape[1]
    inner = heads3 // 3
    for group, (out, dout) in enumerate(((out_a, dout_a), (out_b, dout_b))):
        acc = None
        for p in range(pieces):
            w = weights[group * pieces + p]
            dy = upstream[:, columns(off, p, width)]
            term = dot(dy, w[:, heads3:], 1, 0)
            acc = term if acc is None else acc + term
            grads[p][group, :, heads3:] = dot(dy, out[...], 0, 0).astype(LOW)
        dout[...] = acc.astype(LOW)

    def one_block(b, carry):
        at = pl.ds(pl.multiple_of(b * half, 16), half)
        for joined, dout, djoined in (
            (joined_a, dout_a, djoined_a),
            (joined_b, dout_b, djoined_b),
        ):
            rows3 = joined[at, :]
            do3 = dout[at, :]
            dqs, dks, dvs = [], [], []
            for h in range(inner // HEAD_DIM):
                lo = h * HEAD_DIM
                q = rows3[:, lo : lo + HEAD_DIM]
                k = rows3[:, inner + lo : inner + lo + HEAD_DIM]
                v = rows3[:, 2 * inner + lo : 2 * inner + lo + HEAD_DIM]
                do = do3[:, lo : lo + HEAD_DIM]
                s = dot(q, k, 1, 1) * SCALE + bias[...]
                e = jnp.exp(s - jnp.max(s, axis=-1, keepdims=True))
                w = e / jnp.sum(e, axis=-1, keepdims=True)
                dw = dot(do, v, 1, 1)
                ds = (w * (dw - jnp.sum(w * dw, axis=-1, keepdims=True))).astype(LOW)
                dqs.append(dot(ds, k, 1, 0) * SCALE)
                dks.append(dot(ds, q, 0, 0) * SCALE)
                dvs.append(dot(w.astype(LOW), do, 0, 0))
            djoined[at, :] = jnp.concatenate(dqs + dks + dvs, axis=1).astype(LOW)
        return carry

    lax.fori_loop(0, 2, one_block, 0)
    for p in range(pieces):
        cols = columns(off, p, width)
        wide = normed[:, cols]
        for group, djoined in enumerate((djoined_a, djoined_b)):
            grads[p][group, :, :heads3] = dot(wide, djoined[...], 0, 0).astype(LOW)
        total[:, cols] = dot(djoined_a[...], weights[p][:, :heads3], 1, 1) + dot(
            djoined_b[...], weights[pieces + p][:, :heads3], 1, 1
        )
    part[...] = from_blocks(total[...], frames_cut).astype(LOW)


def feed_kernel(pieces, chunks, packed, *refs):
    off, base_own, base_pair, add_l, add_r, gain, cot_own, cot_pair = refs[:8]
    at = 8
    n_w = chunks * pieces * (1 if packed else 2)
    weights = refs[at : at + n_w]
    at += n_w
    out_part, dn_part = refs[at : at + 2]
    at += 2
    grads = refs[at : at + n_w // 2]
    at += n_w // 2
    normed, cot, total, dtotal = refs[at:]
    half = normed.shape[0] // 2
    for lo, base, c in ((0, base_own, cot_own), (half, base_pair, cot_pair)):
        rows_at = slice(lo, lo + half)
        rows = base[...].astype(F32) + (
            add_l[rows_at, :].astype(F32) + add_r[rows_at, :].astype(F32)
        )
        hat, _ = statistics(rows)
        normed[rows_at, :] = (hat * gain[...]).astype(LOW)
        cot[rows_at, :] = c[...]
    for c in range(chunks):
        group, side = c % 2, c // 2
        ups, downs, up_grads, down_grads = [], [], [], []
        for p in range(pieces):
            k = side * pieces + p
            if packed:
                w, g = weights[c * pieces + p], grads[k]
                wide = w.shape[0] // 2
                ups.append(w[:wide, :])
                downs.append(w[wide:, :])
                up_grads.append(g.at[group, :wide, :])
                down_grads.append(g.at[group, wide:, :])
            else:
                ups.append(weights[2 * (c * pieces + p)][...])
                downs.append(weights[2 * (c * pieces + p) + 1][...])
                up_grads.append(grads[2 * k].at[group])
                down_grads.append(grads[2 * k + 1].at[group])
        width = ups[0].shape[0]
        hidden = dact = None
        for p in range(pieces):
            cols = columns(off, p, width)
            term = dot(normed[:, cols], ups[p], 1, 0)
            dterm = dot(cot[:, cols], downs[p], 1, 1)
            hidden = term if hidden is None else hidden + term
            dact = dterm if dact is None else dact + dterm
        cdf = 0.5 * (1.0 + lax.erf(hidden * (2.0**-0.5)))
        act = (hidden * cdf).astype(LOW)
        slope = cdf + hidden * (jnp.exp(-0.5 * hidden * hidden) * (2.0 * jnp.pi) ** -0.5)
        dhid = (dact * slope).astype(LOW)
        for p in range(pieces):
            cols = columns(off, p, width)
            term = dot(act, downs[p], 1, 0)
            dterm = dot(dhid, ups[p], 1, 1)
            if c == 0:
                total[:, cols] = term
                dtotal[:, cols] = dterm
            else:
                total[:, cols] += term
                dtotal[:, cols] += dterm
            up_grads[p][...] = dot(normed[:, cols], dhid, 0, 0).astype(LOW)
            down_grads[p][...] = dot(act, cot[:, cols], 0, 0).astype(LOW)
    out_part[...] = total[...].astype(LOW)
    dn_part[...] = dtotal[...].astype(LOW)


def norm_back_kernel(part, received, base, gain, carried, out, gain_grad):
    hat, rate = statistics(base[...].astype(F32))
    dn = part[: base.shape[0], :].astype(F32) + received[...].astype(F32)
    out[...] = (carried[...].astype(F32) + norm_back(dn, gain[...], hat, rate)).astype(out.dtype)
    gain_grad[...] = jnp.sum(dn * hat, axis=0, keepdims=True)


def in_vmem(n):
    return [pl.BlockSpec(memory_space=VMEM)] * n


def shape_of(shape, dtype):
    return jax.ShapeDtypeStruct(shape, dtype)


def run(kernel, operands, outs, scratch, flops, name):
    moved = sum(o.size * o.dtype.itemsize for o in operands) + sum(
        o.size * o.dtype.itemsize for o in outs
    )
    scalar = operands[0].dtype == jnp.int32
    specs = in_vmem(len(operands))
    if scalar:
        specs[0] = pl.BlockSpec(memory_space=pltpu.SMEM)
    return pl.pallas_call(
        kernel,
        out_shape=outs,
        in_specs=specs,
        out_specs=in_vmem(len(outs)),
        scratch_shapes=scratch,
        compiler_params=pltpu.CompilerParams(vmem_limit_bytes=48 << 20),
        cost_estimate=pl.CostEstimate(flops=flops, bytes_accessed=moved, transcendentals=0),
        name=name,
    )(*operands)


def body(sizes, tokens, norm_gains, temporal_qkv, temporal_proj, spatial_qkv, spatial_proj, up_weight, down_weight, cotangent):
    n_fsdp, n_ctx, n_tp = sizes
    swap = n_fsdp == 2
    d_model = tokens.shape[3]
    d_part = d_model // n_fsdp
    places = tokens.shape[0]
    block = 2 * (-(-places // 4))
    x, i, z = lax.axis_index("fsdp"), lax.axis_index("ctx"), lax.axis_index("tp")
    core, chip = i % 2, i // 2
    is_source = (z // 2) == core

    def permute_ctx(v, bits):
        return lax.ppermute(v, "ctx", [(a, a ^ bits) for a in range(n_ctx)])

    def permute_tp(v, bits):
        return lax.ppermute(v, "tp", [(a, a ^ bits) for a in range(n_tp)])

    def permute_fsdp(v):
        return lax.ppermute(v, "fsdp", [(0, 1), (1, 0)])

    outward, inward = [], []
    for a in range(n_ctx):
        for b in (2 * (a % 2), 2 * (a % 2) + 1):
            outward.append((a * n_tp + b, a * n_tp + (b ^ 2)))
            inward.append((a * n_tp + (b ^ 2), a * n_tp + b))

    def exclusive(parts, bits):
        low, high = (bits & 1) == 1, (bits & 2) == 2
        parts = [jnp.where(low, parts[d ^ 1], parts[d]) for d in range(4)]
        return [jnp.where(high, parts[d ^ 2], parts[d]) for d in range(4)]

    slot_bits = (z & 2) | ((z & 1) ^ core)

    def to_time(rows):
        t = jnp.transpose(rows, (2, 1, 0, 3))
        t = jnp.pad(t, ((0, 0), (0, 0), (0, 2 * block - places), (0, 0)))
        parts = [t[c, :, b * block : (b + 1) * block] for c in range(2) for b in range(2)]
        parts = exclusive(parts, i)
        got = [parts[0]] + [permute_ctx(parts[e], e) for e in range(1, 4)]
        return jnp.stack(exclusive(got, slot_bits))

    def from_time(own):
        parts = exclusive([own[d] for d in range(4)], slot_bits)
        got = [parts[0]] + [permute_ctx(parts[e], e) for e in range(1, 4)]
        got = exclusive(got, i)
        t = jnp.stack(
            [jnp.concatenate((got[2 * c], got[2 * c + 1]), axis=1)[:, :places] for c in range(2)]
        )
        return jnp.transpose(t, (2, 1, 0, 3))

    def time_to_space(own):
        got = [own[0]] + [permute_tp(own[e], e) for e in range(1, 4)]
        return jnp.stack(got, axis=1)

    def space_to_time(own):
        got = [own[:, 0]] + [permute_tp(own[:, e], e) for e in range(1, 4)]
        return jnp.stack(got)

    rows_n = 8 * block
    flat = (rows_n, d_model)
    space_shape = (2, 4, block, d_model)
    time_shape = (4, 2, block, d_model)

    def spread(shard):
        got = lax.ppermute(shard, ("ctx", "tp"), outward)
        first = jnp.where(is_source, shard, got)
        return first, permute_tp(first, 1)

    def attention_pack(qkv, proj):
        return jnp.concatenate((qkv.reshape(d_part, -1), proj.T), axis=1)

    def attention_weights(qkv, proj):
        first, second = spread(attention_pack(qkv, proj))
        if swap:
            return [first, permute_fsdp(first), second, permute_fsdp(second)]
        return [lax.all_gather(v, "fsdp", axis=0, tiled=True) for v in (first, second)]

    hid_half = up_weight.shape[1] // 2

    def feed_weights():
        up = lax.dynamic_slice_in_dim(up_weight, chip * hid_half, hid_half, axis=1)
        down = lax.dynamic_slice_in_dim(down_weight, chip * hid_half, hid_half, axis=0)
        first, second = spread(jnp.concatenate((up, down.reshape(d_part, hid_half)), axis=0))
        if swap:
            mine = [first, permute_fsdp(first), second, permute_fsdp(second)]
            return mine + [permute_ctx(v, 2) for v in mine]
        mine = [first, second]
        full = []
        for v in mine + [permute_ctx(v, 2) for v in mine]:
            every = lax.all_gather(v, "fsdp", axis=0)
            full.append(every[:, :d_part].reshape(d_model, hid_half))
            down_all = every[:, d_part:].reshape(n_fsdp, hid_half, d_part)
            full.append(jnp.transpose(down_all, (1, 0, 2)).reshape(hid_half, d_model))
        return full

    def owner_sum(both):
        mine = both[0] + permute_tp(both[1], 1)
        return mine + lax.ppermute(mine, ("ctx", "tp"), inward)

    def to_both(mine):
        other = permute_ctx(mine, 2)
        low = jnp.where(chip == 0, mine, other)
        high = jnp.where(chip == 0, other, mine)
        pair_low, pair_high = permute_ctx(low, 1), permute_ctx(high, 1)
        return jnp.where(is_source, low, pair_low), jnp.where(is_source, high, pair_high)

    def attention_grads(grads):
        if swap:
            total = grads[0] + permute_fsdp(grads[1])
        else:
            total = lax.psum_scatter(grads[0], "fsdp", scatter_dimension=1, tiled=True)
        half = total.shape[2] // 2
        keep = lax.dynamic_slice_in_dim(total, chip * half, half, axis=2)
        send = lax.dynamic_slice_in_dim(total, (1 - chip) * half, half, axis=2)
        low, high = to_both(owner_sum(keep + permute_ctx(send, 2)))
        full = jnp.concatenate((low, high), axis=1).astype(F32)
        inner = 3 * full.shape[1] // 4
        return full[:, :inner].reshape(d_part, 3, inner // 3), full[:, inner:].T

    def feed_grads(grads):
        n = len(grads) // 2
        here = [grads[k] + permute_ctx(grads[n + k], 2) for k in range(n)]
        if swap:
            total = here[0] + permute_fsdp(here[1])
        else:
            up = lax.psum_scatter(here[0], "fsdp", scatter_dimension=1, tiled=True)
            down = lax.psum_scatter(here[1], "fsdp", scatter_dimension=2, tiled=True)
            total = jnp.concatenate((up, down.reshape(2, d_part, hid_half)), axis=1)
        low, high = to_both(owner_sum(total))
        up = jnp.concatenate((low[:d_part], high[:d_part]), axis=1)
        down = jnp.concatenate(
            [v[d_part:].reshape(hid_half, d_part) for v in (low, high)], axis=0
        )
        return up.astype(F32), down.astype(F32)

    pieces = 2 if swap else 1
    width = d_model // pieces
    if swap:
        offsets = jnp.stack((x * width, (1 - x) * width)).astype(jnp.int32)
    else:
        offsets = jnp.zeros((1,), jnp.int32)

    weights_t = attention_weights(temporal_qkv, temporal_proj)
    start = to_time(tokens).reshape(flat)
    start_pair = permute_ctx(start, 1)
    weights_s = attention_weights(spatial_qkv, spatial_proj)
    weights_f = feed_weights()
    gains = lax.all_gather(norm_gains, "fsdp", axis=1, tiled=True).astype(F32)
    cot_own = time_to_space(to_time(cotangent)).reshape(flat)
    cot_pair = permute_ctx(cot_own, 1)

    at = jnp.arange(rows_n, dtype=jnp.int32)
    far = jnp.float32(-1e30)
    bias_t = jnp.where((at % block)[:, None] == (at % block)[None, :], 0.0, far).astype(F32)
    owner = jnp.where(at < rows_n // 2, core, 1 - core)
    real = owner * block + at % block < places
    bias_s = jnp.broadcast_to(jnp.where(real, 0.0, far).astype(F32)[None], (rows_n, rows_n))

    two = (2 * rows_n, d_model)
    joined = (2 * rows_n, 3 * temporal_qkv.shape[2])
    heads = (2 * rows_n, temporal_qkv.shape[2])
    unit = 2 * rows_n * d_model * d_model

    def attend_forward(own, pair, gain, bias, weights, cut, name):
        outs = [
            shape_of(two, LOW),
            shape_of(two, LOW),
            shape_of(joined, LOW),
            shape_of(joined, LOW),
            shape_of(heads, LOW),
            shape_of(heads, LOW),
        ]
        return run(
            functools.partial(attend_forward_kernel, pieces, cut),
            [offsets, own, pair, gain, bias, *weights],
            outs,
            [VMEM(two, F32)],
            6 * unit,
            name,
        )

    def attend_backward(saved, bias, head, weights, cut, name):
        group = (2, width, d_model)
        outs = [shape_of(two, LOW)] + [shape_of(group, LOW)] * pieces
        if cut:
            outs += [shape_of(flat, F32), shape_of((1, d_model), F32)]
        return run(
            functools.partial(attend_backward_kernel, pieces, cut),
            [offsets, bias, *saved, *head, *weights],
            outs,
            [
                VMEM(two, LOW),
                VMEM(joined, LOW),
                VMEM(joined, LOW),
                VMEM(heads, LOW),
                VMEM(heads, LOW),
                VMEM(two, F32),
            ],
            12 * unit,
            name,
        )

    def norm_backward(part, received, base, gain, carried, out_dtype, name):
        return run(
            norm_back_kernel,
            [part, received, base, gain, carried],
            [shape_of(flat, out_dtype), shape_of((1, d_model), F32)],
            [],
            20 * rows_n * d_model,
            name,
        )

    part_t, *saved_t = attend_forward(
        start, start_pair, gains[0:1], bias_t, weights_t, False, "time_forward"
    )
    back = permute_ctx(part_t[rows_n:], 1)
    after_time = (
        start.astype(F32) + part_t[:rows_n].astype(F32) + back.astype(F32)
    ).astype(LOW)
    own1 = time_to_space(after_time.reshape(time_shape)).reshape(flat)
    pair1 = permute_ctx(own1, 1)

    part_s, *saved_s = attend_forward(
        own1, pair1, gains[1:2], bias_s, weights_s, True, "space_forward"
    )
    got_s = permute_ctx(part_s, 1)
    got_s = jnp.concatenate((got_s[rows_n:], got_s[:rows_n]), axis=0)

    n_w = len(weights_f)
    if swap:
        outs_f = [shape_of((2, 2 * width, hid_half), LOW)] * 4
    else:
        outs_f = [shape_of((2, width, hid_half), LOW), shape_of((2, hid_half, width), LOW)] * 2
    if swap:
        ordered = weights_f
    else:
        ordered = weights_f
    out_part, dn3, *grads_f = run(
        functools.partial(feed_kernel, pieces, 4, swap),
        [offsets, own1, pair1, part_s, got_s, gains[2:3], cot_own, cot_pair, *ordered],
        [shape_of(two, LOW), shape_of(two, LOW), *outs_f],
        [VMEM(two, LOW), VMEM(two, LOW), VMEM(two, F32), VMEM(two, F32)],
        24 * unit,
        "feed",
    )
    del n_w
    got3 = permute_ctx(dn3, 1)
    got3 = jnp.concatenate((got3[rows_n:], got3[:rows_n]), axis=0)
    got_out = permute_ctx(out_part[rows_n:], 1)
    after_space = own1.astype(F32) + (
        part_s[:rows_n].astype(F32) + got_s[:rows_n].astype(F32)
    )
    block_own = (after_space + out_part[:rows_n].astype(F32) + got_out.astype(F32)).astype(LOW)
    block_out = from_time(space_to_time(block_own.reshape(space_shape)))

    dn2, *rest = attend_backward(
        saved_s,
        bias_s,
        [own1, pair1, part_s, got_s, dn3, got3, gains[2:3], cot_own, cot_pair, gains[1:2]],
        weights_s,
        True,
        "space_backward",
    )
    grads_s, (carried2, gain3) = rest[:pieces], rest[pieces:]
    got2 = permute_ctx(dn2[rows_n:], 1)
    carried1, gain2 = norm_backward(dn2, got2, own1, gains[1:2], carried2, LOW, "space_norm")
    own_t = space_to_time(carried1.reshape(space_shape)).reshape(flat)
    pair_t = permute_ctx(own_t, 1)

    dn1, *grads_t = attend_backward(
        saved_t, bias_t, [own_t, pair_t], weights_t, False, "time_backward"
    )
    got1 = permute_ctx(dn1[rows_n:], 1)
    carried0, gain1 = norm_backward(dn1, got1, start, gains[0:1], own_t, LOW, "time_norm")
    tokens_grad = from_time(carried0.reshape(time_shape)).astype(F32)

    gain_all = jnp.concatenate((gain1, gain2, gain3), axis=0)
    for bits in (1, 2):
        gain_all = gain_all + permute_ctx(gain_all, bits)
    for bits in (1, 2):
        gain_all = gain_all + permute_tp(gain_all, bits)
    gain_grads = lax.psum_scatter(gain_all, "fsdp", scatter_dimension=1, tiled=True)
    up_grad, down_grad = feed_grads(grads_f)
    s_qkv, s_proj = attention_grads(grads_s)
    t_qkv, t_proj = attention_grads(grads_t)
    return (
        block_out,
        tokens_grad,
        gain_grads,
        t_qkv,
        t_proj,
        s_qkv,
        s_proj,
        up_grad,
        down_grad,
    )


def solution(mesh):
    rows = P("tp", "ctx", "fsdp", None)
    weights = (
        P(None, "fsdp"),
        P("fsdp", None, "tp"),
        P("tp", "fsdp"),
        P("fsdp", None, "tp"),
        P("tp", "fsdp"),
        P("fsdp", "tp"),
        P("tp", "fsdp"),
    )
    sizes = (mesh.shape["fsdp"], mesh.shape["ctx"], mesh.shape["tp"])
    return jax.shard_map(
        functools.partial(body, sizes),
        mesh=mesh,
        in_specs=(rows, *weights, rows),
        out_specs=(rows, rows, *weights),
        check_vma=False,
    )
```

time: 959 us -> 461 us (0.48)
  waiting for transfers between devices: 665 us -> 201 us
  starting transfers between devices: 2.61 us -> 108 us
  matrix products: 65.4 us -> 0 us
  Pallas kernels: 0 us -> 57.5 us
  blocking collectives: 55.5 us -> 3.19 us
  other arithmetic: 69.8 us -> 30.1 us
  local copies, waits for them, and re-layouts: 71.4 us -> 36.4 us
    unnamed x36 -> x2, waiting for transfers between devices: 381 us -> 14.2 us
    all_gather x10 -> x0, waiting for transfers between devices: 190 us -> none  [the longest x3 91.6 us: gather_grads(): return lax.all_gather(values, 'tp', axis=0, tiled=True)]
    ppermute x0 -> x76, waiting for transfers between devices: none -> 187 us  [the longest x41 70 us: permute_ctx(): return lax.ppermute(v, 'ctx', [(a, a ^ bits) for a in range(n_ctx)])]
    ppermute x0 -> x76, starting transfers between devices: none -> 108 us  [the longest x41 53.5 us: permute_ctx(): return lax.ppermute(v, 'ctx', [(a, a ^ bits) for a in range(n_ctx)])]
    dot_general x30 -> x0, matrix products: 65.4 us -> none  [the longest x6 8.74 us: row_partial(): jnp.einsum(pattern, operand, weight_part, preferred_element_type=jnp.floa...]
    reduce_scatter x3 -> x0, waiting for transfers between devices: 58.5 us -> none  [the longest x1 30.9 us: temporal_backward(): lax.psum_scatter(key_terms.astype(jnp.bfloat16), 'ctx', scatter_dimension...]
    pallas_call x0 -> x7, Pallas kernels: none -> 57.5 us  [run(): pl.pallas_call(kernel, out_shape=outs, in_specs=specs, out_specs=in_vmem(...]
    psum x1 -> x0, waiting for transfers between devices: 35.3 us -> none  [body(): lax.psum(weight_grads[1].astype(jnp.bfloat16), 'ctx').astype(jnp.float32)]
  transfers between devices with their start and end apart: 25 -> 77, of which waited for: 24 -> 28; matrix products, arithmetic and copies ran while one was open for 10% -> 12% of each run, Pallas kernels for 0% -> 9%
where the time goes in v1:
time: 461 us; the launch traced here: 452 us
  waiting for transfers between devices  201 us (44%)
  starting transfers between devices  108 us (23%)
  Pallas kernels  57.5 us (12%)
  local copies, waits for them, and re-layouts  36.4 us (8%)
  other arithmetic  30.1 us (7%)
  between operations  15.5 us (3%)
    ppermute x41, waiting for transfers between devices, permute_ctx(): return lax.ppermute(v, 'ctx', [(a, a ^ bits) for a in range(n_ctx)])  70 us
    ppermute x20, waiting for transfers between devices, permute_tp(): return lax.ppermute(v, 'tp', [(a, a ^ bits) for a in range(n_tp)])  62.1 us
    pallas_call x7, Pallas kernels, run(): pl.pallas_call(kernel, out_shape=outs, in_specs=specs, out_specs=in_vmem(...  57.5 us
    ppermute x41, starting transfers between devices, permute_ctx(): return lax.ppermute(v, 'ctx', [(a, a ^ bits) for a in range(n_ctx)])  53.5 us
    ppermute x9, waiting for transfers between devices, permute_fsdp(): return lax.ppermute(v, 'fsdp', [(0, 1), (1, 0)])  34.2 us
    ppermute x20, starting transfers between devices, permute_tp(): return lax.ppermute(v, 'tp', [(a, a ^ bits) for a in range(n_tp)])  31.6 us
    unnamed x112, local copies, waits for them, and re-layouts  17.3 us
    unnamed x2, waiting for transfers between devices  14.2 us
  transfers between devices with their start and end apart: 77, of which 28 were waited for; matrix products, arithmetic and copies ran while one was open for 12% of the time, Pallas kernels for 9%

profile of v1, /device:TPU:1, one launch (start us, length us, event | category | flops | bytes accessed | tf_op | source)
XLA Modules:
  0.0 452.4 jit_solution(14655690863323443950)
XLA Ops:
  12.0 5.9 %collective-permute-start = (bf16[2,26,768]{2,1,0:T(8,128)(2,1)}, bf16[2,26,768]{2,1,0:T(8,128)(2,1)}, u32[]{:S(2)}, u32[]{:S(2)}) collective-permute-start(bf16[2,26,768]{2,1,0:T(8,128)(2,1)} %get-tuple-element.149), channel_id=1, source_target_pairs={{0,12},{4,8},{8,4},{12,0},{1,13},{5,9},{9,5},{13,1},{2,14},{6,10},... | collective-permute-start | bytes 239624 | tf_op jit(solution)/shard_map/ppermute | solution.py:291
  21.0 3.2 all_gather.3
  24.2 9.9 %collective-permute-done.4 = bf16[384,768]{1,0:T(8,128)(2,1)S(1)} collective-permute-done((bf16[384,768]{1,0:T(8,128)(2,1)S(1)}, bf16[384,768]{1,0:T(8,128)(2,1)S(1)}, u32[]{:S(2)}, u32[]{:S(2)}) %collective-permute-start.4) | collective-permute-done | bytes 589856 | tf_op jit(solution)/shard_map/ppermute | solution.py:343
  39.8 19.8 %collective-permute-done.6.refs_7_.refs_11_ = bf16[384,768]{1,0:T(8,128)(2,1)S(1)} collective-permute-done((bf16[384,768]{1,0:T(8,128)(2,1)S(1)}, bf16[384,768]{1,0:T(8,128)(2,1)S(1)}, u32[]{:S(2)}, u32[]{:S(2)}) %collective-permute-start.6) | collective-permute-done | bytes 589856 | tf_op jit(solution)/shard_map/ppermute | solution.py:294
  64.7 10.0 %collective-permute-done.7.refs_8_.refs_12_ = bf16[384,768]{1,0:T(8,128)(2,1)S(1)} collective-permute-done((bf16[384,768]{1,0:T(8,128)(2,1)S(1)}, bf16[384,768]{1,0:T(8,128)(2,1)S(1)}, u32[]{:S(2)}, u32[]{:S(2)}) %collective-permute-start.7) | collective-permute-done | bytes 589856 | tf_op jit(solution)/shard_map/ppermute | solution.py:297
  74.7 5.8 %time_forward.1 = (bf16[416,768]{1,0:T(8,128)(2,1)S(1)}, bf16[416,768]{1,0:T(8,128)(2,1)S(1)}, bf16[416,576]{1,0:T(8,128)(2,1)S(1)}, bf16[416,576]{1,0:T(8,128)(...) custom-call(s32[2]{0:T(128)S(1)} %pad_add_fusion.refs_0_, ...), custom_call_target="tpu_custom_call" | custom-call | flops 1472200704 | bytes 5730312 | tf_op jit(solution)/shard_map/time_forward/pallas_call | solution.py:267
  89.9 9.2 %collective-permute-done.15.refs_7_.refs_19_ = bf16[384,768]{1,0:T(8,128)(2,1)S(1)} collective-permute-done((bf16[384,768]{1,0:T(8,128)(2,1)S(1)}, bf16[384,768]{1,0:T(8,128)(2,1)S(1)}, u32[]{:S(2)}, u32[]{:S(2)}) %collective-permute-start.15) | collective-permute-done | bytes 589856 | tf_op jit(solution)/shard_map/ppermute | solution.py:294
  103.0 13.0 %collective-permute-done.9 = bf16[2,26,768]{2,1,0:T(8,128)(2,1)S(1)} collective-permute-done((bf16[2,26,768]{2,1,0:T(8,128)(2,1)S(1)}, bf16[2,26,768]{2,1,0:T(8,128)(2,1)S(1)}, u32[]{:S(2)}, u32[]{:S(2)}) %collective-permute-start.9) | collective-permute-done | bytes 79904 | tf_op jit(solution)/shard_map/ppermute | solution.py:294
  119.1 2.9 collective-permute-done.11
  131.8 7.8 %space_forward.1 = (bf16[416,768]{1,0:T(8,128)(2,1)}, bf16[416,768]{1,0:T(8,128)(2,1)S(1)}, bf16[416,576]{1,0:T(8,128)(2,1)S(1)}, bf16[416,576]{1,0:T(8,128)(2,1...) custom-call(s32[2]{0:T(128)S(1)} %pad_add_fusion.refs_0_, ...), custom_call_target="tpu_custom_call" | custom-call | flops 1472200704 | bytes 5730312 | tf_op jit(solution)/shard_map/space_forward/pallas_call | solution.py:267
  140.9 3.5 collective-permute-start.22
  144.9 4.5 %collective-permute-start.23 = (bf16[2,26,768]{2,1,0:T(8,128)(2,1)S(1)}, bf16[2,26,768]{2,1,0:T(8,128)(2,1)S(1)}, u32[]{:S(2)}, u32[]{:S(2)}) collective-permute-start(bf16[2,26,768]{2,1,0:T(8,128)(2,1)S(1)} %get-tuple-element.124), channel_id=1, source_target_pairs={{0,3},{1,2},{2,1},{3,0},{4,7},{5,6},{6,5},{7,4},{8,11},{9,10},{10,... | collective-permute-start | bytes 239624 | tf_op jit(solution)/shard_map/ppermute | solution.py:294
  163.2 25.3 %collective-permute-done.30.refs_13_ = bf16[768,384]{1,0:T(8,128)(2,1)} collective-permute-done((bf16[768,384]{1,0:T(8,128)(2,1)}, bf16[768,384]{1,0:T(8,128)(2,1)}, u32[]{:S(2)}, u32[]{:S(2)}) %collective-permute-start.30) | collective-permute-done | bytes 589856 | tf_op jit(solution)/shard_map/ppermute | solution.py:291
  188.5 12.6 %collective-permute-done.32.refs_15_ = bf16[768,384]{1,0:T(8,128)(2,1)} collective-permute-done((bf16[768,384]{1,0:T(8,128)(2,1)}, bf16[768,384]{1,0:T(8,128)(2,1)}, u32[]{:S(2)}, u32[]{:S(2)}) %collective-permute-start.32) | collective-permute-done | bytes 589856 | tf_op jit(solution)/shard_map/ppermute | solution.py:291
  201.1 15.0 %feed.1 = (bf16[416,768]{1,0:T(8,128)(2,1)}, bf16[416,768]{1,0:T(8,128)(2,1)}, bf16[2,768,384]{2,1,0:T(8,128)(2,1)}, bf16[2,768,384]{2,1,0:T(8,128)(2,1)}, bf16[...) custom-call(s32[2]{0:T(128)S(1)} %pad_add_fusion.refs_0_, bf16[208,768]{1,0:T(8,128)(2,1)S(1)} %reshape.144.refs_1_.refs_7_.base, ...), custom_call_target="tpu_custom_call" | custom-call | flops 5888802816 | bytes 13274120 | tf_op jit(solution)/shard_map/feed/pallas_call | solution.py:267
  221.2 15.0 %space_backward.1 = (bf16[416,768]{1,0:T(8,128)(2,1)S(1)}, bf16[2,384,768]{2,1,0:T(8,128)(2,1)}, bf16[2,384,768]{2,1,0:T(8,128)(2,1)}, f32[208,768]{1,0:T(8,128)}, f32[1,768]{1,0:T(1,128)S(1)}) custom-call(s32[2]{0:T(128)S(1)} %pad_add_fusion.refs_0_, f32[208,208]{1,0:T(8,128)S(1)} %broadcast_in_dim.38.refs_4_.refs_1_, bf16[416,768]{1,0:T(8,128)(2,1)} %copy-done.14, ...), custom_call_target="tpu_custom_call" | custom-call | flops 2944401408 | bytes 11929608 | tf_op jit(solution)/shard_map/space_backward/pallas_call | solution.py:267
  254.8 3.1 collective-permute-done.35
  258.7 3.2 collective-permute-start.37
  268.5 12.7 %time_backward.1 = (bf16[416,768]{1,0:T(8,128)(2,1)S(1)}, bf16[2,384,768]{2,1,0:T(8,128)(2,1)}, bf16[2,384,768]{2,1,0:T(8,128)(2,1)}) custom-call(s32[2]{0:T(128)S(1)} %pad_add_fusion.refs_0_, f32[208,208]{1,0:T(8,128)S(1)} %compare_select_fusion.refs_4_.refs_1_, bf16[416,768]{1,0:T(8,128)(2,1)S(1)} %copy-done.13, bf16[416,576]{1,0:T(8,128)(2,1)S(1)} %copy-done.16, ...), custom_call_target="tpu_custom_call" | custom-call | flops 2944401408 | bytes 8086536 | tf_op jit(solution)/shard_map/time_backward/pallas_call | solution.py:267
  292.2 2.7 add.147
  295.1 17.4 %collective-permute-done.51 = f32[3,768]{1,0:T(4,128)S(1)} collective-permute-done((f32[3,768]{1,0:T(4,128)S(1)}, f32[3,768]{1,0:T(4,128)S(1)}, u32[]{:S(2)}, u32[]{:S(2)}) %collective-permute-start.51) | collective-permute-done | bytes 9248 | tf_op jit(solution)/shard_map/ppermute | solution.py:291
  312.5 6.7 %collective-permute-start.52 = (f32[3,768]{1,0:T(4,128)S(1)}, f32[3,768]{1,0:T(4,128)S(1)}, u32[]{:S(2)}, u32[]{:S(2)}) collective-permute-start(f32[3,768]{1,0:T(4,128)S(1)} %fusion.16), channel_id=1, source_target_pairs={{0,1},{1,0},{2,3},{3,2},{4,5},{5,4},{6,7},{7,6},{8,9},{9,8},{10,11... | collective-permute-start | bytes 27656 | tf_op jit(solution)/shard_map/ppermute | solution.py:294
  330.1 14.2 %reduce-scatter.4.cloned.1.call-done = f32[384,3]{1,0:T(8,128)} async-done(((f32[768,3]{1,0:T(8,128)}), f32[384,3]{1,0:T(8,128)}) %reduce-scatter.4.cloned.1.call-update) | async-done | bytes 4624
  351.3 21.9 %collective-permute-done.54 = bf16[2,384,768]{2,1,0:T(8,128)(2,1)S(1)} collective-permute-done((bf16[2,384,768]{2,1,0:T(8,128)(2,1)}, bf16[2,384,768]{2,1,0:T(8,128)(2,1)S(1)}, u32[]{:S(2)}, u32[]{:S(2)}) %collective-permute-start.54) | collective-permute-done | bytes 1179680 | tf_op jit(solution)/shard_map/ppermute | solution.py:297
  374.8 5.6 %collective-permute-start.64 = (bf16[384,384]{1,0:T(8,128)(2,1)S(1)}, bf16[384,384]{1,0:T(8,128)(2,1)S(1)}, u32[]{:S(2)}, u32[]{:S(2)}) collective-permute-start(bf16[384,384]{1,0:T(8,128)(2,1)S(1)} %fusion.1), channel_id=1, source_target_pairs={{2,0},{3,1},{4,6},{5,7},{10,8},{11,9},{12,14},{13,15},{18,16},{19,... | collective-permute-start | bytes 884744 | tf_op jit(solution)/shard_map/ppermute | solution.py:376
  380.7 6.0 %collective-permute-done.64 = bf16[384,384]{1,0:T(8,128)(2,1)S(1)} collective-permute-done((bf16[384,384]{1,0:T(8,128)(2,1)S(1)}, bf16[384,384]{1,0:T(8,128)(2,1)S(1)}, u32[]{:S(2)}, u32[]{:S(2)}) %collective-permute-start.64) | collective-permute-done | bytes 294944 | tf_op jit(solution)/shard_map/ppermute | solution.py:376
  387.4 2.7 collective-permute-start.56
  390.1 8.7 %collective-permute-done.71 = bf16[768,384]{1,0:T(8,128)(2,1)S(1)} collective-permute-done((bf16[768,384]{1,0:T(8,128)(2,1)S(1)}, bf16[768,384]{1,0:T(8,128)(2,1)S(1)}, u32[]{:S(2)}, u32[]{:S(2)}) %collective-permute-start.71) | collective-permute-done | bytes 589856 | tf_op jit(solution)/shard_map/ppermute | solution.py:294
  400.8 3.0 collective-permute-done.56
  410.0 2.6 collective-permute-done.57
  413.1 8.7 %collective-permute-done.58 = bf16[384,384]{1,0:T(8,128)(2,1)S(1)} collective-permute-done((bf16[384,384]{1,0:T(8,128)(2,1)S(1)}, bf16[384,384]{1,0:T(8,128)(2,1)S(1)}, u32[]{:S(2)}, u32[]{:S(2)}) %collective-permute-start.58) | collective-permute-done | bytes 294944 | tf_op jit(solution)/shard_map/ppermute | solution.py:291
  421.9 12.2 %collective-permute-start.59 = (bf16[384,384]{1,0:T(8,128)(2,1)S(1)}, bf16[384,384]{1,0:T(8,128)(2,1)}, u32[]{:S(2)}, u32[]{:S(2)}) collective-permute-start(bf16[384,384]{1,0:T(8,128)(2,1)S(1)} %get-tuple-element.119), channel_id=1, source_target_pairs={{0,4},{4,0},{8,12},{12,8},{1,5},{5,1},{9,13},{13,9},{2,6},{6,2},{1... | collective-permute-start | bytes 884744 | tf_op jit(solution)/shard_map/ppermute | solution.py:291
  (349 shorter events, 142.0 us)
Async XLA Ops:
  7.2 337.1 %reduce-scatter.4.cloned.1.call-start = ((), (), s32[]{:S(2)}) async-start(), calls=%async_computation.1 | async-start | bytes 589824
  9.7 24.3 %collective-permute-start.4 = (bf16[384,768]{1,0:T(8,128)(2,1)S(1)}, bf16[384,768]{1,0:T(8,128)(2,1)S(1)}, u32[]{:S(2)}, u32[]{:S(2)}) collective-permute-start(bf16[384,768]{1,0:T(8,128)(2,1)S(1)} %pad_maximum_fusion.2), channel_id=1, source_target_pairs={{0,2},{1,3},{6,4},{7,5},{8,10},{9,11},{14,12},{15,13},{16,18},{17,... | collective-permute-start | bytes 1769480 | tf_op jit(solution)/shard_map/ppermute | solution.py:343
  12.0 24.6 %collective-permute-start = (bf16[2,26,768]{2,1,0:T(8,128)(2,1)}, bf16[2,26,768]{2,1,0:T(8,128)(2,1)}, u32[]{:S(2)}, u32[]{:S(2)}) collective-permute-start(bf16[2,26,768]{2,1,0:T(8,128)(2,1)} %get-tuple-element.149), channel_id=1, source_target_pairs={{0,12},{4,8},{8,4},{12,0},{1,13},{5,9},{9,5},{13,1},{2,14},{6,10},... | collective-permute-start | bytes 239624 | tf_op jit(solution)/shard_map/ppermute | solution.py:291
  17.8 20.0 %collective-permute-start.1 = (bf16[2,26,768]{2,1,0:T(8,128)(2,1)}, bf16[2,26,768]{2,1,0:T(8,128)(2,1)}, u32[]{:S(2)}, u32[]{:S(2)}) collective-permute-start(bf16[2,26,768]{2,1,0:T(8,128)(2,1)} %get-tuple-element.101), channel_id=1, source_target_pairs={{0,8},{4,12},{8,0},{12,4},{1,9},{5,13},{9,1},{13,5},{2,10},{6,14},... | collective-permute-start | bytes 239624 | tf_op jit(solution)/shard_map/ppermute | solution.py:291
  18.1 43.4 %collective-permute-start.2 = (bf16[2,26,768]{2,1,0:T(8,128)(2,1)}, bf16[2,26,768]{2,1,0:T(8,128)(2,1)}, u32[]{:S(2)}, u32[]{:S(2)}) collective-permute-start(bf16[2,26,768]{2,1,0:T(8,128)(2,1)} %get-tuple-element.148), channel_id=1, source_target_pairs={{0,4},{4,0},{8,12},{12,8},{1,5},{5,1},{9,13},{13,9},{2,6},{6,2},{1... | collective-permute-start | bytes 239624 | tf_op jit(solution)/shard_map/ppermute | solution.py:291
  19.6 62.8 %collective-permute-start.13 = (bf16[384,768]{1,0:T(8,128)(2,1)}, bf16[384,768]{1,0:T(8,128)(2,1)}, u32[]{:S(2)}, u32[]{:S(2)}) collective-permute-start(bf16[384,768]{1,0:T(8,128)(2,1)} %pad_maximum_fusion.3), channel_id=1, source_target_pairs={{0,2},{1,3},{6,4},{7,5},{8,10},{9,11},{14,12},{15,13},{16,18},{17,... | collective-permute-start | bytes 1769480 | tf_op jit(solution)/shard_map/ppermute | solution.py:343
  34.3 25.2 %collective-permute-start.6 = (bf16[384,768]{1,0:T(8,128)(2,1)S(1)}, bf16[384,768]{1,0:T(8,128)(2,1)S(1)}, u32[]{:S(2)}, u32[]{:S(2)}) collective-permute-start(bf16[384,768]{1,0:T(8,128)(2,1)S(1)} %broadcast_select_fusion.6.refs_5_.refs_9_), channel_id=1, source_target_pairs={{0,1},{1,0},{2,3},{3,2},{4,5},{5,4},{6,7},{7,6},{8,9},{9,8},{10,11... | collective-permute-start | bytes 1769480 | tf_op jit(solution)/shard_map/ppermute | solution.py:294
  36.5 47.3 %collective-permute-start.25 = (bf16[768,384]{1,0:T(8,128)(2,1)}, bf16[768,384]{1,0:T(8,128)(2,1)}, u32[]{:S(2)}, u32[]{:S(2)}) collective-permute-start(bf16[768,384]{1,0:T(8,128)(2,1)} %pad_maximum_fusion.4), channel_id=1, source_target_pairs={{0,2},{1,3},{6,4},{7,5},{8,10},{9,11},{14,12},{15,13},{16,18},{17,... | collective-permute-start | bytes 1769480 | tf_op jit(solution)/shard_map/ppermute | solution.py:343
  37.8 26.9 %collective-permute-start.5 = (bf16[384,768]{1,0:T(8,128)(2,1)S(1)}, bf16[384,768]{1,0:T(8,128)(2,1)S(1)}, u32[]{:S(2)}, u32[]{:S(2)}) collective-permute-start(bf16[384,768]{1,0:T(8,128)(2,1)S(1)} %broadcast_select_fusion.6.refs_5_.refs_9_), channel_id=1, source_target_pairs={{0,16},{16,0},{1,17},{17,1},{2,18},{18,2},{3,19},{19,3},{4,20},{20... | collective-permute-start | bytes 1769480 | tf_op jit(solution)/shard_map/ppermute | solution.py:297
  85.1 44.1 %collective-permute-start.27 = (bf16[768,384]{1,0:T(8,128)(2,1)S(1)}, bf16[768,384]{1,0:T(8,128)(2,1)}, u32[]{:S(2)}, u32[]{:S(2)}) collective-permute-start(bf16[768,384]{1,0:T(8,128)(2,1)S(1)} %broadcast_select_fusion.4.refs_8_), channel_id=1, source_target_pairs={{0,1},{1,0},{2,3},{3,2},{4,5},{5,4},{6,7},{7,6},{8,9},{9,8},{10,11... | collective-permute-start | bytes 1769480 | tf_op jit(solution)/shard_map/ppermute | solution.py:294
  88.3 27.6 %collective-permute-start.9 = (bf16[2,26,768]{2,1,0:T(8,128)(2,1)S(1)}, bf16[2,26,768]{2,1,0:T(8,128)(2,1)S(1)}, u32[]{:S(2)}, u32[]{:S(2)}) collective-permute-start(bf16[2,26,768]{2,1,0:T(8,128)(2,1)S(1)} %squeeze.57), channel_id=1, source_target_pairs={{0,1},{1,0},{2,3},{3,2},{4,5},{5,4},{6,7},{7,6},{8,9},{9,8},{10,11... | collective-permute-start | bytes 239624 | tf_op jit(solution)/shard_map/ppermute | solution.py:294
  88.4 40.8 %collective-permute-start.14 = (bf16[384,768]{1,0:T(8,128)(2,1)S(1)}, bf16[384,768]{1,0:T(8,128)(2,1)}, u32[]{:S(2)}, u32[]{:S(2)}) collective-permute-start(bf16[384,768]{1,0:T(8,128)(2,1)S(1)} %broadcast_select_fusion.5.refs_5_.refs_17_), channel_id=1, source_target_pairs={{0,16},{16,0},{1,17},{17,1},{2,18},{18,2},{3,19},{19,3},{4,20},{20... | collective-permute-start | bytes 1769480 | tf_op jit(solution)/shard_map/ppermute | solution.py:297
  99.1 32.2 %collective-permute-start.16 = (bf16[384,768]{1,0:T(8,128)(2,1)S(1)}, bf16[384,768]{1,0:T(8,128)(2,1)}, u32[]{:S(2)}, u32[]{:S(2)}) collective-permute-start(bf16[384,768]{1,0:T(8,128)(2,1)S(1)} %collective-permute-done.15.refs_7_.refs_19_), channel_id=1, source_target_pairs={{0,16},{16,0},{1,17},{17,1},{2,18},{18,2},{3,19},{19,3},{4,20},{20... | collective-permute-start | bytes 1769480 | tf_op jit(solution)/shard_map/ppermute | solution.py:297
  127.7 25.3 %collective-permute-start.26 = (bf16[768,384]{1,0:T(8,128)(2,1)S(1)}, bf16[768,384]{1,0:T(8,128)(2,1)}, u32[]{:S(2)}, u32[]{:S(2)}) collective-permute-start(bf16[768,384]{1,0:T(8,128)(2,1)S(1)} %broadcast_select_fusion.4.refs_8_), channel_id=1, source_target_pairs={{0,16},{16,0},{1,17},{17,1},{2,18},{18,2},{3,19},{19,3},{4,20},{20... | collective-permute-start | bytes 1769480 | tf_op jit(solution)/shard_map/ppermute | solution.py:297
  129.2 26.2 %collective-permute-start.28 = (bf16[768,384]{1,0:T(8,128)(2,1)}, bf16[768,384]{1,0:T(8,128)(2,1)}, u32[]{:S(2)}, u32[]{:S(2)}) collective-permute-start(bf16[768,384]{1,0:T(8,128)(2,1)} %collective-permute-done.27.refs_10_), channel_id=1, source_target_pairs={{0,16},{16,0},{1,17},{17,1},{2,18},{18,2},{3,19},{19,3},{4,20},{20... | collective-permute-start | bytes 1769480 | tf_op jit(solution)/shard_map/ppermute | solution.py:297
  151.6 36.9 %collective-permute-start.31 = (bf16[768,384]{1,0:T(8,128)(2,1)}, bf16[768,384]{1,0:T(8,128)(2,1)}, u32[]{:S(2)}, u32[]{:S(2)}) collective-permute-start(bf16[768,384]{1,0:T(8,128)(2,1)} %collective-permute-done.27.refs_10_), channel_id=1, source_target_pairs={{0,8},{4,12},{8,0},{12,4},{1,9},{5,13},{9,1},{13,5},{2,10},{6,14},... | collective-permute-start | bytes 1769480 | tf_op jit(solution)/shard_map/ppermute | solution.py:291
  152.9 35.5 %collective-permute-start.30 = (bf16[768,384]{1,0:T(8,128)(2,1)}, bf16[768,384]{1,0:T(8,128)(2,1)}, u32[]{:S(2)}, u32[]{:S(2)}) collective-permute-start(bf16[768,384]{1,0:T(8,128)(2,1)} %collective-permute-done.26.refs_9_), channel_id=1, source_target_pairs={{0,8},{4,12},{8,0},{12,4},{1,9},{5,13},{9,1},{13,5},{2,10},{6,14},... | collective-permute-start | bytes 1769480 | tf_op jit(solution)/shard_map/ppermute | solution.py:291
  155.4 45.7 %collective-permute-start.32 = (bf16[768,384]{1,0:T(8,128)(2,1)}, bf16[768,384]{1,0:T(8,128)(2,1)}, u32[]{:S(2)}, u32[]{:S(2)}) collective-permute-start(bf16[768,384]{1,0:T(8,128)(2,1)} %collective-permute-done.28.refs_11_), channel_id=1, source_target_pairs={{0,8},{4,12},{8,0},{12,4},{1,9},{5,13},{9,1},{13,5},{2,10},{6,14},... | collective-permute-start | bytes 1769480 | tf_op jit(solution)/shard_map/ppermute | solution.py:291
  253.6 38.6 %collective-permute-start.69 = (bf16[2,768,384]{2,1,0:T(8,128)(2,1)}, bf16[2,768,384]{2,1,0:T(8,128)(2,1)}, u32[]{:S(2)}, u32[]{:S(2)}) collective-permute-start(bf16[2,768,384]{2,1,0:T(8,128)(2,1)} %get-tuple-element.68), channel_id=1, source_target_pairs={{0,8},{4,12},{8,0},{12,4},{1,9},{5,13},{9,1},{13,5},{2,10},{6,14},... | collective-permute-start | bytes 3538952 | tf_op jit(solution)/shard_map/ppermute | solution.py:291
  258.7 25.4 %collective-permute-start.37 = (bf16[2,26,768]{2,1,0:T(8,128)(2,1)}, bf16[2,26,768]{2,1,0:T(8,128)(2,1)}, u32[]{:S(2)}, u32[]{:S(2)}) collective-permute-start(bf16[2,26,768]{2,1,0:T(8,128)(2,1)} %get-tuple-element.107), channel_id=1, source_target_pairs={{0,12},{4,8},{8,4},{12,0},{1,13},{5,9},{9,5},{13,1},{2,14},{6,10},... | collective-permute-start | bytes 239624 | tf_op jit(solution)/shard_map/ppermute | solution.py:291
  261.9 23.8 %collective-permute-start.38 = (bf16[2,26,768]{2,1,0:T(8,128)(2,1)}, bf16[2,26,768]{2,1,0:T(8,128)(2,1)}, u32[]{:S(2)}, u32[]{:S(2)}) collective-permute-start(bf16[2,26,768]{2,1,0:T(8,128)(2,1)} %get-tuple-element.108), channel_id=1, source_target_pairs={{0,8},{4,12},{8,0},{12,4},{1,9},{5,13},{9,1},{13,5},{2,10},{6,14},... | collective-permute-start | bytes 239624 | tf_op jit(solution)/shard_map/ppermute | solution.py:291
  262.2 24.7 %collective-permute-start.39 = (bf16[2,26,768]{2,1,0:T(8,128)(2,1)}, bf16[2,26,768]{2,1,0:T(8,128)(2,1)}, u32[]{:S(2)}, u32[]{:S(2)}) collective-permute-start(bf16[2,26,768]{2,1,0:T(8,128)(2,1)} %get-tuple-element.106), channel_id=1, source_target_pairs={{0,4},{4,0},{8,12},{12,8},{1,5},{5,1},{9,13},{13,9},{2,6},{6,2},{1... | collective-permute-start | bytes 239624 | tf_op jit(solution)/shard_map/ppermute | solution.py:291
  284.2 65.1 %collective-permute-start.68 = (bf16[2,768,384]{2,1,0:T(8,128)(2,1)}, bf16[2,768,384]{2,1,0:T(8,128)(2,1)}, u32[]{:S(2)}, u32[]{:S(2)}) collective-permute-start(bf16[2,768,384]{2,1,0:T(8,128)(2,1)} %get-tuple-element.66), channel_id=1, source_target_pairs={{0,8},{4,12},{8,0},{12,4},{1,9},{5,13},{9,1},{13,5},{2,10},{6,14},... | collective-permute-start | bytes 3538952 | tf_op jit(solution)/shard_map/ppermute | solution.py:291
  285.7 36.8 %collective-permute-start.61 = (bf16[2,384,768]{2,1,0:T(8,128)(2,1)}, bf16[2,384,768]{2,1,0:T(8,128)(2,1)}, u32[]{:S(2)}, u32[]{:S(2)}) collective-permute-start(bf16[2,384,768]{2,1,0:T(8,128)(2,1)} %get-tuple-element.64), channel_id=1, source_target_pairs={{0,16},{16,0},{1,17},{17,1},{2,18},{18,2},{3,19},{19,3},{4,20},{20... | collective-permute-start | bytes 3538952 | tf_op jit(solution)/shard_map/ppermute | solution.py:297
  290.8 21.7 %collective-permute-start.51 = (f32[3,768]{1,0:T(4,128)S(1)}, f32[3,768]{1,0:T(4,128)S(1)}, u32[]{:S(2)}, u32[]{:S(2)}) collective-permute-start(f32[3,768]{1,0:T(4,128)S(1)} %fusion.9), channel_id=1, source_target_pairs={{0,8},{4,12},{8,0},{12,4},{1,9},{5,13},{9,1},{13,5},{2,10},{6,14},... | collective-permute-start | bytes 27656 | tf_op jit(solution)/shard_map/ppermute | solution.py:291
  294.9 54.4 %collective-permute-start.70 = (bf16[2,768,384]{2,1,0:T(8,128)(2,1)}, bf16[2,768,384]{2,1,0:T(8,128)(2,1)}, u32[]{:S(2)}, u32[]{:S(2)}) collective-permute-start(bf16[2,768,384]{2,1,0:T(8,128)(2,1)} %add.147), channel_id=1, source_target_pairs={{0,16},{16,0},{1,17},{17,1},{2,18},{18,2},{3,19},{19,3},{4,20},{20... | collective-permute-start | bytes 3538952 | tf_op jit(solution)/shard_map/ppermute | solution.py:297
  324.1 22.6 %collective-permute-start.62 = (bf16[2,384,384]{2,1,0:T(8,128)(2,1)S(1)}, bf16[2,384,384]{2,1,0:T(8,128)(2,1)S(1)}, u32[]{:S(2)}, u32[]{:S(2)}) collective-permute-start(bf16[2,384,384]{2,1,0:T(8,128)(2,1)S(1)} %constant_dynamic-slice_fusion), channel_id=1, source_target_pairs={{0,8},{4,12},{8,0},{12,4},{1,9},{5,13},{9,1},{13,5},{2,10},{6,14},... | collective-permute-start | bytes 1769480 | tf_op jit(solution)/shard_map/ppermute | solution.py:291
  325.7 20.2 %collective-permute-start.48 = (bf16[2,26,768]{2,1,0:T(8,128)(2,1)S(1)}, bf16[2,26,768]{2,1,0:T(8,128)(2,1)S(1)}, u32[]{:S(2)}, u32[]{:S(2)}) collective-permute-start(bf16[2,26,768]{2,1,0:T(8,128)(2,1)S(1)} %select_n.553), channel_id=1, source_target_pairs={{0,8},{4,12},{8,0},{12,4},{1,9},{5,13},{9,1},{13,5},{2,10},{6,14},... | collective-permute-start | bytes 239624 | tf_op jit(solution)/shard_map/ppermute | solution.py:291
  326.8 19.8 %collective-permute-start.49 = (bf16[2,26,768]{2,1,0:T(8,128)(2,1)S(1)}, bf16[2,26,768]{2,1,0:T(8,128)(2,1)S(1)}, u32[]{:S(2)}, u32[]{:S(2)}) collective-permute-start(bf16[2,26,768]{2,1,0:T(8,128)(2,1)S(1)} %select_n.556), channel_id=1, source_target_pairs={{0,4},{4,0},{8,12},{12,8},{1,5},{5,1},{9,13},{13,9},{2,6},{6,2},{1... | collective-permute-start | bytes 239624 | tf_op jit(solution)/shard_map/ppermute | solution.py:291
  345.9 27.3 %collective-permute-start.54 = (bf16[2,384,768]{2,1,0:T(8,128)(2,1)}, bf16[2,384,768]{2,1,0:T(8,128)(2,1)S(1)}, u32[]{:S(2)}, u32[]{:S(2)}) collective-permute-start(bf16[2,384,768]{2,1,0:T(8,128)(2,1)} %get-tuple-element.62), channel_id=1, source_target_pairs={{0,16},{16,0},{1,17},{17,1},{2,18},{18,2},{3,19},{19,3},{4,20},{20... | collective-permute-start | bytes 3538952 | tf_op jit(solution)/shard_map/ppermute | solution.py:297
  346.9 27.9 %collective-permute-start.63 = (bf16[384,384]{1,0:T(8,128)(2,1)S(1)}, bf16[384,384]{1,0:T(8,128)(2,1)S(1)}, u32[]{:S(2)}, u32[]{:S(2)}) collective-permute-start(bf16[384,384]{1,0:T(8,128)(2,1)S(1)} %slice_bitcast_fusion.2), channel_id=1, source_target_pairs={{0,1},{1,0},{2,3},{3,2},{4,5},{5,4},{6,7},{7,6},{8,9},{9,8},{10,11... | collective-permute-start | bytes 884744 | tf_op jit(solution)/shard_map/ppermute | solution.py:294
  409.6 26.8 %collective-permute-start.73 = (bf16[768,384]{1,0:T(8,128)(2,1)S(1)}, bf16[768,384]{1,0:T(8,128)(2,1)}, u32[]{:S(2)}, u32[]{:S(2)}) collective-permute-start(bf16[768,384]{1,0:T(8,128)(2,1)S(1)} %add.150), channel_id=1, source_target_pairs={{0,8},{4,12},{8,0},{12,4},{1,9},{5,13},{9,1},{13,5},{2,10},{6,14},... | collective-permute-start | bytes 1769480 | tf_op jit(solution)/shard_map/ppermute | solution.py:291
  (96 other events, 893.9 us)
Sparse Core Ops, SparseCore 0:
  326.9 17.2 reduce-scatter.3

commit v2 on v1

v2 whole, which is shorter than its diff:
```python
import functools

import jax
import jax.numpy as jnp
from jax import lax
from jax.experimental import pallas as pl
from jax.experimental.pallas import tpu as pltpu
from jax.sharding import PartitionSpec as P

HEAD_DIM = 64
EPSILON = 1e-06
SCALE = HEAD_DIM ** (-0.5)
F32 = jnp.float32
LOW = jnp.bfloat16
VMEM = pltpu.VMEM


def dot(a, b, ca, cb):
    return lax.dot_general(a, b, (((ca,), (cb,)), ((), ())), preferred_element_type=F32)


def statistics(rows):
    center = rows - jnp.mean(rows, axis=-1, keepdims=True)
    rate = lax.rsqrt(jnp.mean(center * center, axis=-1, keepdims=True) + EPSILON)
    return center * rate, rate


def norm_back(grad, gain, hat, rate):
    t = grad * gain
    return rate * (
        t
        - jnp.mean(t, axis=-1, keepdims=True)
        - hat * jnp.mean(t * hat, axis=-1, keepdims=True)
    )


def to_blocks(own, pair, frames_cut):
    if not frames_cut:
        return jnp.concatenate((own, pair), axis=0)
    n = own.shape[0] // 8
    return jnp.concatenate(
        [
            rows[(2 * d + f) * n : (2 * d + f + 1) * n]
            for f in range(2)
            for rows in (own, pair)
            for d in range(4)
        ],
        axis=0,
    )


def from_blocks(rows, frames_cut):
    half = rows.shape[0] // 2
    if not frames_cut:
        return rows[:half], rows[half:]
    n = half // 8
    return tuple(
        jnp.concatenate(
            [
                rows[f * half + (4 * side + d) * n : f * half + (4 * side + d + 1) * n]
                for d in range(4)
                for f in range(2)
            ],
            axis=0,
        )
        for side in range(2)
    )


def split_store(chip, refs, piece, group, units):
    send_x, keep_x, send_y, keep_y = refs
    to_x = keep_x if piece == 0 else send_x
    to_x[0, group] = jnp.where(chip == 0, units[0], units[1])
    to_x[1, group] = jnp.where(chip == 0, units[1], units[0])
    keep_y[piece, group] = jnp.where(chip == 0, units[2], units[3])
    send_y[piece, group] = jnp.where(chip == 0, units[3], units[2])


def columns(off_ref, piece, width):
    return pl.ds(pl.multiple_of(off_ref[piece], 128), width)


def attend_forward_kernel(pieces, frames_cut, *refs):
    off, own, pair, gain, bias = refs[:5]
    weights = refs[5 : 5 + 2 * pieces]
    rest = list(refs[5 + 2 * pieces :])
    parts_out = [rest.pop(0)] if frames_cut else [rest.pop(0), rest.pop(0)]
    normed, joined_a, joined_b, out_a, out_b, total = rest
    rows = to_blocks(own[...].astype(F32), pair[...].astype(F32), frames_cut)
    hat, _ = statistics(rows)
    normed[...] = (hat * gain[...]).astype(LOW)
    width = weights[0].shape[1]
    heads3 = joined_a.shape[1]
    for group, joined in enumerate((joined_a, joined_b)):
        acc = None
        for p in range(pieces):
            w = weights[group * pieces + p]
            term = dot(normed[:, columns(off, p, width)], w[:heads3, :], 1, 1)
            acc = term if acc is None else acc + term
        joined[...] = acc.astype(LOW)
    block = normed.shape[0] // 2
    inner = heads3 // 3

    def one_block(b, carry):
        at = pl.ds(pl.multiple_of(b * block, 16), block)
        for joined, out in ((joined_a, out_a), (joined_b, out_b)):
            rows3 = joined[at, :]
            parts = []
            for h in range(inner // HEAD_DIM):
                lo = h * HEAD_DIM
                q = rows3[:, lo : lo + HEAD_DIM]
                k = rows3[:, inner + lo : inner + lo + HEAD_DIM]
                v = rows3[:, 2 * inner + lo : 2 * inner + lo + HEAD_DIM]
                s = dot(q, k, 1, 1) * SCALE + bias[...]
                e = jnp.exp(s - jnp.max(s, axis=-1, keepdims=True))
                w = (e / jnp.sum(e, axis=-1, keepdims=True)).astype(LOW)
                parts.append(dot(w, v, 1, 0))
            out[at, :] = jnp.concatenate(parts, axis=1).astype(LOW)
        return carry

    lax.fori_loop(0, 2, one_block, 0)
    for p in range(pieces):
        total[:, columns(off, p, width)] = dot(
            out_a[...], weights[p][heads3:, :], 1, 0
        ) + dot(out_b[...], weights[pieces + p][heads3:, :], 1, 0)
    first, second = from_blocks(total[...], frames_cut)
    if frames_cut:
        parts_out[0][...] = jnp.concatenate((first, second), axis=0).astype(LOW)
    else:
        parts_out[0][...] = first.astype(LOW)
        parts_out[1][...] = second.astype(LOW)


def attend_backward_kernel(pieces, frames_cut, *refs):
    n_in = 10 if frames_cut else 2
    off, bias, normed, joined_a, joined_b, out_a, out_b = refs[:7]
    head = refs[7 : 7 + n_in]
    weights = refs[7 + n_in : 7 + n_in + 2 * pieces]
    rest = list(refs[7 + n_in + 2 * pieces :])
    part_own, part_pair = rest.pop(0), rest.pop(0)
    grads = [rest.pop(0) for _ in range(4 if pieces == 2 else 1)]
    if frames_cut:
        carried, gain_grad = rest.pop(0), rest.pop(0)
    upstream, djoined_a, djoined_b, dout_a, dout_b, total = rest
    half = upstream.shape[0] // 2
    if frames_cut:
        base_own, base_pair, add_l, add_r, grad_l, grad_r, gain, cot_own, cot_pair, _ = head
        both = []
        for lo, base, cot in ((0, base_own, cot_own), (half, base_pair, cot_pair)):
            at = slice(lo, lo + half)
            far = slice(half - lo, 2 * half - lo)
            rows = base[...].astype(F32) + (add_l[at, :].astype(F32) + add_r[far, :].astype(F32))
            hat, rate = statistics(rows)
            dn = grad_l[at, :].astype(F32) + grad_r[far, :].astype(F32)
            dx = cot[...].astype(F32) + norm_back(dn, gain[...], hat, rate)
            if lo == 0:
                carried[...] = dx
                gain_grad[...] = jnp.sum(dn * hat, axis=0, keepdims=True)
            both.append(dx)
        upstream[...] = to_blocks(both[0], both[1], frames_cut).astype(LOW)
    else:
        upstream[:half, :] = head[0][...]
        upstream[half:, :] = head[1][...]
    width = weights[0].shape[1]
    heads3 = joined_a.shape[1]
    inner = heads3 // 3
    for group, (out, dout) in enumerate(((out_a, dout_a), (out_b, dout_b))):
        acc = None
        for p in range(pieces):
            w = weights[group * pieces + p]
            dy = upstream[:, columns(off, p, width)]
            term = dot(dy, w[heads3:, :], 1, 1)
            acc = term if acc is None else acc + term
        dout[...] = acc.astype(LOW)

    def one_block(b, carry):
        at = pl.ds(pl.multiple_of(b * half, 16), half)
        for joined, dout, djoined in (
            (joined_a, dout_a, djoined_a),
            (joined_b, dout_b, djoined_b),
        ):
            rows3 = joined[at, :]
            do3 = dout[at, :]
            dqs, dks, dvs = [], [], []
            for h in range(inner // HEAD_DIM):
                lo = h * HEAD_DIM
                q = rows3[:, lo : lo + HEAD_DIM]
                k = rows3[:, inner + lo : inner + lo + HEAD_DIM]
                v = rows3[:, 2 * inner + lo : 2 * inner + lo + HEAD_DIM]
                do = do3[:, lo : lo + HEAD_DIM]
                s = dot(q, k, 1, 1) * SCALE + bias[...]
                e = jnp.exp(s - jnp.max(s, axis=-1, keepdims=True))
                w = e / jnp.sum(e, axis=-1, keepdims=True)
                dw = dot(do, v, 1, 1)
                ds = (w * (dw - jnp.sum(w * dw, axis=-1, keepdims=True))).astype(LOW)
                dqs.append(dot(ds, k, 1, 0) * SCALE)
                dks.append(dot(ds, q, 0, 0) * SCALE)
                dvs.append(dot(w.astype(LOW), do, 0, 0))
            djoined[at, :] = jnp.concatenate(dqs + dks + dvs, axis=1).astype(LOW)
        return carry

    lax.fori_loop(0, 2, one_block, 0)
    chip = off[pieces]
    for p in range(pieces):
        cols = columns(off, p, width)
        wide = normed[:, cols]
        dy = upstream[:, cols]
        for group, (djoined, out) in enumerate(((djoined_a, out_a), (djoined_b, out_b))):
            value = dot(djoined[...], wide, 0, 0).astype(LOW)
            proj = dot(out[...], dy, 0, 0).astype(LOW)
            if pieces == 2:
                units = [value[u * inner : (u + 1) * inner] for u in range(3)] + [proj]
                split_store(chip, grads, p, group, units)
            else:
                grads[0][group, :heads3] = value
                grads[0][group, heads3:] = proj
        total[:, cols] = dot(djoined_a[...], weights[p][:heads3, :], 1, 0) + dot(
            djoined_b[...], weights[pieces + p][:heads3, :], 1, 0
        )
    first, second = from_blocks(total[...], frames_cut)
    part_own[...] = first.astype(LOW)
    part_pair[...] = second.astype(LOW)


def feed_kernel(pieces, chunks, packed, *refs):
    off, base_own, base_pair, add_l, add_r, gain, cot_own, cot_pair = refs[:8]
    at = 8
    n_w = chunks * pieces * (1 if packed else 2)
    weights = refs[at : at + n_w]
    at += n_w
    out_own, out_pair, dn_part = refs[at : at + 3]
    at += 3
    grads = refs[at : at + 4]
    normed, cot, total, dtotal, base_sum = refs[at + 4 :]
    half = normed.shape[0] // 2
    for lo, base, c in ((0, base_own, cot_own), (half, base_pair, cot_pair)):
        rows_at, far = slice(lo, lo + half), slice(half - lo, 2 * half - lo)
        rows = base[...].astype(F32) + (
            add_l[rows_at, :].astype(F32) + add_r[far, :].astype(F32)
        )
        if lo == 0:
            base_sum[...] = rows
        hat, _ = statistics(rows)
        normed[rows_at, :] = (hat * gain[...]).astype(LOW)
        cot[rows_at, :] = c[...]
    for c in range(chunks):
        group, side = c % 2, c // 2
        ups, downs = [], []
        for p in range(pieces):
            if packed:
                w = weights[c * pieces + p]
                wide = w.shape[0] // 2
                ups.append(w[:wide, :])
                downs.append(w[wide:, :])
            else:
                ups.append(weights[2 * (c * pieces + p)][...])
                downs.append(weights[2 * (c * pieces + p) + 1][...])
        width = ups[0].shape[0]
        hidden = dact = None
        for p in range(pieces):
            cols = columns(off, p, width)
            term = dot(normed[:, cols], ups[p], 1, 0)
            dterm = dot(cot[:, cols], downs[p], 1, 1)
            hidden = term if hidden is None else hidden + term
            dact = dterm if dact is None else dact + dterm
        cdf = 0.5 * (1.0 + lax.erf(hidden * (2.0**-0.5)))
        act = (hidden * cdf).astype(LOW)
        slope = cdf + hidden * (jnp.exp(-0.5 * hidden * hidden) * (2.0 * jnp.pi) ** -0.5)
        dhid = (dact * slope).astype(LOW)
        for p in range(pieces):
            cols = columns(off, p, width)
            term = dot(act, downs[p], 1, 0)
            dterm = dot(dhid, ups[p], 1, 1)
            if c == 0:
                total[:, cols] = term
                dtotal[:, cols] = dterm
            else:
                total[:, cols] += term
                dtotal[:, cols] += dterm
            up_grad = dot(normed[:, cols], dhid, 0, 0).astype(LOW)
            down_grad = dot(act, cot[:, cols], 0, 0).astype(LOW)
            if packed:
                send_x, keep_x, send_y, keep_y = grads
                (keep_x if p == 0 else send_x)[side, group] = up_grad
                (keep_y if side == 0 else send_y)[p, group] = down_grad
            else:
                grads[side][group] = up_grad
                grads[2 + side][group] = down_grad
    out_own[...] = base_sum[...] + total[:half, :]
    out_pair[...] = total[half:, :].astype(LOW)
    dn_part[...] = dtotal[...].astype(LOW)


def store_parts(rows, outs):
    n = rows.shape[0] // len(outs)
    for d, out in enumerate(outs):
        out[...] = rows[d * n : (d + 1) * n].astype(out.dtype)


def norm_back_kernel(part, received, base, gain, carried, *outs):
    hat, rate = statistics(base[...].astype(F32))
    dn = part[...].astype(F32) + received[...].astype(F32)
    store_parts(carried[...].astype(F32) + norm_back(dn, gain[...], hat, rate), outs[:4])
    outs[4][...] = jnp.sum(dn * hat, axis=0, keepdims=True)


def sum_kernel(n, *refs):
    total = refs[n - 1][...].astype(F32)
    for k in range(n - 2, -1, -1):
        total = refs[k][...].astype(F32) + total
    store_parts(total, refs[n:])


def in_vmem(n):
    return [pl.BlockSpec(memory_space=VMEM)] * n


def shape_of(shape, dtype):
    return jax.ShapeDtypeStruct(shape, dtype)


def run(kernel, operands, outs, scratch, flops, name):
    moved = sum(o.size * o.dtype.itemsize for o in operands) + sum(
        o.size * o.dtype.itemsize for o in outs
    )
    scalar = operands[0].dtype == jnp.int32
    specs = in_vmem(len(operands))
    if scalar:
        specs[0] = pl.BlockSpec(memory_space=pltpu.SMEM)
    return pl.pallas_call(
        kernel,
        out_shape=outs,
        in_specs=specs,
        out_specs=in_vmem(len(outs)),
        scratch_shapes=scratch,
        compiler_params=pltpu.CompilerParams(vmem_limit_bytes=20 << 20),
        cost_estimate=pl.CostEstimate(flops=flops, bytes_accessed=moved, transcendentals=0),
        name=name,
    )(*operands)


def after(value, *tokens):
    return lax.optimization_barrier((value, *tokens))[0]


def body(sizes, tokens, norm_gains, temporal_qkv, temporal_proj, spatial_qkv, spatial_proj, up_weight, down_weight, cotangent):
    n_fsdp, n_ctx, n_tp = sizes
    swap = n_fsdp == 2
    d_model = tokens.shape[3]
    d_part = d_model // n_fsdp
    places = tokens.shape[0]
    block = 2 * (-(-places // 4))
    x, i, z = lax.axis_index("fsdp"), lax.axis_index("ctx"), lax.axis_index("tp")
    core, chip = i % 2, i // 2
    is_source = (z // 2) == core

    def permute_ctx(v, bits):
        return lax.ppermute(v, "ctx", [(a, a ^ bits) for a in range(n_ctx)])

    def permute_tp(v, bits):
        return lax.ppermute(v, "tp", [(a, a ^ bits) for a in range(n_tp)])

    def permute_fsdp(v):
        return lax.ppermute(v, "fsdp", [(0, 1), (1, 0)])

    outward, inward = [], []
    for a in range(n_ctx):
        for b in (2 * (a % 2), 2 * (a % 2) + 1):
            outward.append((a * n_tp + b, a * n_tp + (b ^ 2)))
            inward.append((a * n_tp + (b ^ 2), a * n_tp + b))

    def exclusive(parts, bits):
        low, high = (bits & 1) == 1, (bits & 2) == 2
        parts = [jnp.where(low, parts[d ^ 1], parts[d]) for d in range(4)]
        return [jnp.where(high, parts[d ^ 2], parts[d]) for d in range(4)]

    slot_bits = (z & 2) | ((z & 1) ^ core)
    part_rows = 2 * block

    def to_time(rows):
        t = jnp.transpose(rows, (2, 1, 0, 3))
        t = jnp.pad(t, ((0, 0), (0, 0), (0, 2 * block - places), (0, 0)))
        parts = [t[c, :, b * block : (b + 1) * block] for c in range(2) for b in range(2)]
        parts = exclusive([v.reshape(part_rows, d_model) for v in parts], i)
        got = [parts[0]] + [permute_ctx(parts[e], e) for e in range(1, 4)]
        return exclusive(got, slot_bits)

    def from_time(own):
        parts = exclusive(own, slot_bits)
        got = [parts[0]] + [permute_ctx(parts[e], e) for e in range(1, 4)]
        got = [v.reshape(2, block, d_model) for v in exclusive(got, i)]
        t = jnp.stack(
            [jnp.concatenate((got[2 * c], got[2 * c + 1]), axis=1)[:, :places] for c in range(2)]
        )
        return jnp.transpose(t, (2, 1, 0, 3))

    def turn(own):
        return [own[0]] + [permute_tp(own[e], e) for e in range(1, 4)]

    rows_n = 8 * block
    flat = (rows_n, d_model)

    def attention_pack(qkv, proj):
        return jnp.concatenate((jnp.transpose(qkv, (1, 2, 0)).reshape(-1, d_part), proj), axis=0)

    def spread_first(shard):
        return jnp.where(is_source, shard, lax.ppermute(shard, ("ctx", "tp"), outward))

    hid_half = up_weight.shape[1] // 2

    def feed_pack():
        up = lax.dynamic_slice_in_dim(up_weight, chip * hid_half, hid_half, axis=1)
        down = lax.dynamic_slice_in_dim(down_weight, chip * hid_half, hid_half, axis=0)
        return jnp.concatenate((up, down.reshape(d_part, hid_half)), axis=0)

    def feed_full(shard):
        every = lax.all_gather(shard, "fsdp", axis=0)
        up = every[:, :d_part].reshape(d_model, hid_half)
        down = every[:, d_part:].reshape(n_fsdp, hid_half, d_part)
        return [up, jnp.transpose(down, (1, 0, 2)).reshape(hid_half, d_model)]

    def owner_sum(a, b):
        mine = a + permute_tp(b, 1)
        return mine + lax.ppermute(mine, ("ctx", "tp"), inward)

    def ordered(mine, other):
        return jnp.stack((jnp.where(chip == 0, mine, other), jnp.where(chip == 0, other, mine)))

    def to_pair(both):
        return jnp.where(is_source, both, permute_ctx(both, 1))

    def to_both(mine):
        return to_pair(ordered(mine, permute_ctx(mine, 2)))

    def first_sends(grads):
        send_x, _, send_y, _ = grads
        return permute_fsdp(send_x), permute_ctx(send_y, 2)

    def first_sums(grads, got):
        _, keep_x, _, keep_y = grads
        by_x, by_y = keep_x + got[0], keep_y + got[1]
        return (by_x[0], by_y[0]), (by_x[1], by_y[1])

    def second_sends(send):
        return permute_ctx(send[0], 2), permute_fsdp(send[1])

    def second_sums(keep, got):
        by_x, by_y = keep[0] + got[0], keep[1] + got[1]
        return jnp.stack((by_x[0], by_y[0])), jnp.stack((by_x[1], by_y[1]))

    def attention_out(total):
        joined_grad = jnp.stack((total[0, 0], total[1, 0], total[0, 1])).astype(F32)
        return jnp.transpose(joined_grad, (2, 0, 1)), total[1, 1].astype(F32)

    def feed_out(total):
        up = jnp.concatenate((total[0, 0], total[1, 0]), axis=1)
        down = jnp.concatenate((total[0, 1], total[1, 1]), axis=0)
        return up.astype(F32), down.astype(F32)

    def attention_grads_wide(grads):
        total = lax.psum_scatter(grads[0], "fsdp", scatter_dimension=2, tiled=True)
        total = total + permute_ctx(total, 2)
        mine = owner_sum(total[0], total[1])
        full = jnp.where(is_source, mine, permute_ctx(mine, 1)).astype(F32)
        inner = full.shape[0] // 4
        joined_grad = full[: 3 * inner].reshape(3, inner, d_part)
        return jnp.transpose(joined_grad, (2, 0, 1)), full[3 * inner :]

    def feed_grads_wide(grads):
        up = grads[0] + permute_ctx(grads[1], 2)
        down = grads[2] + permute_ctx(grads[3], 2)
        up = lax.psum_scatter(up, "fsdp", scatter_dimension=1, tiled=True)
        down = lax.psum_scatter(down, "fsdp", scatter_dimension=2, tiled=True)
        up = to_both(owner_sum(up[0], up[1]))
        down = to_both(owner_sum(down[0], down[1]))
        return (
            jnp.concatenate((up[0], up[1]), axis=1).astype(F32),
            jnp.concatenate((down[0], down[1]), axis=0).astype(F32),
        )

    pieces = 2 if swap else 1
    width = d_model // pieces
    if swap:
        offsets = jnp.stack((x * width, (1 - x) * width, chip)).astype(jnp.int32)
    else:
        offsets = jnp.stack((0 * chip, chip)).astype(jnp.int32)

    at = jnp.arange(rows_n, dtype=jnp.int32)
    far = jnp.float32(-1e30)
    bias_t = jnp.where((at % block)[:, None] == (at % block)[None, :], 0.0, far).astype(F32)
    owner = jnp.where(at < rows_n // 2, core, 1 - core)
    real = owner * block + at % block < places
    bias_s = jnp.broadcast_to(jnp.where(real, 0.0, far).astype(F32)[None], (rows_n, rows_n))

    two = (2 * rows_n, d_model)
    joined = (2 * rows_n, 3 * temporal_qkv.shape[2])
    heads = (2 * rows_n, temporal_qkv.shape[2])
    unit = 2 * rows_n * d_model * d_model

    def attend_forward(own, pair, gain, bias, weights, cut, name):
        parts = [shape_of(two, LOW)] if cut else [shape_of(flat, LOW)] * 2
        outs = parts + [
            shape_of(two, LOW),
            shape_of(joined, LOW),
            shape_of(joined, LOW),
            shape_of(heads, LOW),
            shape_of(heads, LOW),
        ]
        return run(
            functools.partial(attend_forward_kernel, pieces, cut),
            [offsets, own, pair, gain, bias, *weights],
            outs,
            [VMEM(two, F32)],
            6 * unit,
            name,
        )

    def attend_backward(saved, bias, head, weights, cut, name):
        outs = [shape_of(flat, LOW)] * 2
        if swap:
            outs += [shape_of((2, 2, temporal_qkv.shape[2], width), LOW)] * 4
        else:
            outs += [shape_of((2, 4 * temporal_qkv.shape[2], width), LOW)]
        if cut:
            outs += [shape_of(flat, F32), shape_of((1, d_model), F32)]
        got = run(
            functools.partial(attend_backward_kernel, pieces, cut),
            [offsets, bias, *saved, *head, *weights],
            outs,
            [
                VMEM(two, LOW),
                VMEM(joined, LOW),
                VMEM(joined, LOW),
                VMEM(heads, LOW),
                VMEM(heads, LOW),
                VMEM(two, F32),
            ],
            12 * unit,
            name,
        )
        n = 6 if swap else 3
        return got[0], got[1], got[2:n], got[n:]

    def norm_backward(part, received, base, gain, carried, name):
        *parts, gain_grad = run(
            norm_back_kernel,
            [part, received, base, gain, carried],
            [shape_of((part_rows, d_model), LOW)] * 4 + [shape_of((1, d_model), F32)],
            [],
            20 * rows_n * d_model,
            name,
        )
        return parts, gain_grad

    def sum_parts(terms, name):
        return run(
            functools.partial(sum_kernel, len(terms)),
            list(terms),
            [shape_of((part_rows, d_model), LOW)] * 4,
            [],
            4 * rows_n * d_model,
            name,
        )

    def other_x(v):
        return permute_fsdp(v) if swap else lax.all_gather(v, "fsdp", axis=1, tiled=True)

    def joined_pieces(first, first_x, second, second_x):
        return [first, first_x, second, second_x] if swap else [first_x, second_x]

    barrier = lax.optimization_barrier

    pack_t = attention_pack(temporal_qkv, temporal_proj)
    first_t = spread_first(pack_t)
    start = jnp.concatenate(to_time(tokens), axis=0)
    pack_s = attention_pack(spatial_qkv, spatial_proj)
    pack_f = feed_pack()
    if swap:
        gain_other = permute_fsdp(norm_gains)
        gains = jnp.where(
            x == 0,
            jnp.concatenate((norm_gains, gain_other), axis=1),
            jnp.concatenate((gain_other, norm_gains), axis=1),
        ).astype(F32)
    else:
        gains = lax.all_gather(norm_gains, "fsdp", axis=1, tiled=True).astype(F32)
    first_t, start, pack_s, pack_f, cot = barrier((first_t, start, pack_s, pack_f, cotangent))

    second_t = permute_tp(first_t, 1)
    first_tx = other_x(first_t)
    start_pair = permute_ctx(start, 1)
    cot_time = to_time(cot)
    second_t, first_tx, start_pair, pack_s = barrier((second_t, first_tx, start_pair, pack_s))

    second_tx = other_x(second_t)
    first_s = spread_first(pack_s)
    first_f = spread_first(after(pack_f, second_t))
    second_tx, first_s = barrier((second_tx, first_s))

    second_s = permute_tp(first_s, 1)
    first_sx = other_x(first_s)
    weights_t = joined_pieces(first_t, first_tx, second_t, second_tx)
    part_t, pair_part_t, *saved_t = attend_forward(
        start, start_pair, gains[0:1], bias_t, weights_t, False, "time_forward"
    )
    back_t = permute_ctx(pair_part_t, 1)
    sums = sum_parts((start, part_t, back_t), "time_sum")
    sums, second_s, first_sx, first_f, cot_time = barrier((sums, second_s, first_sx, first_f, cot_time))
    second_sx = other_x(second_s)
    own1 = jnp.concatenate(turn(sums), axis=0)
    if swap:
        first_fy = permute_ctx(first_f, 2)
        own1, second_sx, first_f = barrier((own1, second_sx, first_f))
        first_fx = permute_fsdp(first_f)
    pair1 = permute_ctx(own1, 1)
    second_f = permute_tp(first_f, 1)
    weights_s = joined_pieces(first_s, first_sx, second_s, second_sx)

    part_s, *saved_s = attend_forward(
        own1, pair1, gains[1:2], bias_s, weights_s, True, "space_forward"
    )
    got_s = permute_ctx(part_s, 1)
    if swap:
        got_s, second_f, first_fx, first_fy, cot_time = barrier(
            (got_s, second_f, first_fx, first_fy, cot_time)
        )
        second_fx = permute_fsdp(second_f)
        second_fy = permute_ctx(second_f, 2)
        first_fxy = permute_ctx(first_fx, 2)
        cot_own = jnp.concatenate(turn(cot_time), axis=0)
        cot_pair = permute_ctx(cot_own, 1)
        second_fx, second_fy, cot_pair = barrier((second_fx, second_fy, cot_pair))
        second_fxy = permute_fsdp(second_fy)
        weights_f = [
            first_f,
            first_fx,
            second_f,
            second_fx,
            first_fy,
            first_fxy,
            second_fy,
            second_fxy,
        ]
    else:
        cot_own = jnp.concatenate(turn(cot_time), axis=0)
        cot_pair = permute_ctx(cot_own, 1)
        both_f = (first_f, second_f)
        weights_f = [
            w for v in both_f + tuple(permute_ctx(v, 2) for v in both_f) for w in feed_full(v)
        ]

    if swap:
        outs_f = [shape_of((2, 2, width, hid_half), LOW)] * 4
    else:
        outs_f = [shape_of((2, width, hid_half), LOW)] * 2 + [shape_of((2, hid_half, width), LOW)] * 2
    out_own, out_pair, dn3, *grads_f = run(
        functools.partial(feed_kernel, pieces, 4, swap),
        [offsets, own1, pair1, part_s, got_s, gains[2:3], cot_own, cot_pair, *weights_f],
        [shape_of(flat, F32), shape_of(flat, LOW), shape_of(two, LOW), *outs_f],
        [VMEM(two, LOW), VMEM(two, LOW), VMEM(two, F32), VMEM(two, F32), VMEM(flat, F32)],
        24 * unit,
        "feed",
    )
    got3 = permute_ctx(dn3, 1)
    if swap:
        got_f = first_sends(grads_f)

    dn2, pair_dn2, grads_s, (carried2, gain3) = attend_backward(
        saved_s,
        bias_s,
        [own1, pair1, part_s, got_s, dn3, got3, gains[2:3], cot_own, cot_pair, gains[1:2]],
        weights_s,
        True,
        "space_backward",
    )
    got2 = permute_ctx(pair_dn2, 1)
    parts1, gain2 = norm_backward(dn2, got2, own1, gains[1:2], carried2, "space_norm")
    own_t = jnp.concatenate(turn(parts1), axis=0)
    pair_t = permute_ctx(own_t, 1)
    if swap:
        got_sums_s = first_sends(grads_s)
        own_t, got_f = barrier((own_t, got_f))
        keep_f, send_f = first_sums(grads_f, got_f)
        send_f, own_t, pair_t = barrier((send_f, own_t, pair_t))
        got_f = second_sends(send_f)

    dn1, pair_dn1, grads_t, _ = attend_backward(
        saved_t, bias_t, [own_t, pair_t], weights_t, False, "time_backward"
    )
    if swap:
        grads_t, pair_dn1, got_sums_s, out_pair, gain2 = barrier(
            (grads_t, pair_dn1, got_sums_s, out_pair, gain2)
        )
        got_sums_t = first_sends(grads_t)
    got1 = permute_ctx(pair_dn1, 1)
    parts0, gain1 = norm_backward(dn1, got1, start, gains[0:1], own_t, "time_norm")
    gain_all = jnp.concatenate((gain1, gain2, gain3), axis=0)
    got_out = permute_ctx(out_pair, 1)
    if swap:
        gain_all = gain_all + permute_ctx(gain_all, 1)
        a_f, b_f = second_sums(keep_f, got_f)
        add_f = permute_tp(b_f, 1)
        keep_s, send_s = first_sums(grads_s, got_sums_s)
        got_sums_t, parts0, send_s, gain_all, got_out = barrier(
            (got_sums_t, parts0, send_s, gain_all, got_out)
        )
        keep_t, send_t = first_sums(grads_t, got_sums_t)
        got_sums_t = second_sends(send_t)
        gain_all = gain_all + permute_ctx(gain_all, 2)
        out_parts = sum_parts((out_own, got_out), "feed_sum")
        got_sums_t, send_s, add_f, gain_all, out_parts = barrier(
            (got_sums_t, send_s, add_f, gain_all, out_parts)
        )
        a_t, b_t = second_sums(keep_t, got_sums_t)
        add_t = permute_tp(b_t, 1)
        got_sums_s = second_sends(send_s)
        a_f = a_f + add_f
        add_f = lax.ppermute(a_f, ("ctx", "tp"), inward)
        gain_all = gain_all + permute_tp(gain_all, 1)
        add_t, got_sums_s, parts0, out_parts, gain_all = barrier(
            (add_t, got_sums_s, parts0, out_parts, gain_all)
        )
        a_t = a_t + add_t
        add_t = lax.ppermute(a_t, ("ctx", "tp"), inward)
        a_s, b_s = second_sums(keep_s, got_sums_s)
        add_s = permute_tp(b_s, 1)
        tokens_grad = from_time(parts0).astype(F32)
        add_t, add_s, add_f, out_parts, gain_all, tokens_grad = barrier(
            (add_t, add_s, add_f, out_parts, gain_all, tokens_grad)
        )
        total_t = a_t + add_t
        other_t = permute_ctx(total_t, 2)
        a_s = a_s + add_s
        add_s = lax.ppermute(a_s, ("ctx", "tp"), inward)
        total_f = a_f + add_f
        other_f = permute_ctx(total_f, 2)
        out_time = turn(out_parts)
        other_t, other_f, add_s, out_time, gain_all = barrier(
            (other_t, other_f, add_s, out_time, gain_all)
        )
        total_s = a_s + add_s
        other_s = permute_ctx(total_s, 2)
        t_qkv, t_proj = attention_out(to_pair(ordered(total_t, other_t)))
        up_grad, down_grad = feed_out(to_pair(ordered(total_f, other_f)))
        gain_all = gain_all + permute_tp(gain_all, 2)
        block_out = from_time(out_time)
        s_qkv, s_proj = attention_out(to_pair(ordered(total_s, other_s)))
        keep = lax.dynamic_slice_in_dim(gain_all, x * d_part, d_part, axis=1)
        send = lax.dynamic_slice_in_dim(gain_all, (1 - x) * d_part, d_part, axis=1)
        gain_grads = keep + permute_fsdp(send)
    else:
        tokens_grad = from_time(parts0).astype(F32)
        block_out = from_time(turn(sum_parts((out_own, got_out), "feed_sum")))
        up_grad, down_grad = feed_grads_wide(grads_f)
        s_qkv, s_proj = attention_grads_wide(grads_s)
        t_qkv, t_proj = attention_grads_wide(grads_t)
        for bits in (1, 2):
            gain_all = gain_all + permute_ctx(gain_all, bits)
        for bits in (1, 2):
            gain_all = gain_all + permute_tp(gain_all, bits)
        gain_grads = lax.psum_scatter(gain_all, "fsdp", scatter_dimension=1, tiled=True)
    return (
        block_out,
        tokens_grad,
        gain_grads,
        t_qkv,
        t_proj,
        s_qkv,
        s_proj,
        up_grad,
        down_grad,
    )


def solution(mesh):
    rows = P("tp", "ctx", "fsdp", None)
    weights = (
        P(None, "fsdp"),
        P("fsdp", None, "tp"),
        P("tp", "fsdp"),
        P("fsdp", None, "tp"),
        P("tp", "fsdp"),
        P("fsdp", "tp"),
        P("tp", "fsdp"),
    )
    sizes = (mesh.shape["fsdp"], mesh.shape["ctx"], mesh.shape["tp"])
    return jax.shard_map(
        functools.partial(body, sizes),
        mesh=mesh,
        in_specs=(rows, *weights, rows),
        out_specs=(rows, rows, *weights),
        check_vma=False,
    )
```

time: 461 us -> 347 us (0.75)
  waiting for transfers between devices: 201 us -> 140 us
  local copies, waits for them, and re-layouts: 36.4 us -> 19.2 us
  starting transfers between devices: 108 us -> 92.5 us
  between operations: 15.5 us -> 2.16 us
  other arithmetic: 30.1 us -> 37.7 us
  Pallas kernels: 57.5 us -> 50.6 us
    ppermute x20, starting transfers between devices: 31.6 us -> 13.3 us  [permute_tp(): return lax.ppermute(v, 'tp', [(a, a ^ bits) for a in range(n_tp)])]
    ppermute x41 -> x39, waiting for transfers between devices: 70 us -> 52.4 us  [permute_ctx(): return lax.ppermute(v, 'ctx', [(a, a ^ bits) for a in range(n_ctx)])]
    unnamed x2 -> x0, waiting for transfers between devices: 14.2 us -> none
    ppermute x9 -> x15, waiting for transfers between devices: 34.2 us -> 22.9 us  [permute_fsdp(): return lax.ppermute(v, 'fsdp', [(0, 1), (1, 0)])]
    ppermute x20, waiting for transfers between devices: 62.1 us -> 51.3 us  [permute_tp(): return lax.ppermute(v, 'tp', [(a, a ^ bits) for a in range(n_tp)])]
    unnamed x112 -> x104, local copies, waits for them, and re-layouts: 17.3 us -> 9.48 us
    ppermute x6, waiting for transfers between devices: 20.7 us -> 13.2 us  [the longest x3 8.72 us: spread_first(): lax.ppermute(shard, ('ctx', 'tp'), outward)]
    pallas_call x7 -> x9, Pallas kernels: 57.5 us -> 50.6 us  [run(): pl.pallas_call(kernel, out_shape=outs, in_specs=specs, out_specs=in_vmem(...]
  transfers between devices with their start and end apart: 77 -> 80, of which waited for: 28 -> 37; matrix products, arithmetic and copies ran while one was open for 12% -> 12% of each run, Pallas kernels for 9% -> 10%
where the time goes in v2:
time: 347 us; the launch traced here: 342 us
  waiting for transfers between devices  140 us (40%)
  starting transfers between devices  92.5 us (27%)
  Pallas kernels  50.6 us (15%)
  other arithmetic  37.7 us (11%)
  local copies, waits for them, and re-layouts  19.2 us (6%)
    ppermute x39, waiting for transfers between devices, permute_ctx(): return lax.ppermute(v, 'ctx', [(a, a ^ bits) for a in range(n_ctx)])  52.4 us
    ppermute x20, waiting for transfers between devices, permute_tp(): return lax.ppermute(v, 'tp', [(a, a ^ bits) for a in range(n_tp)])  51.3 us
    pallas_call x9, Pallas kernels, run(): pl.pallas_call(kernel, out_shape=outs, in_specs=specs, out_specs=in_vmem(...  50.6 us
    ppermute x39, starting transfers between devices, permute_ctx(): return lax.ppermute(v, 'ctx', [(a, a ^ bits) for a in range(n_ctx)])  48.5 us
    ppermute x15, waiting for transfers between devices, permute_fsdp(): return lax.ppermute(v, 'fsdp', [(0, 1), (1, 0)])  22.9 us
    ppermute x15, starting transfers between devices, permute_fsdp(): return lax.ppermute(v, 'fsdp', [(0, 1), (1, 0)])  15 us
    ppermute x20, starting transfers between devices, permute_tp(): return lax.ppermute(v, 'tp', [(a, a ^ bits) for a in range(n_tp)])  13.3 us
    unnamed x104, local copies, waits for them, and re-layouts  9.48 us
  transfers between devices with their start and end apart: 80, of which 37 were waited for; matrix products, arithmetic and copies ran while one was open for 12% of the time, Pallas kernels for 10%

profile of v2, /device:TPU:1, one launch (start us, length us, event | category | flops | bytes accessed | tf_op | source)
XLA Modules:
  0.0 341.9 jit_solution(11167870678542747961)
XLA Ops:
  4.2 5.6 %collective-permute-start.3 = (bf16[52,768]{1,0:T(8,128)(2,1)S(1)}, bf16[52,768]{1,0:T(8,128)(2,1)}, u32[]{:S(2)}, u32[]{:S(2)}) collective-permute-start(bf16[52,768]{1,0:T(8,128)(2,1)S(1)} %select_n.472), channel_id=1, source_target_pairs={{0,4},{4,0},{8,12},{12,8},{1,5},{5,1},{9,13},{13,9},{2,6},{6,2},{1... | collective-permute-start | bytes 239624 | tf_op jit(solution)/shard_map/ppermute | solution.py:358
  17.0 3.0 collective-permute-done
  25.5 9.3 %collective-permute-done.7 = bf16[3,384]{1,0:T(4,128)(2,1)S(1)} collective-permute-done((bf16[3,384]{1,0:T(4,128)(2,1)S(1)}, bf16[3,384]{1,0:T(4,128)(2,1)S(1)}, u32[]{:S(2)}, u32[]{:S(2)}) %collective-permute-start.7) | collective-permute-done | bytes 2336 | tf_op jit(solution)/shard_map/ppermute | solution.py:364
  34.8 3.6 %collective-permute-done.4.refs_7_.refs_11_ = bf16[768,384]{1,0:T(8,128)(2,1)S(1)} collective-permute-done((bf16[768,384]{1,0:T(8,128)(2,1)S(1)}, bf16[768,384]{1,0:T(8,128)(2,1)S(1)}, u32[]{:S(2)}, u32[]{:S(2)}) %collective-permute-start.4) | collective-permute-done | bytes 589856 | tf_op jit(solution)/shard_map/ppermute | solution.py:361
  49.6 5.7 %collective-permute-done.9 = bf16[768,384]{1,0:T(8,128)(2,1)} collective-permute-done((bf16[768,384]{1,0:T(8,128)(2,1)S(1)}, bf16[768,384]{1,0:T(8,128)(2,1)}, u32[]{:S(2)}, u32[]{:S(2)}) %collective-permute-start.9) | collective-permute-done | bytes 589856 | tf_op jit(solution)/shard_map/ppermute | solution.py:407
  58.3 6.3 %time_forward.1 = (bf16[208,768]{1,0:T(8,128)(2,1)S(1)}, bf16[208,768]{1,0:T(8,128)(2,1)S(1)}, bf16[416,768]{1,0:T(8,128)(2,1)S(1)}, bf16[416,576]{1,0:T(8,128)(...) custom-call(s32[3]{0:T(128)S(1)} %pad_add_fusion.refs_0_, ...), custom_call_target="tpu_custom_call" | custom-call | flops 1472200704 | bytes 5730316 | tf_op jit(solution)/shard_map/time_forward/pallas_call | solution.py:330
  64.7 4.5 %collective-permute-start.10 = (bf16[208,768]{1,0:T(8,128)(2,1)S(1)}, bf16[208,768]{1,0:T(8,128)(2,1)S(1)}, u32[]{:S(2)}, u32[]{:S(2)}) collective-permute-start(bf16[208,768]{1,0:T(8,128)(2,1)S(1)} %get-tuple-element.177), channel_id=1, source_target_pairs={{0,4},{4,0},{8,12},{12,8},{1,5},{5,1},{9,13},{13,9},{2,6},{6,2},{1... | collective-permute-start | bytes 958472 | tf_op jit(solution)/shard_map/ppermute | solution.py:358
  72.0 5.7 %collective-permute-done.11.refs_7_.refs_19_ = bf16[768,384]{1,0:T(8,128)(2,1)S(1)} collective-permute-done((bf16[768,384]{1,0:T(8,128)(2,1)S(1)}, bf16[768,384]{1,0:T(8,128)(2,1)S(1)}, u32[]{:S(2)}, u32[]{:S(2)}) %collective-permute-start.11) | collective-permute-done | bytes 589856 | tf_op jit(solution)/shard_map/ppermute | solution.py:361
  80.6 4.0 %collective-permute-start.18 = (bf16[52,768]{1,0:T(8,128)(2,1)S(1)}, bf16[52,768]{1,0:T(8,128)(2,1)S(1)}, u32[]{:S(2)}, u32[]{:S(2)}) collective-permute-start(bf16[52,768]{1,0:T(8,128)(2,1)S(1)} %get-tuple-element.188), channel_id=1, source_target_pairs={{0,2},{1,3},{2,0},{3,1},{4,6},{5,7},{6,4},{7,5},{8,10},{9,11},{10,... | collective-permute-start | bytes 239624 | tf_op jit(solution)/shard_map/ppermute | solution.py:361
  86.8 3.1 collective-permute-done.19
  92.0 2.9 collective-permute-start.21
  99.4 6.4 %space_forward.1 = (bf16[416,768]{1,0:T(8,128)(2,1)S(1)}, bf16[416,768]{1,0:T(8,128)(2,1)S(1)}, bf16[416,576]{1,0:T(8,128)(2,1)S(1)}, bf16[416,576]{1,0:T(8,128)...) custom-call(s32[3]{0:T(128)S(1)} %pad_add_fusion.refs_0_, ...), custom_call_target="tpu_custom_call" | custom-call | flops 1472200704 | bytes 5730316 | tf_op jit(solution)/shard_map/space_forward/pallas_call | solution.py:330
  109.0 12.1 %collective-permute-done.25.refs_12_ = bf16[768,384]{1,0:T(8,128)(2,1)S(1)} collective-permute-done((bf16[768,384]{1,0:T(8,128)(2,1)S(1)}, bf16[768,384]{1,0:T(8,128)(2,1)S(1)}, u32[]{:S(2)}, u32[]{:S(2)}) %collective-permute-start.25) | collective-permute-done | bytes 589856 | tf_op jit(solution)/shard_map/ppermute | solution.py:358
  123.8 4.0 %collective-permute-start.27 = (bf16[52,768]{1,0:T(8,128)(2,1)S(1)}, bf16[52,768]{1,0:T(8,128)(2,1)S(1)}, u32[]{:S(2)}, u32[]{:S(2)}) collective-permute-start(bf16[52,768]{1,0:T(8,128)(2,1)S(1)} %copy-done.48), channel_id=1, source_target_pairs={{0,2},{1,3},{2,0},{3,1},{4,6},{5,7},{6,4},{7,5},{8,10},{9,11},{10,... | collective-permute-start | bytes 239624 | tf_op jit(solution)/shard_map/ppermute | solution.py:361
  130.7 3.0 collective-permute-done.28
  133.8 3.0 collective-permute-start.31
  139.4 12.4 %collective-permute-done.32.refs_13_ = bf16[768,384]{1,0:T(8,128)(2,1)S(1)} collective-permute-done((bf16[768,384]{1,0:T(8,128)(2,1)S(1)}, bf16[768,384]{1,0:T(8,128)(2,1)S(1)}, u32[]{:S(2)}, u32[]{:S(2)}) %collective-permute-start.32) | collective-permute-done | bytes 589856 | tf_op jit(solution)/shard_map/ppermute | solution.py:358
  152.2 11.4 %feed.1 = (f32[208,768]{1,0:T(8,128)S(1)}, bf16[208,768]{1,0:T(8,128)(2,1)S(1)}, bf16[416,768]{1,0:T(8,128)(2,1)S(1)}, bf16[2,2,384,384]{3,2,1,0:T(8,128)(2,1)S(...) custom-call(s32[3]{0:T(128)S(1)} %pad_add_fusion.refs_0_, ...), custom_call_target="tpu_custom_call" | custom-call | flops 5888802816 | bytes 13593612 | tf_op jit(solution)/shard_map/feed/pallas_call | solution.py:330
  167.8 12.9 %space_backward.1 = (bf16[208,768]{1,0:T(8,128)(2,1)S(1)}, bf16[208,768]{1,0:T(8,128)(2,1)S(1)}, bf16[2,2,192,384]{3,2,1,0:T(8,128)(2,1)S(1)}, bf16[2,2,192,384]...) custom-call(s32[3]{0:T(128)S(1)} %pad_add_fusion.refs_0_, ...), custom_call_target="tpu_custom_call" | custom-call | flops 2944401408 | bytes 11929612 | tf_op jit(solution)/shard_map/space_backward/pallas_call | solution.py:330
  188.4 3.5 %collective-permute-done.38 = bf16[52,768]{1,0:T(8,128)(2,1)S(1)} collective-permute-done((bf16[52,768]{1,0:T(8,128)(2,1)S(1)}, bf16[52,768]{1,0:T(8,128)(2,1)S(1)}, u32[]{:S(2)}, u32[]{:S(2)}) %collective-permute-start.38) | collective-permute-done | bytes 79904 | tf_op jit(solution)/shard_map/ppermute | solution.py:361
  196.2 12.2 %time_backward.1 = (bf16[208,768]{1,0:T(8,128)(2,1)S(1)}, bf16[208,768]{1,0:T(8,128)(2,1)S(1)}, bf16[2,2,192,384]{3,2,1,0:T(8,128)(2,1)S(1)}, bf16[2,2,192,384]{...) custom-call(s32[3]{0:T(128)S(1)} %pad_add_fusion.refs_0_, ...), custom_call_target="tpu_custom_call" | custom-call | flops 2944401408 | bytes 8086540 | tf_op jit(solution)/shard_map/time_backward/pallas_call | solution.py:330
  216.3 8.7 %collective-permute-done.44 = bf16[2,2,192,384]{3,2,1,0:T(8,128)(2,1)S(1)} collective-permute-done((bf16[2,2,192,384]{3,2,1,0:T(8,128)(2,1)S(1)}, bf16[2,2,192,384]{3,2,1,0:T(8,128)(2,1)S(1)}, u32[]{:S(2)}, u32[]{:S(2)}) %collective-permute-start.44) | collective-permute-done | bytes 589856 | tf_op jit(solution)/shard_map/ppermute | solution.py:364
  225.0 12.6 %collective-permute-done.51 = bf16[2,384,384]{2,1,0:T(8,128)(2,1)S(1)} collective-permute-done((bf16[2,384,384]{2,1,0:T(8,128)(2,1)S(1)}, bf16[2,384,384]{2,1,0:T(8,128)(2,1)S(1)}, u32[]{:S(2)}, u32[]{:S(2)}) %collective-permute-start.51) | collective-permute-done | bytes 589856 | tf_op jit(solution)/shard_map/ppermute | solution.py:358
  241.3 4.6 %collective-permute-done.54 = f32[3,768]{1,0:T(4,128)S(1)} collective-permute-done((f32[3,768]{1,0:T(4,128)S(1)}, f32[3,768]{1,0:T(4,128)S(1)}, u32[]{:S(2)}, u32[]{:S(2)}) %collective-permute-start.54) | collective-permute-done | bytes 9248 | tf_op jit(solution)/shard_map/ppermute | solution.py:358
  246.8 5.0 %collective-permute-done.53 = bf16[2,384,384]{2,1,0:T(8,128)(2,1)S(1)} collective-permute-done((bf16[2,384,384]{2,1,0:T(8,128)(2,1)S(1)}, bf16[2,384,384]{2,1,0:T(8,128)(2,1)S(1)}, u32[]{:S(2)}, u32[]{:S(2)}) %collective-permute-start.53) | collective-permute-done | bytes 589856 | tf_op jit(solution)/shard_map/ppermute | solution.py:361
  256.8 4.2 %collective-permute-start.61 = (bf16[2,384,384]{2,1,0:T(8,128)(2,1)}, bf16[2,384,384]{2,1,0:T(8,128)(2,1)}, u32[]{:S(2)}, u32[]{:S(2)}) collective-permute-start(bf16[2,384,384]{2,1,0:T(8,128)(2,1)} %maximum_add_fusion), channel_id=1, source_target_pairs={{2,0},{3,1},{4,6},{5,7},{10,8},{11,9},{12,14},{13,15},{18,16},{19,... | collective-permute-start | bytes 1769480 | tf_op jit(solution)/shard_map/ppermute | solution.py:718
  265.4 5.1 %collective-permute-start.59 = (bf16[2,192,384]{2,1,0:T(8,128)(2,1)}, bf16[2,192,384]{2,1,0:T(8,128)(2,1)}, u32[]{:S(2)}, u32[]{:S(2)}) collective-permute-start(bf16[2,192,384]{2,1,0:T(8,128)(2,1)} %maximum_add_fusion.1), channel_id=1, source_target_pairs={{2,0},{3,1},{4,6},{5,7},{10,8},{11,9},{12,14},{13,15},{18,16},{19,... | collective-permute-start | bytes 884744 | tf_op jit(solution)/shard_map/ppermute | solution.py:724
  272.4 4.5 %collective-permute-done.59 = bf16[2,192,384]{2,1,0:T(8,128)(2,1)} collective-permute-done((bf16[2,192,384]{2,1,0:T(8,128)(2,1)}, bf16[2,192,384]{2,1,0:T(8,128)(2,1)}, u32[]{:S(2)}, u32[]{:S(2)}) %collective-permute-start.59) | collective-permute-done | bytes 294944 | tf_op jit(solution)/shard_map/ppermute | solution.py:724
  276.8 10.1 %collective-permute-done.60 = bf16[2,192,384]{2,1,0:T(8,128)(2,1)S(1)} collective-permute-done((bf16[2,192,384]{2,1,0:T(8,128)(2,1)}, bf16[2,192,384]{2,1,0:T(8,128)(2,1)S(1)}, u32[]{:S(2)}, u32[]{:S(2)}) %collective-permute-start.60) | collective-permute-done | bytes 294944 | tf_op jit(solution)/shard_map/ppermute | solution.py:361
  294.6 5.2 %collective-permute-done.68 = bf16[52,768]{1,0:T(8,128)(2,1)S(1)} collective-permute-done((bf16[52,768]{1,0:T(8,128)(2,1)S(1)}, bf16[52,768]{1,0:T(8,128)(2,1)S(1)}, u32[]{:S(2)}, u32[]{:S(2)}) %collective-permute-start.68) | collective-permute-done | bytes 79904 | tf_op jit(solution)/shard_map/ppermute | solution.py:361
  301.7 4.4 %collective-permute-done.70 = bf16[52,768]{1,0:T(8,128)(2,1)S(1)} collective-permute-done((bf16[52,768]{1,0:T(8,128)(2,1)S(1)}, bf16[52,768]{1,0:T(8,128)(2,1)S(1)}, u32[]{:S(2)}, u32[]{:S(2)}) %collective-permute-start.70) | collective-permute-done | bytes 79904 | tf_op jit(solution)/shard_map/ppermute | solution.py:361
  306.1 4.3 %collective-permute-done.65 = bf16[2,192,384]{2,1,0:T(8,128)(2,1)S(1)} collective-permute-done((bf16[2,192,384]{2,1,0:T(8,128)(2,1)S(1)}, bf16[2,192,384]{2,1,0:T(8,128)(2,1)S(1)}, u32[]{:S(2)}, u32[]{:S(2)}) %collective-permute-start.65) | collective-permute-done | bytes 294944 | tf_op jit(solution)/shard_map/ppermute | solution.py:358
  (363 shorter events, 136.5 us)
Async XLA Ops:
  1.9 18.1 %collective-permute-start = (bf16[768,384]{1,0:T(8,128)(2,1)S(1)}, bf16[768,384]{1,0:T(8,128)(2,1)}, u32[]{:S(2)}, u32[]{:S(2)}) collective-permute-start(bf16[768,384]{1,0:T(8,128)(2,1)S(1)} %pad_maximum_fusion.1), channel_id=1, source_target_pairs={{0,2},{1,3},{6,4},{7,5},{8,10},{9,11},{14,12},{15,13},{16,18},{17,... | collective-permute-start | bytes 1769480 | tf_op jit(solution)/shard_map/ppermute | solution.py:407
  23.2 15.3 %collective-permute-start.4 = (bf16[768,384]{1,0:T(8,128)(2,1)S(1)}, bf16[768,384]{1,0:T(8,128)(2,1)S(1)}, u32[]{:S(2)}, u32[]{:S(2)}) collective-permute-start(bf16[768,384]{1,0:T(8,128)(2,1)S(1)} %broadcast_select_fusion.5.refs_5_.refs_9_), channel_id=1, source_target_pairs={{0,1},{1,0},{2,3},{3,2},{4,5},{5,4},{6,7},{7,6},{8,9},{9,8},{10,11... | collective-permute-start | bytes 1769480 | tf_op jit(solution)/shard_map/ppermute | solution.py:361
  38.4 16.9 %collective-permute-start.9 = (bf16[768,384]{1,0:T(8,128)(2,1)S(1)}, bf16[768,384]{1,0:T(8,128)(2,1)}, u32[]{:S(2)}, u32[]{:S(2)}) collective-permute-start(bf16[768,384]{1,0:T(8,128)(2,1)S(1)} %pad_maximum_fusion.2), channel_id=1, source_target_pairs={{0,2},{1,3},{6,4},{7,5},{8,10},{9,11},{14,12},{15,13},{16,18},{17,... | collective-permute-start | bytes 1769480 | tf_op jit(solution)/shard_map/ppermute | solution.py:407
  39.7 18.4 %collective-permute-start.8 = (bf16[768,384]{1,0:T(8,128)(2,1)S(1)}, bf16[768,384]{1,0:T(8,128)(2,1)}, u32[]{:S(2)}, u32[]{:S(2)}) collective-permute-start(bf16[768,384]{1,0:T(8,128)(2,1)S(1)} %collective-permute-done.4.refs_7_.refs_11_), channel_id=1, source_target_pairs={{0,16},{16,0},{1,17},{17,1},{2,18},{18,2},{3,19},{19,3},{4,20},{20... | collective-permute-start | bytes 1769480 | tf_op jit(solution)/shard_map/ppermute | solution.py:364
  44.0 14.1 %collective-permute-start.16 = (bf16[52,768]{1,0:T(8,128)(2,1)}, bf16[52,768]{1,0:T(8,128)(2,1)}, u32[]{:S(2)}, u32[]{:S(2)}) collective-permute-start(bf16[52,768]{1,0:T(8,128)(2,1)} %select_n.497), channel_id=1, source_target_pairs={{0,4},{4,0},{8,12},{12,8},{1,5},{5,1},{9,13},{13,9},{2,6},{6,2},{1... | collective-permute-start | bytes 239624 | tf_op jit(solution)/shard_map/ppermute | solution.py:358
  47.9 16.8 %collective-permute-start.15 = (bf16[52,768]{1,0:T(8,128)(2,1)}, bf16[52,768]{1,0:T(8,128)(2,1)}, u32[]{:S(2)}, u32[]{:S(2)}) collective-permute-start(bf16[52,768]{1,0:T(8,128)(2,1)} %select_n.494), channel_id=1, source_target_pairs={{0,8},{4,12},{8,0},{12,4},{1,9},{5,13},{9,1},{13,5},{2,10},{6,14},... | collective-permute-start | bytes 239624 | tf_op jit(solution)/shard_map/ppermute | solution.py:358
  49.3 19.8 %collective-permute-start.14 = (bf16[52,768]{1,0:T(8,128)(2,1)S(1)}, bf16[52,768]{1,0:T(8,128)(2,1)S(1)}, u32[]{:S(2)}, u32[]{:S(2)}) collective-permute-start(bf16[52,768]{1,0:T(8,128)(2,1)S(1)} %select_n.490), channel_id=1, source_target_pairs={{0,12},{4,8},{8,4},{12,0},{1,13},{5,9},{9,5},{13,1},{2,14},{6,10},... | collective-permute-start | bytes 239624 | tf_op jit(solution)/shard_map/ppermute | solution.py:358
  55.4 15.5 %collective-permute-start.13 = (bf16[768,384]{1,0:T(8,128)(2,1)}, bf16[768,384]{1,0:T(8,128)(2,1)S(1)}, u32[]{:S(2)}, u32[]{:S(2)}) collective-permute-start(bf16[768,384]{1,0:T(8,128)(2,1)} %pad_maximum_fusion.3), channel_id=1, source_target_pairs={{0,2},{1,3},{6,4},{7,5},{8,10},{9,11},{14,12},{15,13},{16,18},{17,... | collective-permute-start | bytes 1769480 | tf_op jit(solution)/shard_map/ppermute | solution.py:407
  58.2 19.6 %collective-permute-start.11 = (bf16[768,384]{1,0:T(8,128)(2,1)S(1)}, bf16[768,384]{1,0:T(8,128)(2,1)S(1)}, u32[]{:S(2)}, u32[]{:S(2)}) collective-permute-start(bf16[768,384]{1,0:T(8,128)(2,1)S(1)} %broadcast_select_fusion.4.refs_5_.refs_17_), channel_id=1, source_target_pairs={{0,1},{1,0},{2,3},{3,2},{4,5},{5,4},{6,7},{7,6},{8,9},{9,8},{10,11... | collective-permute-start | bytes 1769480 | tf_op jit(solution)/shard_map/ppermute | solution.py:361
  105.8 17.3 %collective-permute-start.22 = (bf16[416,768]{1,0:T(8,128)(2,1)S(1)}, bf16[416,768]{1,0:T(8,128)(2,1)S(1)}, u32[]{:S(2)}, u32[]{:S(2)}) collective-permute-start(bf16[416,768]{1,0:T(8,128)(2,1)S(1)} %get-tuple-element.195.refs_3_.refs_9_), channel_id=1, source_target_pairs={{0,4},{4,0},{8,12},{12,8},{1,5},{5,1},{9,13},{13,9},{2,6},{6,2},{1... | collective-permute-start | bytes 1916936 | tf_op jit(solution)/shard_map/ppermute | solution.py:358
  106.2 14.8 %collective-permute-start.25 = (bf16[768,384]{1,0:T(8,128)(2,1)S(1)}, bf16[768,384]{1,0:T(8,128)(2,1)S(1)}, u32[]{:S(2)}, u32[]{:S(2)}) collective-permute-start(bf16[768,384]{1,0:T(8,128)(2,1)S(1)} %broadcast_select_fusion.3.refs_8_), channel_id=1, source_target_pairs={{0,8},{4,12},{8,0},{12,4},{1,9},{5,13},{9,1},{13,5},{2,10},{6,14},... | collective-permute-start | bytes 1769480 | tf_op jit(solution)/shard_map/ppermute | solution.py:358
  107.5 14.5 %collective-permute-start.24 = (bf16[768,384]{1,0:T(8,128)(2,1)S(1)}, bf16[768,384]{1,0:T(8,128)(2,1)S(1)}, u32[]{:S(2)}, u32[]{:S(2)}) collective-permute-start(bf16[768,384]{1,0:T(8,128)(2,1)S(1)} %broadcast_select_fusion.3.refs_8_), channel_id=1, source_target_pairs={{0,16},{16,0},{1,17},{17,1},{2,18},{18,2},{3,19},{19,3},{4,20},{20... | collective-permute-start | bytes 1769480 | tf_op jit(solution)/shard_map/ppermute | solution.py:364
  109.0 14.2 %collective-permute-start.23 = (bf16[768,384]{1,0:T(8,128)(2,1)S(1)}, bf16[768,384]{1,0:T(8,128)(2,1)S(1)}, u32[]{:S(2)}, u32[]{:S(2)}) collective-permute-start(bf16[768,384]{1,0:T(8,128)(2,1)S(1)} %broadcast_select_fusion.3.refs_8_), channel_id=1, source_target_pairs={{0,1},{1,0},{2,3},{3,2},{4,5},{5,4},{6,7},{7,6},{8,9},{9,8},{10,11... | collective-permute-start | bytes 1769480 | tf_op jit(solution)/shard_map/ppermute | solution.py:361
  123.1 15.0 %collective-permute-start.30 = (bf16[768,384]{1,0:T(8,128)(2,1)S(1)}, bf16[768,384]{1,0:T(8,128)(2,1)S(1)}, u32[]{:S(2)}, u32[]{:S(2)}) collective-permute-start(bf16[768,384]{1,0:T(8,128)(2,1)S(1)} %collective-permute-done.23.refs_10_), channel_id=1, source_target_pairs={{0,8},{4,12},{8,0},{12,4},{1,9},{5,13},{9,1},{13,5},{2,10},{6,14},... | collective-permute-start | bytes 1769480 | tf_op jit(solution)/shard_map/ppermute | solution.py:358
  123.3 14.8 %collective-permute-start.29 = (bf16[768,384]{1,0:T(8,128)(2,1)S(1)}, bf16[768,384]{1,0:T(8,128)(2,1)S(1)}, u32[]{:S(2)}, u32[]{:S(2)}) collective-permute-start(bf16[768,384]{1,0:T(8,128)(2,1)S(1)} %collective-permute-done.23.refs_10_), channel_id=1, source_target_pairs={{0,16},{16,0},{1,17},{17,1},{2,18},{18,2},{3,19},{19,3},{4,20},{20... | collective-permute-start | bytes 1769480 | tf_op jit(solution)/shard_map/ppermute | solution.py:364
  136.8 14.9 %collective-permute-start.32 = (bf16[768,384]{1,0:T(8,128)(2,1)S(1)}, bf16[768,384]{1,0:T(8,128)(2,1)S(1)}, u32[]{:S(2)}, u32[]{:S(2)}) collective-permute-start(bf16[768,384]{1,0:T(8,128)(2,1)S(1)} %collective-permute-done.24.refs_9_), channel_id=1, source_target_pairs={{0,8},{4,12},{8,0},{12,4},{1,9},{5,13},{9,1},{13,5},{2,10},{6,14},... | collective-permute-start | bytes 1769480 | tf_op jit(solution)/shard_map/ppermute | solution.py:358
  138.2 14.1 %collective-permute-start.33 = (bf16[768,384]{1,0:T(8,128)(2,1)S(1)}, bf16[768,384]{1,0:T(8,128)(2,1)S(1)}, u32[]{:S(2)}, u32[]{:S(2)}) collective-permute-start(bf16[768,384]{1,0:T(8,128)(2,1)S(1)} %collective-permute-done.30.refs_14_), channel_id=1, source_target_pairs={{0,16},{16,0},{1,17},{17,1},{2,18},{18,2},{3,19},{19,3},{4,20},{20... | collective-permute-start | bytes 1769480 | tf_op jit(solution)/shard_map/ppermute | solution.py:364
  165.4 28.7 %collective-permute-start.39 = (bf16[2,2,384,384]{3,2,1,0:T(8,128)(2,1)S(1)}, bf16[2,2,384,384]{3,2,1,0:T(8,128)(2,1)S(1)}, u32[]{:S(2)}, u32[]{:S(2)}) collective-permute-start(bf16[2,2,384,384]{3,2,1,0:T(8,128)(2,1)S(1)} %get-tuple-element.226), channel_id=1, source_target_pairs={{0,16},{16,0},{1,17},{17,1},{2,18},{18,2},{3,19},{19,3},{4,20},{20... | collective-permute-start | bytes 3538952 | tf_op jit(solution)/shard_map/ppermute | solution.py:364
  166.6 27.5 %collective-permute-start.40 = (bf16[2,2,384,384]{3,2,1,0:T(8,128)(2,1)S(1)}, bf16[2,2,384,384]{3,2,1,0:T(8,128)(2,1)S(1)}, u32[]{:S(2)}, u32[]{:S(2)}) collective-permute-start(bf16[2,2,384,384]{3,2,1,0:T(8,128)(2,1)S(1)} %get-tuple-element.227), channel_id=1, source_target_pairs={{0,8},{4,12},{8,0},{12,4},{1,9},{5,13},{9,1},{13,5},{2,10},{6,14},... | collective-permute-start | bytes 3538952 | tf_op jit(solution)/shard_map/ppermute | solution.py:358
  187.0 21.4 %collective-permute-start.42 = (bf16[2,2,192,384]{3,2,1,0:T(8,128)(2,1)S(1)}, bf16[2,2,192,384]{3,2,1,0:T(8,128)(2,1)S(1)}, u32[]{:S(2)}, u32[]{:S(2)}) collective-permute-start(bf16[2,2,192,384]{3,2,1,0:T(8,128)(2,1)S(1)} %get-tuple-element.239), channel_id=1, source_target_pairs={{0,16},{16,0},{1,17},{17,1},{2,18},{18,2},{3,19},{19,3},{4,20},{20... | collective-permute-start | bytes 1769480 | tf_op jit(solution)/shard_map/ppermute | solution.py:364
  188.0 20.4 %collective-permute-start.43 = (bf16[2,2,192,384]{3,2,1,0:T(8,128)(2,1)S(1)}, bf16[2,2,192,384]{3,2,1,0:T(8,128)(2,1)S(1)}, u32[]{:S(2)}, u32[]{:S(2)}) collective-permute-start(bf16[2,2,192,384]{3,2,1,0:T(8,128)(2,1)S(1)} %get-tuple-element.240), channel_id=1, source_target_pairs={{0,8},{4,12},{8,0},{12,4},{1,9},{5,13},{9,1},{13,5},{2,10},{6,14},... | collective-permute-start | bytes 1769480 | tf_op jit(solution)/shard_map/ppermute | solution.py:358
  210.1 14.9 %collective-permute-start.44 = (bf16[2,2,192,384]{3,2,1,0:T(8,128)(2,1)S(1)}, bf16[2,2,192,384]{3,2,1,0:T(8,128)(2,1)S(1)}, u32[]{:S(2)}, u32[]{:S(2)}) collective-permute-start(bf16[2,2,192,384]{3,2,1,0:T(8,128)(2,1)S(1)} %get-tuple-element.244), channel_id=1, source_target_pairs={{0,16},{16,0},{1,17},{17,1},{2,18},{18,2},{3,19},{19,3},{4,20},{20... | collective-permute-start | bytes 1769480 | tf_op jit(solution)/shard_map/ppermute | solution.py:364
  210.5 14.6 %collective-permute-start.45 = (bf16[2,2,192,384]{3,2,1,0:T(8,128)(2,1)S(1)}, bf16[2,2,192,384]{3,2,1,0:T(8,128)(2,1)S(1)}, u32[]{:S(2)}, u32[]{:S(2)}) collective-permute-start(bf16[2,2,192,384]{3,2,1,0:T(8,128)(2,1)S(1)} %get-tuple-element.245), channel_id=1, source_target_pairs={{0,8},{4,12},{8,0},{12,4},{1,9},{5,13},{9,1},{13,5},{2,10},{6,14},... | collective-permute-start | bytes 1769480 | tf_op jit(solution)/shard_map/ppermute | solution.py:358
  211.6 26.0 %collective-permute-start.51 = (bf16[2,384,384]{2,1,0:T(8,128)(2,1)S(1)}, bf16[2,384,384]{2,1,0:T(8,128)(2,1)S(1)}, u32[]{:S(2)}, u32[]{:S(2)}) collective-permute-start(bf16[2,384,384]{2,1,0:T(8,128)(2,1)S(1)} %slice_bitcast_fusion.3), channel_id=1, source_target_pairs={{0,8},{4,12},{8,0},{12,4},{1,9},{5,13},{9,1},{13,5},{2,10},{6,14},... | collective-permute-start | bytes 1769480 | tf_op jit(solution)/shard_map/ppermute | solution.py:358
  215.1 22.7 %collective-permute-start.52 = (bf16[2,384,384]{2,1,0:T(8,128)(2,1)S(1)}, bf16[2,384,384]{2,1,0:T(8,128)(2,1)S(1)}, u32[]{:S(2)}, u32[]{:S(2)}) collective-permute-start(bf16[2,384,384]{2,1,0:T(8,128)(2,1)S(1)} %slice_bitcast_fusion.2), channel_id=1, source_target_pairs={{0,16},{16,0},{1,17},{17,1},{2,18},{18,2},{3,19},{19,3},{4,20},{20... | collective-permute-start | bytes 1769480 | tf_op jit(solution)/shard_map/ppermute | solution.py:364
  256.8 30.9 %collective-permute-start.61 = (bf16[2,384,384]{2,1,0:T(8,128)(2,1)}, bf16[2,384,384]{2,1,0:T(8,128)(2,1)}, u32[]{:S(2)}, u32[]{:S(2)}) collective-permute-start(bf16[2,384,384]{2,1,0:T(8,128)(2,1)} %maximum_add_fusion), channel_id=1, source_target_pairs={{2,0},{3,1},{4,6},{5,7},{10,8},{11,9},{12,14},{13,15},{18,16},{19,... | collective-permute-start | bytes 1769480 | tf_op jit(solution)/shard_map/ppermute | solution.py:718
  271.2 15.7 %collective-permute-start.60 = (bf16[2,192,384]{2,1,0:T(8,128)(2,1)}, bf16[2,192,384]{2,1,0:T(8,128)(2,1)S(1)}, u32[]{:S(2)}, u32[]{:S(2)}) collective-permute-start(bf16[2,192,384]{2,1,0:T(8,128)(2,1)} %pad_maximum_fusion.12), channel_id=1, source_target_pairs={{0,1},{1,0},{2,3},{3,2},{4,5},{5,4},{6,7},{7,6},{8,9},{9,8},{10,11... | collective-permute-start | bytes 884744 | tf_op jit(solution)/shard_map/ppermute | solution.py:361
  289.0 22.2 %collective-permute-start.66 = (bf16[2,384,384]{2,1,0:T(8,128)(2,1)S(1)}, bf16[2,384,384]{2,1,0:T(8,128)(2,1)S(1)}, u32[]{:S(2)}, u32[]{:S(2)}) collective-permute-start(bf16[2,384,384]{2,1,0:T(8,128)(2,1)S(1)} %fusion.20), channel_id=1, source_target_pairs={{0,8},{4,12},{8,0},{12,4},{1,9},{5,13},{9,1},{13,5},{2,10},{6,14},... | collective-permute-start | bytes 1769480 | tf_op jit(solution)/shard_map/ppermute | solution.py:358
  290.9 15.1 %collective-permute-start.67 = (bf16[2,192,384]{2,1,0:T(8,128)(2,1)}, bf16[2,192,384]{2,1,0:T(8,128)(2,1)}, u32[]{:S(2)}, u32[]{:S(2)}) collective-permute-start(bf16[2,192,384]{2,1,0:T(8,128)(2,1)} %maximum_add_fusion.2), channel_id=1, source_target_pairs={{2,0},{3,1},{4,6},{5,7},{10,8},{11,9},{12,14},{13,15},{18,16},{19,... | collective-permute-start | bytes 884744 | tf_op jit(solution)/shard_map/ppermute | solution.py:734
  293.2 17.2 %collective-permute-start.65 = (bf16[2,192,384]{2,1,0:T(8,128)(2,1)S(1)}, bf16[2,192,384]{2,1,0:T(8,128)(2,1)S(1)}, u32[]{:S(2)}, u32[]{:S(2)}) collective-permute-start(bf16[2,192,384]{2,1,0:T(8,128)(2,1)S(1)} %fusion.21), channel_id=1, source_target_pairs={{0,8},{4,12},{8,0},{12,4},{1,9},{5,13},{9,1},{13,5},{2,10},{6,14},... | collective-permute-start | bytes 884744 | tf_op jit(solution)/shard_map/ppermute | solution.py:358
  314.5 17.0 %collective-permute-start.77 = (bf16[2,192,384]{2,1,0:T(8,128)(2,1)S(1)}, bf16[2,192,384]{2,1,0:T(8,128)(2,1)}, u32[]{:S(2)}, u32[]{:S(2)}) collective-permute-start(bf16[2,192,384]{2,1,0:T(8,128)(2,1)S(1)} %fusion.19), channel_id=1, source_target_pairs={{0,8},{4,12},{8,0},{12,4},{1,9},{5,13},{9,1},{13,5},{2,10},{6,14},... | collective-permute-start | bytes 884744 | tf_op jit(solution)/shard_map/ppermute | solution.py:358
  321.8 16.1 %collective-permute-start.79 = (bf16[2,2,384,384]{3,2,1,0:T(8,128)(2,1)S(1)}, bf16[2,2,384,384]{3,2,1,0:T(8,128)(2,1)}, u32[]{:S(2)}, u32[]{:S(2)}) collective-permute-start(bf16[2,2,384,384]{3,2,1,0:T(8,128)(2,1)S(1)} %pad_maximum_fusion), channel_id=1, source_target_pairs={{0,4},{4,0},{8,12},{12,8},{1,5},{5,1},{9,13},{13,9},{2,6},{6,2},{1... | collective-permute-start | bytes 3538952 | tf_op jit(solution)/shard_map/ppermute | solution.py:358
  (99 other events, 778.2 us)

commit v3 on v2

v3 whole, which is shorter than its diff:
```python
import functools

import jax
import jax.numpy as jnp
from jax import lax
from jax.experimental import pallas as pl
from jax.experimental.pallas import tpu as pltpu
from jax.sharding import PartitionSpec as P

HEAD_DIM = 64
EPSILON = 1e-06
SCALE = HEAD_DIM ** (-0.5)
F32 = jnp.float32
LOW = jnp.bfloat16
VMEM = pltpu.VMEM


def dot(a, b, ca, cb):
    return lax.dot_general(a, b, (((ca,), (cb,)), ((), ())), preferred_element_type=F32)


def statistics(rows):
    center = rows - jnp.mean(rows, axis=-1, keepdims=True)
    rate = lax.rsqrt(jnp.mean(center * center, axis=-1, keepdims=True) + EPSILON)
    return center * rate, rate


def norm_back(grad, gain, hat, rate):
    t = grad * gain
    return rate * (
        t
        - jnp.mean(t, axis=-1, keepdims=True)
        - hat * jnp.mean(t * hat, axis=-1, keepdims=True)
    )


def to_blocks(own, pair, frames_cut):
    if not frames_cut:
        return jnp.concatenate((own, pair), axis=0)
    n = own.shape[0] // 8
    return jnp.concatenate(
        [
            rows[(2 * d + f) * n : (2 * d + f + 1) * n]
            for f in range(2)
            for rows in (own, pair)
            for d in range(4)
        ],
        axis=0,
    )


def from_blocks(rows, frames_cut):
    half = rows.shape[0] // 2
    if not frames_cut:
        return rows[:half], rows[half:]
    n = half // 8
    return tuple(
        jnp.concatenate(
            [
                rows[f * half + (4 * side + d) * n : f * half + (4 * side + d + 1) * n]
                for d in range(4)
                for f in range(2)
            ],
            axis=0,
        )
        for side in range(2)
    )


def split_store(chip, refs, piece, group, units):
    send_x, keep_x, send_y, keep_y = refs
    to_x = keep_x if piece == 0 else send_x
    to_x[0, group] = jnp.where(chip == 0, units[0], units[1])
    to_x[1, group] = jnp.where(chip == 0, units[1], units[0])
    keep_y[piece, group] = jnp.where(chip == 0, units[2], units[3])
    send_y[piece, group] = jnp.where(chip == 0, units[3], units[2])


def columns(off_ref, piece, width):
    return pl.ds(pl.multiple_of(off_ref[piece], 128), width)


def store_partial(total, outs, frames_cut):
    n, halves = total.shape[0], len(outs) - 1
    first, second = from_blocks(total[: n // halves, :], frames_cut)
    outs[0][...] = first.astype(LOW)
    if halves == 1:
        outs[1][...] = second.astype(LOW)
        return
    half = n // 4
    outs[2][:half, :] = second.astype(LOW)
    first, second = from_blocks(total[n // 2 :, :], frames_cut)
    outs[1][...] = first.astype(LOW)
    outs[2][half:, :] = second.astype(LOW)


def attend_forward_kernel(pieces, halves, groups, frames_cut, *refs):
    off = refs[0]
    rows_in = refs[1 : 1 + 2 * halves]
    rest = list(refs[1 + 2 * halves :])
    gain, bias = rest.pop(0), rest.pop(0)
    weights = [[rest.pop(0) for _ in range(pieces)] for _ in range(groups)]
    parts_out = [rest.pop(0) for _ in range(1 + halves)]
    saved_at = [rest.pop(0) for _ in range(1 + 2 * groups)]
    kept_at = [rest.pop(0) for _ in range(groups * pieces)]
    normed = rest.pop(0)
    joined, out = [rest.pop(0) for _ in range(groups)], [rest.pop(0) for _ in range(groups)]
    total, sems = rest
    copies = []

    def leave(source, target):
        copy = pltpu.make_async_copy(source, target, sems.at[len(copies)])
        copy.start()
        copies.append(copy)

    for g in range(groups):
        for p in range(pieces):
            leave(weights[g][p], kept_at[g * pieces + p])
    two = normed.shape[0] // halves
    for h in range(halves):
        rows = to_blocks(
            rows_in[2 * h][...].astype(F32), rows_in[2 * h + 1][...].astype(F32), frames_cut
        )
        hat, _ = statistics(rows)
        normed[h * two : (h + 1) * two, :] = (hat * gain[...]).astype(LOW)
    leave(normed, saved_at[0])
    width = weights[0][0].shape[1]
    heads3 = joined[0].shape[1]
    for g in range(groups):
        acc = None
        for p in range(pieces):
            term = dot(normed[:, columns(off, p, width)], weights[g][p][:heads3, :], 1, 1)
            acc = term if acc is None else acc + term
        joined[g][...] = acc.astype(LOW)
        leave(joined[g], saved_at[1 + g])
    block = two // 2
    inner = heads3 // 3

    def one_block(b, carry):
        at = pl.ds(pl.multiple_of(b * block, 16), block)
        for g in range(groups):
            rows3 = joined[g][at, :]
            parts = []
            for h in range(inner // HEAD_DIM):
                lo = h * HEAD_DIM
                q = rows3[:, lo : lo + HEAD_DIM]
                k = rows3[:, inner + lo : inner + lo + HEAD_DIM]
                v = rows3[:, 2 * inner + lo : 2 * inner + lo + HEAD_DIM]
                s = dot(q, k, 1, 1) * SCALE + bias[...]
                e = jnp.exp(s - jnp.max(s, axis=-1, keepdims=True))
                w = (e / jnp.sum(e, axis=-1, keepdims=True)).astype(LOW)
                parts.append(dot(w, v, 1, 0))
            out[g][at, :] = jnp.concatenate(parts, axis=1).astype(LOW)
        return carry

    lax.fori_loop(0, 2 * halves, one_block, 0)
    for g in range(groups):
        leave(out[g], saved_at[1 + groups + g])
    for p in range(pieces):
        acc = dot(out[0][...], weights[0][p][heads3:, :], 1, 0)
        for g in range(1, groups):
            acc = acc + dot(out[g][...], weights[g][p][heads3:, :], 1, 0)
        total[:, columns(off, p, width)] = acc
    store_partial(total, parts_out, frames_cut)
    for copy in copies:
        copy.wait()


def attend_backward_kernel(pieces, halves, groups, frames_cut, *refs):
    off, bias, normed = refs[:3]
    rest = list(refs[3:])
    joined, out = [rest.pop(0) for _ in range(groups)], [rest.pop(0) for _ in range(groups)]
    n_head = 9 if frames_cut else 2 * halves
    head = [rest.pop(0) for _ in range(n_head)]
    weights = [[rest.pop(0) for _ in range(pieces)] for _ in range(groups)]
    parts_out = [rest.pop(0) for _ in range(1 + halves)]
    grads = [rest.pop(0) for _ in range(4 if pieces == 2 else 1)]
    if frames_cut:
        carried, gain_grad = rest.pop(0), rest.pop(0)
    upstream = rest.pop(0)
    djoined, dout = [rest.pop(0) for _ in range(groups)], [rest.pop(0) for _ in range(groups)]
    total = rest.pop(0)
    two = upstream.shape[0] // halves
    half = two // 2
    if frames_cut:
        base_own, base_pair, grad_l, grad_r, far_own, far_pair, gain, cot_own, cot_pair = head
        both = []
        for lo, base, far_sum, cot in (
            (0, base_own, far_own, cot_own),
            (half, base_pair, far_pair, cot_pair),
        ):
            at = slice(lo, lo + half)
            far = slice(half - lo, 2 * half - lo)
            hat, rate = statistics(base[...].astype(F32))
            dn = grad_l[at, :].astype(F32) + grad_r[far, :].astype(F32) + far_sum[...].astype(F32)
            dx = cot[...].astype(F32) + norm_back(dn, gain[...], hat, rate)
            if lo == 0:
                carried[...] = dx
                gain_grad[...] = jnp.sum(dn * hat, axis=0, keepdims=True)
            both.append(dx)
        upstream[...] = to_blocks(both[0], both[1], frames_cut).astype(LOW)
    else:
        for r in range(2 * halves):
            upstream[r * half : (r + 1) * half, :] = head[r][...]
    width = weights[0][0].shape[1]
    heads3 = joined[0].shape[1]
    inner = heads3 // 3
    for g in range(groups):
        acc = None
        for p in range(pieces):
            term = dot(upstream[:, columns(off, p, width)], weights[g][p][heads3:, :], 1, 1)
            acc = term if acc is None else acc + term
        dout[g][...] = acc.astype(LOW)

    def one_block(b, carry):
        at = pl.ds(pl.multiple_of(b * half, 16), half)
        for g in range(groups):
            rows3 = joined[g][at, :]
            do3 = dout[g][at, :]
            dqs, dks, dvs = [], [], []
            for h in range(inner // HEAD_DIM):
                lo = h * HEAD_DIM
                q = rows3[:, lo : lo + HEAD_DIM]
                k = rows3[:, inner + lo : inner + lo + HEAD_DIM]
                v = rows3[:, 2 * inner + lo : 2 * inner + lo + HEAD_DIM]
                do = do3[:, lo : lo + HEAD_DIM]
                s = dot(q, k, 1, 1) * SCALE + bias[...]
                e = jnp.exp(s - jnp.max(s, axis=-1, keepdims=True))
                w = e / jnp.sum(e, axis=-1, keepdims=True)
                dw = dot(do, v, 1, 1)
                ds = (w * (dw - jnp.sum(w * dw, axis=-1, keepdims=True))).astype(LOW)
                dqs.append(dot(ds, k, 1, 0) * SCALE)
                dks.append(dot(ds, q, 0, 0) * SCALE)
                dvs.append(dot(w.astype(LOW), do, 0, 0))
            djoined[g][at, :] = jnp.concatenate(dqs + dks + dvs, axis=1).astype(LOW)
        return carry

    lax.fori_loop(0, 2 * halves, one_block, 0)
    chip = off[pieces]
    for p in range(pieces):
        cols = columns(off, p, width)
        wide = normed[:, cols]
        dy = upstream[:, cols]
        acc = None
        for g in range(groups):
            value = dot(djoined[g][...], wide, 0, 0).astype(LOW)
            proj = dot(out[g][...], dy, 0, 0).astype(LOW)
            if pieces == 2:
                units = [value[u * inner : (u + 1) * inner] for u in range(3)] + [proj]
                split_store(chip, grads, p, g, units)
            else:
                grads[0][g, :heads3] = value
                grads[0][g, heads3:] = proj
            term = dot(djoined[g][...], weights[g][p][:heads3, :], 1, 0)
            acc = term if acc is None else acc + term
        total[:, cols] = acc
    store_partial(total, parts_out, frames_cut)


def feed_kernel(pieces, packed, *refs):
    off, gain = refs[:2]
    rows_in, cots = refs[2:6], refs[6:10]
    at = 10
    n_w = 2 * pieces * (1 if packed else 2)
    weights = refs[at : at + n_w]
    at += n_w
    out_own, out_send, out_far, dn_near, dn_send, dn_far = refs[at : at + 6]
    at += 6
    n_g = 4 if packed else 2
    grads = refs[at : at + n_g]
    normed, cot, total, dtotal = refs[at + n_g :]
    n = rows_in[0].shape[0]
    for r in range(4):
        rows_at = slice(r * n, (r + 1) * n)
        hat, _ = statistics(rows_in[r][...].astype(F32))
        normed[rows_at, :] = (hat * gain[...]).astype(LOW)
        cot[rows_at, :] = cots[r][...]
    for c in range(2):
        ups, downs = [], []
        for p in range(pieces):
            if packed:
                w = weights[c * pieces + p]
                wide = w.shape[0] // 2
                ups.append(w[:wide, :])
                downs.append(w[wide:, :])
            else:
                ups.append(weights[2 * (c * pieces + p)][...])
                downs.append(weights[2 * (c * pieces + p) + 1][...])
        width = ups[0].shape[0]
        hidden = dact = None
        for p in range(pieces):
            cols = columns(off, p, width)
            term = dot(normed[:, cols], ups[p], 1, 0)
            dterm = dot(cot[:, cols], downs[p], 1, 1)
            hidden = term if hidden is None else hidden + term
            dact = dterm if dact is None else dact + dterm
        cdf = 0.5 * (1.0 + lax.erf(hidden * (2.0**-0.5)))
        act = (hidden * cdf).astype(LOW)
        slope = cdf + hidden * (jnp.exp(-0.5 * hidden * hidden) * (2.0 * jnp.pi) ** -0.5)
        dhid = (dact * slope).astype(LOW)
        for p in range(pieces):
            cols = columns(off, p, width)
            term = dot(act, downs[p], 1, 0)
            dterm = dot(dhid, ups[p], 1, 1)
            if c == 0:
                total[:, cols] = term
                dtotal[:, cols] = dterm
            else:
                total[:, cols] += term
                dtotal[:, cols] += dterm
            up_grad = dot(normed[:, cols], dhid, 0, 0).astype(LOW)
            down_grad = dot(act, cot[:, cols], 0, 0).astype(LOW)
            if packed:
                grads[2 * p + c][:width, :] = up_grad
                grads[2 * p + c][width:, :] = down_grad
            else:
                grads[0][c] = up_grad
                grads[1][c] = down_grad
    out_own[...] = rows_in[0][...].astype(F32) + total[:n, :]
    out_send[:n, :] = total[n : 2 * n, :].astype(LOW)
    out_send[n:, :] = total[3 * n :, :].astype(LOW)
    out_far[...] = total[2 * n : 3 * n, :].astype(LOW)
    dn_near[...] = dtotal[: 2 * n, :].astype(LOW)
    dn_far[...] = dtotal[2 * n : 3 * n, :].astype(LOW)
    dn_send[...] = dtotal[3 * n :, :].astype(LOW)


def store_parts(rows, outs):
    n = rows.shape[0] // len(outs)
    for d, out in enumerate(outs):
        out[...] = rows[d * n : (d + 1) * n].astype(out.dtype)


def norm_back_kernel(n, firsts, *refs):
    base, gain, carried = refs[n : n + 3]
    outs = refs[n + 3 :]
    rows = base.shape[0]
    hat, rate = statistics(base[...].astype(F32))
    dn = refs[n - 1][firsts[n - 1] : firsts[n - 1] + rows, :].astype(F32)
    for k in range(n - 2, -1, -1):
        dn = refs[k][firsts[k] : firsts[k] + rows, :].astype(F32) + dn
    store_parts(carried[...].astype(F32) + norm_back(dn, gain[...], hat, rate), outs[:-1])
    outs[-1][...] = jnp.sum(dn * hat, axis=0, keepdims=True)


def sum_kernel(n, firsts, *refs):
    outs = refs[n:]
    rows = outs[0].shape[0] * len(outs)
    total = refs[n - 1][firsts[n - 1] : firsts[n - 1] + rows, :].astype(F32)
    for k in range(n - 2, -1, -1):
        total = refs[k][firsts[k] : firsts[k] + rows, :].astype(F32) + total
    store_parts(total, outs)


def in_vmem(n):
    return [pl.BlockSpec(memory_space=VMEM)] * n


def shape_of(shape, dtype):
    return jax.ShapeDtypeStruct(shape, dtype)


def run(kernel, operands, outs, scratch, flops, name, vmem=12, anywhere=0):
    moved = sum(o.size * o.dtype.itemsize for o in operands) + sum(
        o.size * o.dtype.itemsize for o in outs
    )
    scalar = operands[0].dtype == jnp.int32
    specs = in_vmem(len(operands))
    if scalar:
        specs[0] = pl.BlockSpec(memory_space=pltpu.SMEM)
    return pl.pallas_call(
        kernel,
        out_shape=outs,
        in_specs=specs,
        out_specs=in_vmem(len(outs) - anywhere)
        + [pl.BlockSpec(memory_space=pl.ANY)] * anywhere,
        scratch_shapes=scratch,
        compiler_params=pltpu.CompilerParams(vmem_limit_bytes=vmem << 20),
        cost_estimate=pl.CostEstimate(flops=flops, bytes_accessed=moved, transcendentals=0),
        name=name,
    )(*operands)


def after(value, *tokens):
    return lax.optimization_barrier((value, *tokens))[0]


def body(sizes, tokens, norm_gains, temporal_qkv, temporal_proj, spatial_qkv, spatial_proj, up_weight, down_weight, cotangent):
    n_fsdp, n_ctx, n_tp = sizes
    swap = n_fsdp == 2
    d_model = tokens.shape[3]
    d_part = d_model // n_fsdp
    places = tokens.shape[0]
    block = 2 * (-(-places // 4))
    x, i, z = lax.axis_index("fsdp"), lax.axis_index("ctx"), lax.axis_index("tp")
    core, chip = i % 2, i // 2
    is_source = (z // 2) == core

    def permute_ctx(v, bits):
        return lax.ppermute(v, "ctx", [(a, a ^ bits) for a in range(n_ctx)])

    def permute_tp(v, bits):
        return lax.ppermute(v, "tp", [(a, a ^ bits) for a in range(n_tp)])

    def permute_fsdp(v):
        return lax.ppermute(v, "fsdp", [(0, 1), (1, 0)])

    def along(v, bits, back=False):
        pairs = []
        for a in range(n_ctx):
            for b in (2 * (a % 2), 2 * (a % 2) + 1):
                there, here = a * n_tp + (b ^ bits), a * n_tp + b
                pairs.append((there, here) if back else (here, there))
        return lax.ppermute(v, ("ctx", "tp"), pairs)

    def exclusive(parts, bits):
        low, high = (bits & 1) == 1, (bits & 2) == 2
        parts = [jnp.where(low, parts[d ^ 1], parts[d]) for d in range(4)]
        return [jnp.where(high, parts[d ^ 2], parts[d]) for d in range(4)]

    slot_bits = (z & 2) | ((z & 1) ^ core)
    part_rows = 2 * block

    def to_time(rows):
        t = jnp.transpose(rows, (2, 1, 0, 3))
        t = jnp.pad(t, ((0, 0), (0, 0), (0, 2 * block - places), (0, 0)))
        parts = [t[c, :, b * block : (b + 1) * block] for c in range(2) for b in range(2)]
        parts = exclusive([v.reshape(part_rows, d_model) for v in parts], i)
        got = [parts[0]] + [permute_ctx(parts[e], e) for e in range(1, 4)]
        return exclusive(got, slot_bits)

    def time_sends(own):
        parts = exclusive(own, slot_bits)
        return [parts[0]] + [permute_ctx(parts[e], e) for e in range(1, 4)]

    def time_finish(got):
        got = [v.reshape(2, block, d_model) for v in exclusive(got, i)]
        t = jnp.stack(
            [jnp.concatenate((got[2 * c], got[2 * c + 1]), axis=1)[:, :places] for c in range(2)]
        )
        return jnp.transpose(t, (2, 1, 0, 3))

    def turn(own):
        return [own[0]] + [permute_tp(own[e], e) for e in range(1, 4)]

    rows_n = 8 * block
    flat = (rows_n, d_model)

    def attention_pack(qkv, proj):
        return jnp.concatenate((jnp.transpose(qkv, (1, 2, 0)).reshape(-1, d_part), proj), axis=0)

    def spread_first(shard):
        return jnp.where(is_source, shard, along(shard, 2))

    hid_half = up_weight.shape[1] // 2

    def feed_pack():
        up = lax.dynamic_slice_in_dim(up_weight, chip * hid_half, hid_half, axis=1)
        down = lax.dynamic_slice_in_dim(down_weight, chip * hid_half, hid_half, axis=0)
        return jnp.concatenate((up, down.reshape(d_part, hid_half)), axis=0)

    def feed_full(shard):
        every = lax.all_gather(shard, "fsdp", axis=0)
        up = every[:, :d_part].reshape(d_model, hid_half)
        down = every[:, d_part:].reshape(n_fsdp, hid_half, d_part)
        return [up, jnp.transpose(down, (1, 0, 2)).reshape(hid_half, d_model)]

    def owner_sum(a, b):
        mine = a + permute_tp(b, 1)
        return mine + along(mine, 2, True)

    def owner_sends(a, b):
        return along(a, 2, True), along(b, 3, True), along(b, 1)

    def ordered(mine, other):
        return jnp.stack((jnp.where(chip == 0, mine, other), jnp.where(chip == 0, other, mine)))

    def to_pair(both):
        return jnp.where(is_source, both, permute_ctx(both, 1))

    def to_both(mine):
        return to_pair(ordered(mine, permute_ctx(mine, 2)))

    def first_sends(grads):
        send_x, _, send_y, _ = grads
        return permute_fsdp(send_x), permute_ctx(send_y, 2)

    def first_sums(grads, got):
        _, keep_x, _, keep_y = grads
        by_x, by_y = keep_x + got[0], keep_y + got[1]
        return (by_x[0], by_y[0]), (by_x[1], by_y[1])

    def second_sends(send):
        return permute_ctx(send[0], 2), permute_fsdp(send[1])

    def second_sums(keep, got):
        by_x, by_y = keep[0] + got[0], keep[1] + got[1]
        return [jnp.stack((by_x[g], by_y[g])) for g in range(by_x.shape[0])]

    def attention_out(total):
        joined_grad = jnp.stack((total[0, 0], total[1, 0], total[0, 1])).astype(F32)
        return jnp.transpose(joined_grad, (2, 0, 1)), total[1, 1].astype(F32)

    def feed_out(total):
        up = jnp.concatenate((total[0, :d_part], total[1, :d_part]), axis=1)
        down = jnp.concatenate((total[0, d_part:], total[1, d_part:]), axis=0)
        return up.astype(F32), down.astype(F32)

    def attention_grads_wide(grads):
        total = lax.psum_scatter(grads[0], "fsdp", scatter_dimension=2, tiled=True)
        total = total + permute_ctx(total, 2)
        if total.shape[0] == 2:
            mine = owner_sum(total[0], total[1])
        else:
            mine = total[0] + along(total[0], 2, True)
        full = jnp.where(is_source, mine, permute_ctx(mine, 1)).astype(F32)
        inner = full.shape[0] // 4
        joined_grad = full[: 3 * inner].reshape(3, inner, d_part)
        return jnp.transpose(joined_grad, (2, 0, 1)), full[3 * inner :]

    def feed_grads_wide(grads):
        up = lax.psum_scatter(grads[0], "fsdp", scatter_dimension=1, tiled=True)
        down = lax.psum_scatter(grads[1], "fsdp", scatter_dimension=2, tiled=True)
        up = to_both(owner_sum(up[0], up[1]))
        down = to_both(owner_sum(down[0], down[1]))
        return (
            jnp.concatenate((up[0], up[1]), axis=1).astype(F32),
            jnp.concatenate((down[0], down[1]), axis=0).astype(F32),
        )

    pieces = 2 if swap else 1
    width = d_model // pieces
    if swap:
        offsets = jnp.stack((x * width, (1 - x) * width, chip)).astype(jnp.int32)
    else:
        offsets = jnp.stack((0 * chip, chip)).astype(jnp.int32)

    at = jnp.arange(rows_n, dtype=jnp.int32)
    far = jnp.float32(-1e30)
    bias_t = jnp.where((at % block)[:, None] == (at % block)[None, :], 0.0, far).astype(F32)
    owner = jnp.where(at < rows_n // 2, core, 1 - core)
    real = owner * block + at % block < places
    bias_s = jnp.broadcast_to(jnp.where(real, 0.0, far).astype(F32)[None], (rows_n, rows_n))

    two = (2 * rows_n, d_model)
    unit = 2 * rows_n * d_model * d_model

    inner = temporal_qkv.shape[2]

    def shapes(rows, groups):
        all_rows = len(rows) * rows_n
        return (all_rows, d_model), [(all_rows, 3 * inner)] * groups, [(all_rows, inner)] * groups

    def part_shapes(rows):
        if len(rows) == 2:
            return [shape_of(flat, LOW)] * 2
        return [shape_of(flat, LOW)] * 2 + [shape_of(two, LOW)]

    def attend_forward(rows, gain, bias, weights, cut, name):
        groups = len(weights) // pieces
        wide, joined, heads = shapes(rows, groups)
        kept = [shape_of(s, LOW) for s in (wide, *joined, *heads)]
        kept += [shape_of(w.shape, LOW) for w in weights]
        outs = part_shapes(rows) + kept
        got = run(
            functools.partial(attend_forward_kernel, pieces, len(rows) // 2, groups, cut),
            [offsets, *rows, gain, bias, *weights],
            outs,
            [VMEM(s, LOW) for s in (wide, *joined, *heads)]
            + [VMEM(wide, F32), pltpu.SemaphoreType.DMA((len(kept),))],
            6 * unit,
            name,
            16,
            len(kept),
        )
        n = len(part_shapes(rows))
        m = n + 1 + 2 * groups
        return got[:n], got[n:m], got[m:]

    def attend_backward(rows, saved, bias, head, weights, cut, name):
        groups = len(weights) // pieces
        wide, joined, heads = shapes(rows, groups)
        outs = part_shapes(rows)
        n = len(outs)
        if swap:
            outs += [shape_of((2, groups, inner, width), LOW)] * 4
        else:
            outs += [shape_of((groups, 4 * inner, width), LOW)]
        m = len(outs)
        if cut:
            outs += [shape_of(flat, F32), shape_of((1, d_model), F32)]
        got = run(
            functools.partial(attend_backward_kernel, pieces, len(rows) // 2, groups, cut),
            [offsets, bias, *saved, *head, *weights],
            outs,
            [VMEM(s, LOW) for s in (wide, *joined, *heads)] + [VMEM(wide, F32)],
            12 * unit,
            name,
        )
        return got[:n], got[n:m], got[m:]

    def norm_backward(terms, base, gain, carried, name):
        *parts, gain_grad = run(
            functools.partial(norm_back_kernel, len(terms), [lo for _, lo in terms]),
            [v for v, _ in terms] + [base, gain, carried],
            [shape_of((part_rows, d_model), LOW)] * 4 + [shape_of((1, d_model), F32)],
            [],
            20 * rows_n * d_model,
            name,
        )
        return parts, gain_grad

    def sum_parts(terms, name, n=4):
        return run(
            functools.partial(sum_kernel, len(terms), [lo for _, lo in terms]),
            [v for v, _ in terms],
            [shape_of((rows_n // n, d_model), LOW)] * n,
            [],
            4 * rows_n * d_model,
            name,
        )

    def other_x(v):
        return permute_fsdp(v) if swap else lax.all_gather(v, "fsdp", axis=1, tiled=True)

    def joined_pieces(first, first_x, second, second_x):
        return [first, first_x, second, second_x] if swap else [first_x, second_x]

    barrier = lax.optimization_barrier

    pack_t = attention_pack(temporal_qkv, temporal_proj)
    got_first_t = along(pack_t, 2)
    pack_s = attention_pack(spatial_qkv, spatial_proj)
    pack_f = feed_pack()
    if swap:
        gain_other = permute_fsdp(norm_gains)
        gains = jnp.where(
            x == 0,
            jnp.concatenate((norm_gains, gain_other), axis=1),
            jnp.concatenate((gain_other, norm_gains), axis=1),
        ).astype(F32)
    else:
        gains = lax.all_gather(norm_gains, "fsdp", axis=1, tiled=True).astype(F32)
    start = jnp.concatenate(to_time(tokens), axis=0)
    got_first_t, start, pack_s, pack_f, gains, cot = barrier(
        (got_first_t, start, pack_s, pack_f, gains, cotangent)
    )
    first_t = jnp.where(is_source, pack_t, got_first_t)
    first_tx = other_x(first_t)
    weights_t = [first_t, first_tx] if swap else [first_tx]
    near_start = permute_tp(start, 1)
    rows_t = [start, permute_ctx(start, 1), near_start, permute_ctx(near_start, 1)]
    got_first_s = along(pack_s, 2)
    cot_time = jnp.concatenate(to_time(cot), axis=0)
    first_tx, rows_t, got_first_s, cot_time = barrier((first_tx, rows_t, got_first_s, cot_time))
    first_s = jnp.where(is_source, pack_s, got_first_s)
    weights_t = [first_t, first_tx] if swap else [first_tx]

    second_s = permute_tp(first_s, 1)
    first_sx = other_x(first_s)
    parts_t, saved_t, weights_t = attend_forward(
        rows_t, gains[0:1], bias_t, weights_t, False, "time_forward"
    )
    parts_t, second_s, first_sx, pack_f, cot_time = barrier(
        (parts_t, second_s, first_sx, pack_f, cot_time)
    )
    got_t = permute_ctx(parts_t[2], 1)
    (chip_t,) = sum_parts(((parts_t[1], 0), (got_t, rows_n)), "time_near", 1)
    near_t = permute_tp(chip_t, 1)
    far_cot_time = permute_ctx(after(cot_time, chip_t), 2)
    got_first_f = along(after(pack_f, chip_t), 2)
    second_sx = other_x(second_s)
    sums = sum_parts(((start, 0), (parts_t[0], 0), (got_t, 0), (near_t, 0)), "time_sum")
    sums, far_cot_time, got_first_f = barrier((sums, far_cot_time, got_first_f))
    own1 = jnp.concatenate(turn(sums), axis=0)
    own1, second_sx = barrier((own1, second_sx))
    pair1 = permute_ctx(own1, 1)
    first_f = jnp.where(is_source, pack_f, got_first_f)
    pair1, first_f = barrier((pair1, first_f))
    weights_s = joined_pieces(first_s, first_sx, second_s, second_sx)

    second_f = permute_tp(first_f, 1)
    if swap:
        first_fx = permute_fsdp(first_f)
    parts_s, saved_s, weights_s = attend_forward(
        [own1, pair1], gains[1:2], bias_s, weights_s, True, "space_forward"
    )
    back_s = permute_ctx(parts_s[1], 1)
    (own2,) = sum_parts(((own1, 0), (parts_s[0], 0), (back_s, 0)), "space_sum", 1)
    if swap:
        second_f, first_fx, own2 = barrier((second_f, first_fx, own2))
        second_fx = permute_fsdp(second_f)
        weights_f = [first_f, first_fx, second_f, second_fx]
    else:
        weights_f = [w for v in (first_f, second_f) for w in feed_full(v)]
    far_own2 = permute_ctx(own2, 2)
    rows_f = [own2, permute_ctx(own2, 1), far_own2, permute_ctx(far_own2, 1)]

    both_cot = []
    for d in range(4):
        at_d = slice(d * part_rows, (d + 1) * part_rows)
        both_cot.append(jnp.concatenate((cot_time[at_d], far_cot_time[at_d]), axis=0))
    both_cot = turn(after(both_cot, own2))
    if swap:
        both_cot, second_fx = barrier((both_cot, second_fx))
        weights_f = [first_f, first_fx, second_f, second_fx]
    cot_own = jnp.concatenate([v[:part_rows] for v in both_cot], axis=0)
    far_cot = jnp.concatenate([v[part_rows:] for v in both_cot], axis=0)
    cots = [cot_own, permute_ctx(cot_own, 1), far_cot, permute_ctx(far_cot, 1)]

    if swap:
        outs_f = [shape_of((2 * width, hid_half), LOW)] * 4
    else:
        outs_f = [shape_of((2, width, hid_half), LOW), shape_of((2, hid_half, width), LOW)]
    four = (4 * rows_n, d_model)
    out_own, out_send, out_far, dn3, dn3_send, dn3_far, *grads_f = run(
        functools.partial(feed_kernel, pieces, swap),
        [offsets, gains[2:3], *rows_f, *cots, *weights_f],
        [
            shape_of(flat, F32),
            shape_of(two, LOW),
            shape_of(flat, LOW),
            shape_of(two, LOW),
            shape_of(flat, LOW),
            shape_of(flat, LOW),
            *outs_f,
        ],
        [VMEM(four, LOW), VMEM(four, LOW), VMEM(four, F32), VMEM(four, F32)],
        24 * unit,
        "feed",
        20,
    )
    (chip_sum,) = sum_parts(((dn3_far, 0), (permute_ctx(dn3_send, 1), 0)), "feed_near", 1)
    far3 = permute_ctx(chip_sum, 2)
    far3_pair = permute_ctx(far3, 1)
    got3 = permute_ctx(dn3, 1)
    if swap:
        got_f = permute_fsdp(grads_f[3])
        got_f, far3_pair = barrier((got_f, far3_pair))
        b_f = grads_f[1] + got_f
        got_f = permute_fsdp(grads_f[2])
        add_f = permute_tp(b_f, 1)
    got_out = permute_ctx(out_send, 1)
    (chip_out,) = sum_parts(((out_far, 0), (got_out, rows_n)), "feed_out_near", 1)
    far_out = permute_ctx(after(chip_out, far3), 2)

    parts_s, grads_s, (carried2, gain3) = attend_backward(
        [own1, pair1],
        saved_s,
        bias_s,
        [rows_f[0], rows_f[1], dn3, got3, far3, far3_pair, gains[2:3], cots[0], cots[1]],
        weights_s,
        True,
        "space_backward",
    )
    if swap:
        parts_s, far_out, got_f, add_f = barrier((parts_s, far_out, got_f, add_f))
    got2 = permute_ctx(parts_s[1], 1)
    parts1, gain2 = norm_backward(
        ((parts_s[0], 0), (got2, 0)), own1, gains[1:2], carried2, "space_norm"
    )
    own_t = jnp.concatenate(turn(parts1), axis=0)
    near_own_t = permute_tp(own_t, 1)
    head_t = [own_t, permute_ctx(own_t, 1), near_own_t, permute_ctx(near_own_t, 1)]
    out_parts = sum_parts(((out_own, 0), (got_out, 0), (far_out, 0)), "feed_sum")
    out_time = turn(after(out_parts, own_t))
    if swap:
        got_sums_s = first_sends(grads_s)
        keep_s, send_s = first_sums(grads_s, after(got_sums_s, own_t))
        got_sums_s = second_sends(send_s)
        near_own_t, got_sums_s = barrier((near_own_t, got_sums_s))
        sums_s = second_sums(keep_s, got_sums_s)
        add_s = permute_tp(sums_s[1], 1)
        a_f = grads_f[0] + got_f + add_f
        add_f = along(after(a_f, near_own_t), 2, True)

    parts_t, grads_t, _ = attend_backward(
        rows_t, saved_t, bias_t, head_t, weights_t, False, "time_backward"
    )
    if swap:
        parts_t, grads_t, add_s, add_f, gain2, out_time = barrier(
            (parts_t, grads_t, add_s, add_f, gain2, out_time)
        )
        got_sums_t = first_sends(grads_t)
    got1 = permute_ctx(parts_t[2], 1)
    (chip1,) = sum_parts(((parts_t[1], 0), (got1, rows_n)), "time_back_near", 1)
    near1 = permute_tp(chip1, 1)
    if swap:
        got_sums_t, near1 = barrier((got_sums_t, near1))
        keep_t, send_t = first_sums(grads_t, got_sums_t)
        got_sums_t = second_sends(send_t)
    parts0, gain1 = norm_backward(
        ((parts_t[0], 0), (got1, 0), (near1, 0)), start, gains[0:1], own_t, "time_norm"
    )
    gain_all = jnp.concatenate((gain1, gain2, gain3), axis=0)
    if swap:
        a_s = sums_s[0] + add_s
        add_s = along(after(a_s, near1), 2, True)
        total_f = a_f + add_f
        gain_got = permute_ctx(gain_all, 1)
        got_sums_t, add_s, total_f, gain_got = barrier((got_sums_t, add_s, total_f, gain_got))
        (a_t,) = second_sums(keep_t, got_sums_t)
        got_t = along(a_t, 2, True)
        total_s = a_s + add_s
        other_s = permute_ctx(total_s, 2)
        other_f = permute_ctx(total_f, 2)
        gain_all = gain_all + gain_got
        gain_got = permute_fsdp(gain_all)
        got_t, other_f, other_s, gain_got, parts0, out_time = barrier(
            (got_t, other_f, other_s, gain_got, parts0, out_time)
        )
        total_t = a_t + got_t
        other_t = permute_ctx(total_t, 2)
        gain_all = gain_all + gain_got
        gain_got = permute_tp(gain_all, 1)
        both_f, both_s = ordered(total_f, other_f), ordered(total_s, other_s)
        up_grad, down_grad = feed_out(to_pair(both_f))
        s_qkv, s_proj = attention_out(to_pair(both_s))
        both_rows = [jnp.concatenate(pair, axis=0) for pair in zip(out_time, parts0)]
        other_t, gain_got, both_rows, up_grad, down_grad, s_qkv, s_proj = barrier(
            (other_t, gain_got, both_rows, up_grad, down_grad, s_qkv, s_proj)
        )
        got_both = time_sends(both_rows)
        both_t = ordered(total_t, other_t)
        pair_t = permute_ctx(both_t, 1)
        gain_all = gain_all + gain_got
        here = [(a, b) for a in range(n_ctx) for b in range(n_tp)]
        gain_got = [
            lax.ppermute(
                gain_all,
                ("ctx", "tp"),
                [(a * n_tp + b, (a ^ da) * n_tp + (b ^ db)) for a, b in here],
            )
            for da, db in ((0, 2), (2, 0), (2, 2))
        ]
        gain_all = gain_all + gain_got[0] + (gain_got[1] + gain_got[2])
        block_out = time_finish([v[:part_rows] for v in got_both])
        tokens_grad = time_finish([v[part_rows:] for v in got_both]).astype(F32)
        t_qkv, t_proj = attention_out(jnp.where(is_source, both_t, pair_t))
        gain_grads = lax.dynamic_slice_in_dim(gain_all, x * d_part, d_part, axis=1)
    else:
        tokens_grad = time_finish(time_sends(parts0)).astype(F32)
        block_out = time_finish(time_sends(out_time))
        up_grad, down_grad = feed_grads_wide(grads_f)
        s_qkv, s_proj = attention_grads_wide(grads_s)
        t_qkv, t_proj = attention_grads_wide(grads_t)
        for bits in (1, 2):
            gain_all = gain_all + permute_ctx(gain_all, bits)
        for bits in (1, 2):
            gain_all = gain_all + permute_tp(gain_all, bits)
        gain_grads = lax.psum_scatter(gain_all, "fsdp", scatter_dimension=1, tiled=True)
    return (
        block_out,
        tokens_grad,
        gain_grads,
        t_qkv,
        t_proj,
        s_qkv,
        s_proj,
        up_grad,
        down_grad,
    )


def solution(mesh):
    rows = P("tp", "ctx", "fsdp", None)
    weights = (
        P(None, "fsdp"),
        P("fsdp", None, "tp"),
        P("tp", "fsdp"),
        P("fsdp", None, "tp"),
        P("tp", "fsdp"),
        P("fsdp", "tp"),
        P("tp", "fsdp"),
    )
    sizes = (mesh.shape["fsdp"], mesh.shape["ctx"], mesh.shape["tp"])
    return jax.shard_map(
        functools.partial(body, sizes),
        mesh=mesh,
        in_specs=(rows, *weights, rows),
        out_specs=(rows, rows, *weights),
        check_vma=False,
    )
```

time: 347 us -> 306 us (0.88)
  waiting for transfers between devices: 140 us -> 94.2 us
  starting transfers between devices: 92.5 us -> 122 us
  other arithmetic: 37.7 us -> 21.5 us
  local copies, waits for them, and re-layouts: 19.2 us -> 6.98 us
  Pallas kernels: 50.6 us -> 55.2 us
    ppermute x20 -> x21, waiting for transfers between devices: 51.3 us -> 29.5 us  [permute_tp(): return lax.ppermute(v, 'tp', [(a, a ^ bits) for a in range(n_tp)])]
    ppermute x20 -> x21, starting transfers between devices: 13.3 us -> 26.9 us  [permute_tp(): return lax.ppermute(v, 'tp', [(a, a ^ bits) for a in range(n_tp)])]
    ppermute x39 -> x41, waiting for transfers between devices: 52.4 us -> 39.2 us  [permute_ctx(): return lax.ppermute(v, 'ctx', [(a, a ^ bits) for a in range(n_ctx)])]
    ppermute x6 -> x9, starting transfers between devices: 15.6 us -> 28.2 us  [the longest x6 24.2 us: along(): return lax.ppermute(v, ('ctx', 'tp'), pairs)]
    ppermute x6 -> x9, waiting for transfers between devices: 13.2 us -> 5.02 us  [the longest x6 5.01 us: along(): return lax.ppermute(v, ('ctx', 'tp'), pairs)]
    ppermute x39 -> x41, starting transfers between devices: 48.5 us -> 56.7 us  [permute_ctx(): return lax.ppermute(v, 'ctx', [(a, a ^ bits) for a in range(n_ctx)])]
    unnamed x104 -> x56, local copies, waits for them, and re-layouts: 9.48 us -> 3.92 us
    pallas_call x9 -> x14, Pallas kernels: 50.6 us -> 55.2 us  [run(): pl.pallas_call(kernel, out_shape=outs, in_specs=specs, out_specs=in_vmem(...]
  transfers between devices with their start and end apart: 80 -> 84, of which waited for: 37 -> 44; matrix products, arithmetic and copies ran while one was open for 12% -> 8% of each run, Pallas kernels for 10% -> 14%
where the time goes in v3:
time: 306 us; the launch traced here: 302 us
  starting transfers between devices  122 us (40%)
  waiting for transfers between devices  94.2 us (31%)
  Pallas kernels  55.2 us (18%)
  other arithmetic  21.5 us (7%)
  local copies, waits for them, and re-layouts  6.98 us (2%)
    ppermute x41, starting transfers between devices, permute_ctx(): return lax.ppermute(v, 'ctx', [(a, a ^ bits) for a in range(n_ctx)])  56.7 us
    pallas_call x14, Pallas kernels, run(): pl.pallas_call(kernel, out_shape=outs, in_specs=specs, out_specs=in_vmem(...  55.2 us
    ppermute x41, waiting for transfers between devices, permute_ctx(): return lax.ppermute(v, 'ctx', [(a, a ^ bits) for a in range(n_ctx)])  39.2 us
    ppermute x21, waiting for transfers between devices, permute_tp(): return lax.ppermute(v, 'tp', [(a, a ^ bits) for a in range(n_tp)])  29.5 us
    ppermute x21, starting transfers between devices, permute_tp(): return lax.ppermute(v, 'tp', [(a, a ^ bits) for a in range(n_tp)])  26.9 us
    ppermute x6, starting transfers between devices, along(): return lax.ppermute(v, ('ctx', 'tp'), pairs)  24.2 us
    ppermute x13, waiting for transfers between devices, permute_fsdp(): return lax.ppermute(v, 'fsdp', [(0, 1), (1, 0)])  20.5 us
    ppermute x13, starting transfers between devices, permute_fsdp(): return lax.ppermute(v, 'fsdp', [(0, 1), (1, 0)])  10.7 us
  transfers between devices with their start and end apart: 84, of which 44 were waited for; matrix products, arithmetic and copies ran while one was open for 8% of the time, Pallas kernels for 14%

profile of v3, /device:TPU:1, one launch (start us, length us, event | category | flops | bytes accessed | tf_op | source)
XLA Modules:
  0.0 302.4 jit_solution(15723628869683029202)
XLA Ops:
  6.3 4.3 %collective-permute-start.3 = (bf16[52,768]{1,0:T(8,128)(2,1)S(1)}, bf16[52,768]{1,0:T(8,128)(2,1)}, u32[]{:S(2)}, u32[]{:S(2)}) collective-permute-start(bf16[52,768]{1,0:T(8,128)(2,1)S(1)} %select_n.442), channel_id=1, source_target_pairs={{0,4},{4,0},{8,12},{12,8},{1,5},{5,1},{9,13},{13,9},{2,6},{6,2},{1... | collective-permute-start | bytes 239624 | tf_op jit(solution)/shard_map/ppermute | solution.py:400
  17.7 4.0 %collective-permute-done = bf16[768,384]{1,0:T(8,128)(2,1)S(1)} collective-permute-done((bf16[768,384]{1,0:T(8,128)(2,1)S(1)}, bf16[768,384]{1,0:T(8,128)(2,1)S(1)}, u32[]{:S(2)}, u32[]{:S(2)}) %collective-permute-start) | collective-permute-done | bytes 589856 | tf_op jit(solution)/shard_map/ppermute | solution.py:414
  25.1 8.2 %collective-permute-start.12 = (bf16[52,768]{1,0:T(8,128)(2,1)S(1)}, bf16[52,768]{1,0:T(8,128)(2,1)S(1)}, u32[]{:S(2)}, u32[]{:S(2)}) collective-permute-start(bf16[52,768]{1,0:T(8,128)(2,1)S(1)} %select_n.466), channel_id=1, source_target_pairs={{0,4},{4,0},{8,12},{12,8},{1,5},{5,1},{9,13},{13,9},{2,6},{6,2},{1... | collective-permute-start | bytes 239624 | tf_op jit(solution)/shard_map/ppermute | solution.py:400
  44.5 8.8 %time_forward.1 = (bf16[208,768]{1,0:T(8,128)(2,1)S(1)}, bf16[208,768]{1,0:T(8,128)(2,1)S(1)}, bf16[416,768]{1,0:T(8,128)(2,1)S(1)}, bf16[832,768]{1,0:T(8,128)(...) custom-call(s32[3]{0:T(128)S(1)} %pad_add_fusion.refs_0_, ...), custom_call_target="tpu_custom_call" | custom-call | flops 1472200704 | bytes 7647244 | tf_op jit(solution)/shard_map/time_forward/pallas_call | solution.py:371
  55.0 3.3 %collective-permute-done.14.refs_6_ = bf16[768,384]{1,0:T(8,128)(2,1)S(1)} collective-permute-done((bf16[768,384]{1,0:T(8,128)(2,1)S(1)}, bf16[768,384]{1,0:T(8,128)(2,1)S(1)}, u32[]{:S(2)}, u32[]{:S(2)}) %collective-permute-start.14) | collective-permute-done | bytes 589856 | tf_op jit(solution)/shard_map/ppermute | solution.py:406
  61.9 12.6 %collective-permute-start.18 = (bf16[768,384]{1,0:T(8,128)(2,1)S(1)}, bf16[768,384]{1,0:T(8,128)(2,1)}, u32[]{:S(2)}, u32[]{:S(2)}) collective-permute-start(bf16[768,384]{1,0:T(8,128)(2,1)S(1)} %copy-done.14), channel_id=1, source_target_pairs={{0,2},{1,3},{6,4},{7,5},{8,10},{9,11},{14,12},{15,13},{16,18},{17,... | collective-permute-start | bytes 1769480 | tf_op jit(solution)/shard_map/ppermute | solution.py:414
  75.2 10.1 %collective-permute-done.16.refs_3_ = bf16[208,768]{1,0:T(8,128)(2,1)S(1)} collective-permute-done((bf16[208,768]{1,0:T(8,128)(2,1)S(1)}, bf16[208,768]{1,0:T(8,128)(2,1)S(1)}, u32[]{:S(2)}, u32[]{:S(2)}) %collective-permute-start.16) | collective-permute-done | bytes 319520 | tf_op jit(solution)/shard_map/ppermute | solution.py:403
  85.6 3.2 %collective-permute-start.20 = (bf16[52,768]{1,0:T(8,128)(2,1)S(1)}, bf16[52,768]{1,0:T(8,128)(2,1)S(1)}, u32[]{:S(2)}, u32[]{:S(2)}) collective-permute-start(bf16[52,768]{1,0:T(8,128)(2,1)S(1)} %get-tuple-element.208), channel_id=1, source_target_pairs={{0,2},{1,3},{2,0},{3,1},{4,6},{5,7},{6,4},{7,5},{8,10},{9,11},{10,... | collective-permute-start | bytes 239624 | tf_op jit(solution)/shard_map/ppermute | solution.py:403
  90.7 4.2 %collective-permute-done.21 = bf16[52,768]{1,0:T(8,128)(2,1)} collective-permute-done((bf16[52,768]{1,0:T(8,128)(2,1)S(1)}, bf16[52,768]{1,0:T(8,128)(2,1)}, u32[]{:S(2)}, u32[]{:S(2)}) %collective-permute-start.21) | collective-permute-done | bytes 79904 | tf_op jit(solution)/shard_map/ppermute | solution.py:403
  101.5 7.5 %space_forward.1 = (bf16[208,768]{1,0:T(8,128)(2,1)S(1)}, bf16[208,768]{1,0:T(8,128)(2,1)S(1)}, bf16[416,768]{1,0:T(8,128)(2,1)S(1)}, bf16[416,576]{1,0:T(8,128)...) custom-call(s32[3]{0:T(128)S(1)} %pad_add_fusion.refs_0_, ...), custom_call_target="tpu_custom_call" | custom-call | flops 1472200704 | bytes 8089612 | tf_op jit(solution)/shard_map/space_forward/pallas_call | solution.py:371
  111.4 2.6 collective-permute-done.25.refs_11_
  120.7 4.6 %collective-permute-start.27 = (bf16[208,768]{1,0:T(8,128)(2,1)S(1)}, bf16[208,768]{1,0:T(8,128)(2,1)S(1)}, u32[]{:S(2)}, u32[]{:S(2)}) collective-permute-start(bf16[208,768]{1,0:T(8,128)(2,1)S(1)} %space_sum.1.refs_2_.refs_7_), channel_id=1, source_target_pairs={{0,4},{4,0},{8,12},{12,8},{1,5},{5,1},{9,13},{13,9},{2,6},{6,2},{1... | collective-permute-start | bytes 958472 | tf_op jit(solution)/shard_map/ppermute | solution.py:400
  125.3 3.2 %collective-permute-done.32 = bf16[104,768]{1,0:T(8,128)(2,1)S(1)} collective-permute-done((bf16[104,768]{1,0:T(8,128)(2,1)S(1)}, bf16[104,768]{1,0:T(8,128)(2,1)S(1)}, u32[]{:S(2)}, u32[]{:S(2)}) %collective-permute-start.32) | collective-permute-done | bytes 159776 | tf_op jit(solution)/shard_map/ppermute | solution.py:403
  128.7 5.3 %collective-permute-start.34 = (bf16[208,768]{1,0:T(8,128)(2,1)S(1)}, bf16[208,768]{1,0:T(8,128)(2,1)S(1)}, u32[]{:S(2)}, u32[]{:S(2)}) collective-permute-start(bf16[208,768]{1,0:T(8,128)(2,1)S(1)} %pad_maximum_fusion.9.refs_6_.refs_14_), channel_id=1, source_target_pairs={{0,4},{4,0},{8,12},{12,8},{1,5},{5,1},{9,13},{13,9},{2,6},{6,2},{1... | collective-permute-start | bytes 958472 | tf_op jit(solution)/shard_map/ppermute | solution.py:400
  135.7 12.0 %feed.1 = (f32[208,768]{1,0:T(8,128)S(1)}, bf16[416,768]{1,0:T(8,128)(2,1)S(1)}, bf16[208,768]{1,0:T(8,128)(2,1)S(1)}, bf16[416,768]{1,0:T(8,128)(2,1)S(1)}, bf1...) custom-call(s32[3]{0:T(128)S(1)} %pad_add_fusion.refs_0_, ...), custom_call_target="tpu_custom_call" | custom-call | flops 5888802816 | bytes 10152972 | tf_op jit(solution)/shard_map/feed/pallas_call | solution.py:371
  151.6 6.8 %collective-permute-done.38.refs_11_ = bf16[208,768]{1,0:T(8,128)(2,1)S(1)} collective-permute-done((bf16[208,768]{1,0:T(8,128)(2,1)S(1)}, bf16[208,768]{1,0:T(8,128)(2,1)S(1)}, u32[]{:S(2)}, u32[]{:S(2)}) %collective-permute-start.38) | collective-permute-done | bytes 319520 | tf_op jit(solution)/shard_map/ppermute | solution.py:400
  160.5 3.8 %collective-permute-done.39 = bf16[768,384]{1,0:T(8,128)(2,1)S(1)} collective-permute-done((bf16[768,384]{1,0:T(8,128)(2,1)S(1)}, bf16[768,384]{1,0:T(8,128)(2,1)S(1)}, u32[]{:S(2)}, u32[]{:S(2)}) %collective-permute-start.39) | collective-permute-done | bytes 589856 | tf_op jit(solution)/shard_map/ppermute | solution.py:406
  167.7 12.7 %space_backward.1 = (bf16[208,768]{1,0:T(8,128)(2,1)S(1)}, bf16[208,768]{1,0:T(8,128)(2,1)S(1)}, bf16[2,2,192,384]{3,2,1,0:T(8,128)(2,1)S(1)}, bf16[2,2,192,384]...) custom-call(s32[3]{0:T(128)S(1)} %pad_add_fusion.refs_0_, ...), custom_call_target="tpu_custom_call" | custom-call | flops 2944401408 | bytes 11287564 | tf_op jit(solution)/shard_map/space_backward/pallas_call | solution.py:371
  181.7 3.8 %collective-permute-start.45 = (bf16[208,768]{1,0:T(8,128)(2,1)S(1)}, bf16[208,768]{1,0:T(8,128)(2,1)S(1)}, u32[]{:S(2)}, u32[]{:S(2)}) collective-permute-start(bf16[208,768]{1,0:T(8,128)(2,1)S(1)} %get-tuple-element.255), channel_id=1, source_target_pairs={{0,4},{4,0},{8,12},{12,8},{1,5},{5,1},{9,13},{13,9},{2,6},{6,2},{1... | collective-permute-start | bytes 958472 | tf_op jit(solution)/shard_map/ppermute | solution.py:400
  192.1 2.7 collective-permute-done.48
  194.9 3.1 %collective-permute-start.50 = (bf16[208,768]{1,0:T(8,128)(2,1)S(1)}, bf16[208,768]{1,0:T(8,128)(2,1)S(1)}, u32[]{:S(2)}, u32[]{:S(2)}) collective-permute-start(bf16[208,768]{1,0:T(8,128)(2,1)S(1)} %pad_maximum_fusion.11.refs_5_), channel_id=1, source_target_pairs={{0,1},{1,0},{2,3},{3,2},{4,5},{5,4},{6,7},{7,6},{8,9},{9,8},{10,11... | collective-permute-start | bytes 958472 | tf_op jit(solution)/shard_map/ppermute | solution.py:403
  200.4 2.8 collective-permute-start.57
  206.6 2.7 collective-permute-start.51
  213.9 12.2 %time_backward.1 = (bf16[208,768]{1,0:T(8,128)(2,1)S(1)}, bf16[208,768]{1,0:T(8,128)(2,1)S(1)}, bf16[416,768]{1,0:T(8,128)(2,1)S(1)}, bf16[2,1,192,384]{3,2,1,0:...) custom-call(s32[3]{0:T(128)S(1)} %pad_add_fusion.refs_0_, ...), custom_call_target="tpu_custom_call" | custom-call | flops 2944401408 | bytes 7644172 | tf_op jit(solution)/shard_map/time_backward/pallas_call | solution.py:371
  226.1 3.8 %collective-permute-done.58 = bf16[52,768]{1,0:T(8,128)(2,1)S(1)} collective-permute-done((bf16[52,768]{1,0:T(8,128)(2,1)S(1)}, bf16[52,768]{1,0:T(8,128)(2,1)S(1)}, u32[]{:S(2)}, u32[]{:S(2)}) %collective-permute-start.58) | collective-permute-done | bytes 79904 | tf_op jit(solution)/shard_map/ppermute | solution.py:403
  233.4 7.6 %collective-permute-done.61 = bf16[2,1,192,384]{3,2,1,0:T(8,128)(2,1)S(1)} collective-permute-done((bf16[2,1,192,384]{3,2,1,0:T(8,128)(2,1)S(1)}, bf16[2,1,192,384]{3,2,1,0:T(8,128)(2,1)S(1)}, u32[]{:S(2)}, u32[]{:S(2)}) %collective-permute-start.61) | collective-permute-done | bytes 294944 | tf_op jit(solution)/shard_map/ppermute | solution.py:406
  250.1 4.1 %collective-permute-start.69 = (bf16[2,192,384]{2,1,0:T(8,128)(2,1)S(1)}, bf16[2,192,384]{2,1,0:T(8,128)(2,1)S(1)}, u32[]{:S(2)}, u32[]{:S(2)}) collective-permute-start(bf16[2,192,384]{2,1,0:T(8,128)(2,1)S(1)} %pad_maximum_fusion.13), channel_id=1, source_target_pairs={{2,0},{3,1},{4,6},{5,7},{10,8},{11,9},{12,14},{13,15},{18,16},{19,... | collective-permute-start | bytes 884744 | tf_op jit(solution)/shard_map/ppermute | solution.py:414
  257.9 6.1 %collective-permute-done.71 = bf16[2,192,384]{2,1,0:T(8,128)(2,1)S(1)} collective-permute-done((bf16[2,192,384]{2,1,0:T(8,128)(2,1)S(1)}, bf16[2,192,384]{2,1,0:T(8,128)(2,1)S(1)}, u32[]{:S(2)}, u32[]{:S(2)}) %collective-permute-start.71) | collective-permute-done | bytes 294944 | tf_op jit(solution)/shard_map/ppermute | solution.py:400
  264.0 5.2 %collective-permute-start.74 = (f32[3,768]{1,0:T(4,128)S(1)}, f32[3,768]{1,0:T(4,128)S(1)}, u32[]{:S(2)}, u32[]{:S(2)}) collective-permute-start(f32[3,768]{1,0:T(4,128)S(1)} %fusion.21), channel_id=1, source_target_pairs={{0,1},{1,0},{2,3},{3,2},{4,5},{5,4},{6,7},{7,6},{8,9},{9,8},{10,11... | collective-permute-start | bytes 27656 | tf_op jit(solution)/shard_map/ppermute | solution.py:403
  269.5 4.3 %collective-permute-start.76 = (bf16[2,2,192,384]{3,2,1,0:T(8,128)(2,1)S(1)}, bf16[2,2,192,384]{3,2,1,0:T(8,128)(2,1)S(1)}, u32[]{:S(2)}, u32[]{:S(2)}) collective-permute-start(bf16[2,2,192,384]{3,2,1,0:T(8,128)(2,1)S(1)} %pad_maximum_fusion.4), channel_id=1, source_target_pairs={{0,4},{4,0},{8,12},{12,8},{1,5},{5,1},{9,13},{13,9},{2,6},{6,2},{1... | collective-permute-start | bytes 1769480 | tf_op jit(solution)/shard_map/ppermute | solution.py:400
  282.2 2.8 collective-permute-start.82
  291.2 5.1 %collective-permute-done.77 = bf16[104,768]{1,0:T(8,128)(2,1)S(1)} collective-permute-done((bf16[104,768]{1,0:T(8,128)(2,1)S(1)}, bf16[104,768]{1,0:T(8,128)(2,1)S(1)}, u32[]{:S(2)}, u32[]{:S(2)}) %collective-permute-start.77) | collective-permute-done | bytes 159776 | tf_op jit(solution)/shard_map/ppermute | solution.py:400
  (328 shorter events, 117.0 us)
Async XLA Ops:
  0.7 13.9 %collective-permute-start.4 = (bf16[3,384]{1,0:T(4,128)(2,1)}, bf16[3,384]{1,0:T(4,128)(2,1)S(1)}, u32[]{:S(2)}, u32[]{:S(2)}) collective-permute-start(bf16[3,384]{1,0:T(4,128)(2,1)} %param.10), channel_id=1, source_target_pairs={{0,16},{16,0},{1,17},{17,1},{2,18},{18,2},{3,19},{19,3},{4,20},{20... | collective-permute-start | bytes 6920 | tf_op jit(solution)/shard_map/ppermute | solution.py:406
  3.9 17.8 %collective-permute-start = (bf16[768,384]{1,0:T(8,128)(2,1)S(1)}, bf16[768,384]{1,0:T(8,128)(2,1)S(1)}, u32[]{:S(2)}, u32[]{:S(2)}) collective-permute-start(bf16[768,384]{1,0:T(8,128)(2,1)S(1)} %pad_maximum_fusion.1), channel_id=1, source_target_pairs={{0,2},{1,3},{6,4},{7,5},{8,10},{9,11},{14,12},{15,13},{16,18},{17,... | collective-permute-start | bytes 1769480 | tf_op jit(solution)/shard_map/ppermute | solution.py:414
  21.8 18.4 %collective-permute-start.7 = (bf16[208,768]{1,0:T(8,128)(2,1)S(1)}, bf16[208,768]{1,0:T(8,128)(2,1)S(1)}, u32[]{:S(2)}, u32[]{:S(2)}) collective-permute-start(bf16[208,768]{1,0:T(8,128)(2,1)S(1)} %pad_maximum_fusion.6.refs_1_.refs_0_.refs_3_), channel_id=1, source_target_pairs={{0,1},{1,0},{2,3},{3,2},{4,5},{5,4},{6,7},{7,6},{8,9},{9,8},{10,11... | collective-permute-start | bytes 958472 | tf_op jit(solution)/shard_map/ppermute | solution.py:403
  21.9 19.5 %collective-permute-start.5 = (bf16[768,384]{1,0:T(8,128)(2,1)S(1)}, bf16[768,384]{1,0:T(8,128)(2,1)S(1)}, u32[]{:S(2)}, u32[]{:S(2)}) collective-permute-start(bf16[768,384]{1,0:T(8,128)(2,1)S(1)} %broadcast_select_fusion.5.refs_7_), channel_id=1, source_target_pairs={{0,16},{16,0},{1,17},{17,1},{2,18},{18,2},{3,19},{19,3},{4,20},{20... | collective-permute-start | bytes 1769480 | tf_op jit(solution)/shard_map/ppermute | solution.py:406
  22.1 19.4 %collective-permute-start.9 = (bf16[768,384]{1,0:T(8,128)(2,1)S(1)}, bf16[768,384]{1,0:T(8,128)(2,1)}, u32[]{:S(2)}, u32[]{:S(2)}) collective-permute-start(bf16[768,384]{1,0:T(8,128)(2,1)S(1)} %pad_maximum_fusion.2), channel_id=1, source_target_pairs={{0,2},{1,3},{6,4},{7,5},{8,10},{9,11},{14,12},{15,13},{16,18},{17,... | collective-permute-start | bytes 1769480 | tf_op jit(solution)/shard_map/ppermute | solution.py:414
  43.1 15.1 %collective-permute-start.14 = (bf16[768,384]{1,0:T(8,128)(2,1)S(1)}, bf16[768,384]{1,0:T(8,128)(2,1)S(1)}, u32[]{:S(2)}, u32[]{:S(2)}) collective-permute-start(bf16[768,384]{1,0:T(8,128)(2,1)S(1)} %broadcast_select_fusion.4.refs_5_), channel_id=1, source_target_pairs={{0,16},{16,0},{1,17},{17,1},{2,18},{18,2},{3,19},{19,3},{4,20},{20... | collective-permute-start | bytes 1769480 | tf_op jit(solution)/shard_map/ppermute | solution.py:406
  44.4 15.2 %collective-permute-start.13 = (bf16[768,384]{1,0:T(8,128)(2,1)S(1)}, bf16[768,384]{1,0:T(8,128)(2,1)S(1)}, u32[]{:S(2)}, u32[]{:S(2)}) collective-permute-start(bf16[768,384]{1,0:T(8,128)(2,1)S(1)} %broadcast_select_fusion.4.refs_5_), channel_id=1, source_target_pairs={{0,1},{1,0},{2,3},{3,2},{4,5},{5,4},{6,7},{7,6},{8,9},{9,8},{10,11... | collective-permute-start | bytes 1769480 | tf_op jit(solution)/shard_map/ppermute | solution.py:403
  61.9 23.6 %collective-permute-start.18 = (bf16[768,384]{1,0:T(8,128)(2,1)S(1)}, bf16[768,384]{1,0:T(8,128)(2,1)}, u32[]{:S(2)}, u32[]{:S(2)}) collective-permute-start(bf16[768,384]{1,0:T(8,128)(2,1)S(1)} %copy-done.14), channel_id=1, source_target_pairs={{0,2},{1,3},{6,4},{7,5},{8,10},{9,11},{14,12},{15,13},{16,18},{17,... | collective-permute-start | bytes 1769480 | tf_op jit(solution)/shard_map/ppermute | solution.py:414
  74.5 21.3 %collective-permute-start.22 = (bf16[768,384]{1,0:T(8,128)(2,1)S(1)}, bf16[768,384]{1,0:T(8,128)(2,1)S(1)}, u32[]{:S(2)}, u32[]{:S(2)}) collective-permute-start(bf16[768,384]{1,0:T(8,128)(2,1)S(1)} %collective-permute-done.13.refs_7_), channel_id=1, source_target_pairs={{0,16},{16,0},{1,17},{17,1},{2,18},{18,2},{3,19},{19,3},{4,20},{20... | collective-permute-start | bytes 1769480 | tf_op jit(solution)/shard_map/ppermute | solution.py:406
  74.8 10.4 %collective-permute-start.16 = (bf16[208,768]{1,0:T(8,128)(2,1)S(1)}, bf16[208,768]{1,0:T(8,128)(2,1)S(1)}, u32[]{:S(2)}, u32[]{:S(2)}) collective-permute-start(bf16[208,768]{1,0:T(8,128)(2,1)S(1)} %time_near.1), channel_id=1, source_target_pairs={{0,1},{1,0},{2,3},{3,2},{4,5},{5,4},{6,7},{7,6},{8,9},{9,8},{10,11... | collective-permute-start | bytes 958472 | tf_op jit(solution)/shard_map/ppermute | solution.py:403
  74.8 10.7 %collective-permute-start.17 = (bf16[208,768]{1,0:T(8,128)(2,1)S(1)}, bf16[208,768]{1,0:T(8,128)(2,1)S(1)}, u32[]{:S(2)}, u32[]{:S(2)}) collective-permute-start(bf16[208,768]{1,0:T(8,128)(2,1)S(1)} %pad_maximum_fusion.7), channel_id=1, source_target_pairs={{0,8},{4,12},{8,0},{12,4},{1,9},{5,13},{9,1},{13,5},{2,10},{6,14},... | collective-permute-start | bytes 958472 | tf_op jit(solution)/shard_map/ppermute | solution.py:400
  99.5 14.5 %collective-permute-start.25 = (bf16[768,384]{1,0:T(8,128)(2,1)S(1)}, bf16[768,384]{1,0:T(8,128)(2,1)S(1)}, u32[]{:S(2)}, u32[]{:S(2)}) collective-permute-start(bf16[768,384]{1,0:T(8,128)(2,1)S(1)} %broadcast_select_fusion.3.refs_10_), channel_id=1, source_target_pairs={{0,16},{16,0},{1,17},{17,1},{2,18},{18,2},{3,19},{19,3},{4,20},{20... | collective-permute-start | bytes 1769480 | tf_op jit(solution)/shard_map/ppermute | solution.py:406
  100.2 14.2 %collective-permute-start.24 = (bf16[768,384]{1,0:T(8,128)(2,1)S(1)}, bf16[768,384]{1,0:T(8,128)(2,1)S(1)}, u32[]{:S(2)}, u32[]{:S(2)}) collective-permute-start(bf16[768,384]{1,0:T(8,128)(2,1)S(1)} %broadcast_select_fusion.3.refs_10_), channel_id=1, source_target_pairs={{0,1},{1,0},{2,3},{3,2},{4,5},{5,4},{6,7},{7,6},{8,9},{9,8},{10,11... | collective-permute-start | bytes 1769480 | tf_op jit(solution)/shard_map/ppermute | solution.py:403
  114.4 14.1 %collective-permute-start.33 = (bf16[768,384]{1,0:T(8,128)(2,1)S(1)}, bf16[768,384]{1,0:T(8,128)(2,1)S(1)}, u32[]{:S(2)}, u32[]{:S(2)}) collective-permute-start(bf16[768,384]{1,0:T(8,128)(2,1)S(1)} %collective-permute-done.24.refs_12_), channel_id=1, source_target_pairs={{0,16},{16,0},{1,17},{17,1},{2,18},{18,2},{3,19},{19,3},{4,20},{20... | collective-permute-start | bytes 1769480 | tf_op jit(solution)/shard_map/ppermute | solution.py:406
  120.7 13.4 %collective-permute-start.27 = (bf16[208,768]{1,0:T(8,128)(2,1)S(1)}, bf16[208,768]{1,0:T(8,128)(2,1)S(1)}, u32[]{:S(2)}, u32[]{:S(2)}) collective-permute-start(bf16[208,768]{1,0:T(8,128)(2,1)S(1)} %space_sum.1.refs_2_.refs_7_), channel_id=1, source_target_pairs={{0,4},{4,0},{8,12},{12,8},{1,5},{5,1},{9,13},{13,9},{2,6},{6,2},{1... | collective-permute-start | bytes 958472 | tf_op jit(solution)/shard_map/ppermute | solution.py:400
  150.0 14.3 %collective-permute-start.39 = (bf16[768,384]{1,0:T(8,128)(2,1)S(1)}, bf16[768,384]{1,0:T(8,128)(2,1)S(1)}, u32[]{:S(2)}, u32[]{:S(2)}) collective-permute-start(bf16[768,384]{1,0:T(8,128)(2,1)S(1)} %get-tuple-element.240), channel_id=1, source_target_pairs={{0,16},{16,0},{1,17},{17,1},{2,18},{18,2},{3,19},{19,3},{4,20},{20... | collective-permute-start | bytes 1769480 | tf_op jit(solution)/shard_map/ppermute | solution.py:406
  150.7 15.8 %collective-permute-start.41 = (bf16[416,768]{1,0:T(8,128)(2,1)S(1)}, bf16[416,768]{1,0:T(8,128)(2,1)S(1)}, u32[]{:S(2)}, u32[]{:S(2)}) collective-permute-start(bf16[416,768]{1,0:T(8,128)(2,1)S(1)} %get-tuple-element.249), channel_id=1, source_target_pairs={{0,4},{4,0},{8,12},{12,8},{1,5},{5,1},{9,13},{13,9},{2,6},{6,2},{1... | collective-permute-start | bytes 1916936 | tf_op jit(solution)/shard_map/ppermute | solution.py:400
  151.6 16.0 %collective-permute-start.36 = (bf16[416,768]{1,0:T(8,128)(2,1)S(1)}, bf16[416,768]{1,0:T(8,128)(2,1)S(1)}, u32[]{:S(2)}, u32[]{:S(2)}) collective-permute-start(bf16[416,768]{1,0:T(8,128)(2,1)S(1)} %get-tuple-element.237.refs_9_), channel_id=1, source_target_pairs={{0,4},{4,0},{8,12},{12,8},{1,5},{5,1},{9,13},{13,9},{2,6},{6,2},{1... | collective-permute-start | bytes 1916936 | tf_op jit(solution)/shard_map/ppermute | solution.py:400
  159.5 22.2 %collective-permute-start.43 = (bf16[768,384]{1,0:T(8,128)(2,1)S(1)}, bf16[768,384]{1,0:T(8,128)(2,1)S(1)}, u32[]{:S(2)}, u32[]{:S(2)}) collective-permute-start(bf16[768,384]{1,0:T(8,128)(2,1)S(1)} %get-tuple-element.251), channel_id=1, source_target_pairs={{0,16},{16,0},{1,17},{17,1},{2,18},{18,2},{3,19},{19,3},{4,20},{20... | collective-permute-start | bytes 1769480 | tf_op jit(solution)/shard_map/ppermute | solution.py:406
  164.4 17.3 %collective-permute-start.44 = (bf16[768,384]{1,0:T(8,128)(2,1)S(1)}, bf16[768,384]{1,0:T(8,128)(2,1)S(1)}, u32[]{:S(2)}, u32[]{:S(2)}) collective-permute-start(bf16[768,384]{1,0:T(8,128)(2,1)S(1)} %add.116), channel_id=1, source_target_pairs={{0,1},{1,0},{2,3},{3,2},{4,5},{5,4},{6,7},{7,6},{8,9},{9,8},{10,11... | collective-permute-start | bytes 1769480 | tf_op jit(solution)/shard_map/ppermute | solution.py:403
  166.6 15.1 %collective-permute-start.42 = (bf16[208,768]{1,0:T(8,128)(2,1)S(1)}, bf16[208,768]{1,0:T(8,128)(2,1)S(1)}, u32[]{:S(2)}, u32[]{:S(2)}) collective-permute-start(bf16[208,768]{1,0:T(8,128)(2,1)S(1)} %feed_out_near.1), channel_id=1, source_target_pairs={{0,8},{4,12},{8,0},{12,4},{1,9},{5,13},{9,1},{13,5},{2,10},{6,14},... | collective-permute-start | bytes 958472 | tf_op jit(solution)/shard_map/ppermute | solution.py:400
  180.4 17.7 %collective-permute-start.52 = (bf16[2,2,192,384]{3,2,1,0:T(8,128)(2,1)S(1)}, bf16[2,2,192,384]{3,2,1,0:T(8,128)(2,1)S(1)}, u32[]{:S(2)}, u32[]{:S(2)}) collective-permute-start(bf16[2,2,192,384]{3,2,1,0:T(8,128)(2,1)S(1)} %get-tuple-element.271), channel_id=1, source_target_pairs={{0,16},{16,0},{1,17},{17,1},{2,18},{18,2},{3,19},{19,3},{4,20},{20... | collective-permute-start | bytes 1769480 | tf_op jit(solution)/shard_map/ppermute | solution.py:406
  181.5 16.6 %collective-permute-start.53 = (bf16[2,2,192,384]{3,2,1,0:T(8,128)(2,1)S(1)}, bf16[2,2,192,384]{3,2,1,0:T(8,128)(2,1)S(1)}, u32[]{:S(2)}, u32[]{:S(2)}) collective-permute-start(bf16[2,2,192,384]{3,2,1,0:T(8,128)(2,1)S(1)} %get-tuple-element.272), channel_id=1, source_target_pairs={{0,8},{4,12},{8,0},{12,4},{1,9},{5,13},{9,1},{13,5},{2,10},{6,14},... | collective-permute-start | bytes 1769480 | tf_op jit(solution)/shard_map/ppermute | solution.py:400
  194.9 11.5 %collective-permute-start.50 = (bf16[208,768]{1,0:T(8,128)(2,1)S(1)}, bf16[208,768]{1,0:T(8,128)(2,1)S(1)}, u32[]{:S(2)}, u32[]{:S(2)}) collective-permute-start(bf16[208,768]{1,0:T(8,128)(2,1)S(1)} %pad_maximum_fusion.11.refs_5_), channel_id=1, source_target_pairs={{0,1},{1,0},{2,3},{3,2},{4,5},{5,4},{6,7},{7,6},{8,9},{9,8},{10,11... | collective-permute-start | bytes 958472 | tf_op jit(solution)/shard_map/ppermute | solution.py:403
  200.4 29.5 %collective-permute-start.57 = (bf16[768,384]{1,0:T(8,128)(2,1)S(1)}, bf16[768,384]{1,0:T(8,128)(2,1)S(1)}, u32[]{:S(2)}, u32[]{:S(2)}) collective-permute-start(bf16[768,384]{1,0:T(8,128)(2,1)S(1)} %add_add_fusion), channel_id=1, source_target_pairs={{2,0},{3,1},{4,6},{5,7},{10,8},{11,9},{12,14},{13,15},{18,16},{19,... | collective-permute-start | bytes 1769480 | tf_op jit(solution)/shard_map/ppermute | solution.py:414
  209.5 20.4 %collective-permute-start.56 = (bf16[2,192,384]{2,1,0:T(8,128)(2,1)S(1)}, bf16[2,192,384]{2,1,0:T(8,128)(2,1)S(1)}, u32[]{:S(2)}, u32[]{:S(2)}) collective-permute-start(bf16[2,192,384]{2,1,0:T(8,128)(2,1)S(1)} %pad_maximum_fusion.12), channel_id=1, source_target_pairs={{0,1},{1,0},{2,3},{3,2},{4,5},{5,4},{6,7},{7,6},{8,9},{9,8},{10,11... | collective-permute-start | bytes 884744 | tf_op jit(solution)/shard_map/ppermute | solution.py:403
  210.2 19.6 %collective-permute-start.58 = (bf16[52,768]{1,0:T(8,128)(2,1)S(1)}, bf16[52,768]{1,0:T(8,128)(2,1)S(1)}, u32[]{:S(2)}, u32[]{:S(2)}) collective-permute-start(bf16[52,768]{1,0:T(8,128)(2,1)S(1)} %get-tuple-element.289), channel_id=1, source_target_pairs={{0,1},{1,0},{2,3},{3,2},{4,5},{5,4},{6,7},{7,6},{8,9},{9,8},{10,11... | collective-permute-start | bytes 239624 | tf_op jit(solution)/shard_map/ppermute | solution.py:403
  211.2 18.7 %collective-permute-start.59 = (bf16[52,768]{1,0:T(8,128)(2,1)S(1)}, bf16[52,768]{1,0:T(8,128)(2,1)S(1)}, u32[]{:S(2)}, u32[]{:S(2)}) collective-permute-start(bf16[52,768]{1,0:T(8,128)(2,1)S(1)} %get-tuple-element.290), channel_id=1, source_target_pairs={{0,2},{1,3},{2,0},{3,1},{4,6},{5,7},{6,4},{7,5},{8,10},{9,11},{10,... | collective-permute-start | bytes 239624 | tf_op jit(solution)/shard_map/ppermute | solution.py:403
  212.0 17.9 %collective-permute-start.60 = (bf16[52,768]{1,0:T(8,128)(2,1)S(1)}, bf16[52,768]{1,0:T(8,128)(2,1)S(1)}, u32[]{:S(2)}, u32[]{:S(2)}) collective-permute-start(bf16[52,768]{1,0:T(8,128)(2,1)S(1)} %get-tuple-element.291), channel_id=1, source_target_pairs={{0,3},{1,2},{2,1},{3,0},{4,7},{5,6},{6,5},{7,4},{8,11},{9,10},{10,... | collective-permute-start | bytes 239624 | tf_op jit(solution)/shard_map/ppermute | solution.py:403
  249.2 14.8 %collective-permute-start.70 = (bf16[768,384]{1,0:T(8,128)(2,1)S(1)}, bf16[768,384]{1,0:T(8,128)(2,1)S(1)}, u32[]{:S(2)}, u32[]{:S(2)}) collective-permute-start(bf16[768,384]{1,0:T(8,128)(2,1)S(1)} %add.126), channel_id=1, source_target_pairs={{0,8},{4,12},{8,0},{12,4},{1,9},{5,13},{9,1},{13,5},{2,10},{6,14},... | collective-permute-start | bytes 1769480 | tf_op jit(solution)/shard_map/ppermute | solution.py:400
  264.0 15.7 %collective-permute-start.74 = (f32[3,768]{1,0:T(4,128)S(1)}, f32[3,768]{1,0:T(4,128)S(1)}, u32[]{:S(2)}, u32[]{:S(2)}) collective-permute-start(f32[3,768]{1,0:T(4,128)S(1)} %fusion.21), channel_id=1, source_target_pairs={{0,1},{1,0},{2,3},{3,2},{4,5},{5,4},{6,7},{7,6},{8,9},{9,8},{10,11... | collective-permute-start | bytes 27656 | tf_op jit(solution)/shard_map/ppermute | solution.py:403
  290.0 10.3 %collective-permute-start.83 = (bf16[2,2,192,384]{3,2,1,0:T(8,128)(2,1)S(1)}, bf16[2,2,192,384]{3,2,1,0:T(8,128)(2,1)S(1)}, u32[]{:S(2)}, u32[]{:S(2)}) collective-permute-start(bf16[2,2,192,384]{3,2,1,0:T(8,128)(2,1)S(1)} %pad_maximum_fusion.5), channel_id=1, source_target_pairs={{0,4},{4,0},{8,12},{12,8},{1,5},{5,1},{9,13},{13,9},{2,6},{6,2},{1... | collective-permute-start | bytes 1769480 | tf_op jit(solution)/shard_map/ppermute | solution.py:400
  (79 other events, 524.3 us)
